TPU v7x, 32 devices: a whole 2x2x4 slice. The times are simulated.
32 devices in a mesh: ctx: 4 (over z), head: 4 (over x, core), grp: 2 (over y).
Axes of the slice: x: 2, y: 2, z: 4, core: 2. Of those that a mesh axis runs over, the one named last changes fastest.
Arguments:
- queries: bfloat16 [2, 256, 8192], P('grp', 'ctx', 'head'), may hold values from -40 to 40
- new_keys: bfloat16 [2, 256, 1024], P('grp', 'ctx', 'head'), may hold values from -40 to 40
- new_values: bfloat16 [2, 256, 1024], P('grp', 'ctx', 'head'), may hold values from -6 to 6
- page_keys: bfloat16 [2, 2048, 1024], P('grp', 'ctx', 'head'), may hold values from -6 to 6
- page_values: bfloat16 [2, 2048, 1024], P('grp', 'ctx', 'head'), may hold values from -6 to 6
- page_table: int32 [2, 1, 16], P('grp'), may hold values from 0 to 31, as said below
- page_slot: int32 [2, 32], P('grp'), may hold values from 0 to 31, each once within a row
- page_length: int32 [2, 32], P('grp'), may hold values from 1 to 64
Outputs:
- attended: bfloat16 [2, 256, 8192], P('grp', 'ctx', 'head')
Inputs may be any that keep to these rules, and one draw needn't show every extreme that they name: `page_table`: the 16 page numbers of one request are distinct.
All inputs are finite; a program needn't handle non-finite values.
Results may differ from a plain program's by a relative error of at most 0.0055.
Values may be sent and summed in bfloat16 or wider, within the bound.
No kernel may reach another device: no remote copies, remote signals or barrier semaphores. Data moves between devices by JAX's collectives and lax.ppermute only.
A program may use at most 64 MiB of HBM per device.

v0:
```python
import math

import jax
import jax.numpy as jnp
from jax import lax
from jax.sharding import PartitionSpec as P

HD = 128
SPAN = 4
PAGE = 64


neg_floor = -1e30
far_limit = 1 << 30


def passed_along(block, axis, distance):
    devices = range(lax.axis_size(axis))
    route = [(i - distance, i) for i in devices if i - distance in devices]
    return lax.ppermute(block, axis, route)


def passed_along_2(block, axis, distance):
    devices = range(lax.axis_size(axis))
    route = [((i - distance) % len(devices), i) for i in devices]
    return lax.ppermute(block, axis, route)


def local(
    queries, new_keys, new_values, page_keys, page_values, page_table, page_slot, page_length
):
    query_rows = queries[0]
    rows_dev = query_rows.shape[0]
    key_width = new_keys.shape[2]
    shared_heads = key_width // HD
    query_count = query_rows.shape[1] // HD
    group_size = query_count // shared_heads
    scaling = 1.0 / math.sqrt(HD)
    position = lax.axis_index("ctx")
    cycle_size = lax.axis_size("ctx")
    pool_index = lax.axis_index("grp")
    request = position // SPAN
    row_ids = position * rows_dev + jnp.arange(rows_dev, dtype=jnp.int32)
    query_heads = query_rows.reshape(rows_dev, shared_heads, group_size, HD).transpose(1, 2, 0, 3)
    pages_total = page_slot.shape[1]
    numbers = jnp.arange(pages_total, dtype=jnp.int32)
    listed = jnp.any(page_table[0][:, :, None] == numbers[None, None, :], axis=1).astype(
        jnp.float32
    )
    own_listed = lax.dynamic_index_in_dim(listed, request, 0, keepdims=False)
    placed = (page_slot[0][:, None] == numbers[None, :]).astype(jnp.float32)
    listed_slot = jnp.dot(own_listed, placed, precision=lax.Precision.HIGHEST)
    length_slot = jnp.dot(
        page_length[0].astype(jnp.float32), placed, precision=lax.Precision.HIGHEST
    )
    offsets = jnp.arange(PAGE, dtype=jnp.int32).astype(jnp.float32)
    page_open = (listed_slot[:, None] > 0.5) & (offsets[None, :] < length_slot[:, None])
    page_limits = jnp.where(page_open, 0, far_limit).astype(jnp.int32).reshape(cycle_size, -1)

    def own_limits(holder):
        same = holder // SPAN == request
        return jnp.where(same, holder * rows_dev + jnp.arange(rows_dev, dtype=jnp.int32), far_limit)

    def taken_limits(holder):
        same = (holder // SPAN == request) & (pool_index == 1)
        return jnp.where(same, jnp.zeros((rows_dev,), jnp.int32), far_limit)

    def absorb_rows(carried, key_rows, value_rows, limits):
        maxima, totals, accumulated = carried
        pieces = key_rows.shape[0]
        key_heads = key_rows.reshape(pieces, shared_heads, HD)
        value_heads = value_rows.reshape(pieces, shared_heads, HD)
        scores = (
            jnp.einsum("kgrd,nkd->kgrn", query_heads, key_heads, preferred_element_type=jnp.float32)
            * scaling
        )
        allowed = row_ids[:, None] >= limits[None, :]
        masked = jnp.where(allowed, scores, neg_floor)
        new_max = jnp.maximum(maxima, jnp.max(masked, axis=-1))
        weights = jnp.where(allowed, jnp.exp(masked - new_max[..., None]), 0.0)
        rescale = jnp.exp(maxima - new_max)
        totals = totals * rescale + jnp.sum(weights, axis=-1)
        product = jnp.einsum(
            "kgrn,nkd->kgrd",
            weights.astype(jnp.bfloat16),
            value_heads,
            preferred_element_type=jnp.float32,
        )
        accumulated = accumulated * rescale[..., None] + product
        return (new_max, totals, accumulated)

    own_pairs = jnp.stack([new_keys[0], new_values[0]])
    taken_pairs = passed_along(own_pairs, "grp", 1)
    page_pairs = jnp.stack([page_keys[0], page_values[0]])
    carried = (
        jnp.full((shared_heads, group_size, rows_dev), neg_floor, jnp.float32),
        jnp.zeros((shared_heads, group_size, rows_dev), jnp.float32),
        jnp.zeros((shared_heads, group_size, rows_dev, HD), jnp.float32),
    )
    moving_rows = jnp.concatenate([page_pairs, own_pairs, taken_pairs], axis=1)

    def block_limits(holder):
        page_part = lax.dynamic_index_in_dim(page_limits, holder, 0, keepdims=False)
        return jnp.concatenate([page_part, own_limits(holder), taken_limits(holder)])

    def advance(stride, state_pair):
        inner, travelling = state_pair
        holder = (position - stride) % cycle_size
        inner = absorb_rows(inner, travelling[0], travelling[1], block_limits(holder))
        travelling = passed_along_2(travelling, "ctx", 1)
        return (inner, travelling)

    carried, moving_rows = lax.fori_loop(0, cycle_size - 1, advance, (carried, moving_rows))
    carried = absorb_rows(
        carried, moving_rows[0], moving_rows[1], block_limits((position + 1) % cycle_size)
    )
    maxima, totals, accumulated = carried
    attended = accumulated / totals[..., None]
    attended = attended.transpose(2, 0, 1, 3).reshape(rows_dev, query_count * HD)
    return attended.astype(jnp.bfloat16)[None]


def solution(mesh):
    in_specs = (
        P("grp", "ctx", "head"),
        P("grp", "ctx", "head"),
        P("grp", "ctx", "head"),
        P("grp", "ctx", "head"),
        P("grp", "ctx", "head"),
        P("grp", None, None),
        P("grp", None),
        P("grp", None),
    )
    out_specs = P("grp", "ctx", "head")
    return jax.shard_map(local, mesh=mesh, in_specs=in_specs, out_specs=out_specs, check_vma=False)
```

profile of v0, /device:TPU:0, one launch (start us, length us, event | category | flops | bytes accessed | tf_op | source)
XLA Modules:
  0.0 77.1 jit_solution(15543521188503115114)
XLA Ops:
  0.0 0.9 %copy.25 = bf16[1,64,256]{1,2,0:T(8,128)(2,1)S(1)} copy(bf16[1,64,256]{2,1,0:T(8,128)(2,1)} %param.12) | data formatting | bytes 65536 | tf_op args[2]
  0.9 0.9 %copy.24 = bf16[1,64,256]{1,2,0:T(8,128)(2,1)S(1)} copy(bf16[1,64,256]{2,1,0:T(8,128)(2,1)} %param.11) | data formatting | bytes 65536 | tf_op args[1]
  1.8 4.9 %collective-permute-start.1 = (bf16[2,64,256]{1,2,0:T(8,128)(2,1)S(1)}, bf16[2,64,256]{1,2,0:T(8,128)(2,1)S(1)}, u32[]{:S(2)}, u32[]{:S(2)}) collective-permute-start(bf16[2,64,256]{1,2,0:T(8,128)(2,1)S(1)} %pad_maximum_fusion.1), channel_id=1, source_target_pairs={{0,1},{2,3},{4,5},{6,7},{8,9},{10,11},{12,13},{14,15},{16,17},{18,... | collective-permute-start | bytes 196616 | tf_op jit(solution)/shard_map/ppermute | solution.py:20
  6.8 0.7 fusion.39
  7.5 0.8 %fusion.24 = pred[32]{0:T(512)(128)(4,1)S(1)} fusion(s32[32]{0:T(128)} %bitcast.95, pred[32]{0:T(512)(128)(4,1)S(1)} %fusion.39), kind=kOutput, calls=%fused_computation.31 | convolution fusion | flops 3104 | bytes 192 | tf_op jit(solution)/shard_map/dot_general | solution.py:52
  8.3 0.1 and.71
  8.4 0.1 and.72
  8.5 0.1 and.73
  8.6 1.0 %fusion.34 = f32[1,4,8]{2,0,1:T(1,128)S(1)} fusion(s32[4,8]{1,0:T(4,128)S(1)} %multiply_add_fusion.1, s32[32]{0:T(128)} %bitcast.96, s32[1,32]{1,0:T(1,128)} %param.17), kind=kOutput, calls=%fused_computation.39 | convolution fusion | flops 13344 | bytes 512 | tf_op jit(solution)/shard_map/dot_general | solution.py:53
  9.6 0.1 lt.60
  9.6 0.1 lt.61
  9.7 0.1 lt.58
  9.8 0.6 and_select_fusion
  10.4 0.7 constant_dynamic-slice_fusion.1
  11.1 0.1 pad_add_fusion.1
  11.2 0.7 broadcast_compare_fusion.1
  11.9 1.1 %copy.23 = bf16[1,512,256]{1,2,0:T(8,128)(2,1)S(1)} copy(bf16[1,512,256]{2,1,0:T(8,128)(2,1)} %param.14) | data formatting | bytes 524288 | tf_op args[4]
  13.0 1.1 %copy.22 = bf16[1,512,256]{1,2,0:T(8,128)(2,1)S(1)} copy(bf16[1,512,256]{2,1,0:T(8,128)(2,1)} %param.13) | data formatting | bytes 524288 | tf_op args[3]
  14.1 1.0 %copy.44 = bf16[8,8,16,128]{3,2,1,0:T(8,128)(2,1)S(1)} copy(bf16[8,8,16,128]{3,1,2,0:T(8,128)(2,1)} %bitcast.90) | data formatting | bytes 524288
  15.1 0.0 copy-start.1
  15.1 0.1 copy.26
  15.2 0.0 collective-permute-done.1
  15.2 0.9 %pad_maximum_fusion = bf16[2,640,256]{1,2,0:T(8,128)(2,1)} fusion(bf16[2,64,256]{1,2,0:T(8,128)(2,1)S(1)} %collective-permute-done.1, bf16[1,64,256]{1,2,0:T(8,128)(2,1)S(1)} %copy.25, bf16[1,64,256]{1,2,0:T(8,128)(2,1)S(1)} %copy.24, bf16[1,512,256]{1,2,0:T(8,128)(2,1)S(1)} %copy.23, bf16[1,512,256]{1,2,0:T(8,128)(2,1)S(1)} %copy.22), kind=kLoop, calls=%fused_computation.35 | loop fusion | flops 3276800 | bytes 1310720 | tf_op jit(solution)/shard_map/concatenate | solution.py:100
  16.2 55.2 %while.22 = (s32[]{:T(128)}, f32[2,8,64]{2,1,0:T(8,128)S(1)}, f32[2,8,64]{2,1,0:T(8,128)}, f32[2,8,64,128]{3,2,1,0:T(8,128)}, bf16[2,640,256]{1,2,0:T(8,128)(2,1...) while((s32[]{:T(128)}, f32[2,8,64]{2,1,0:T(8,128)S(1)}, ...), condition=%wide.region_4.5_spmd.clone, body=%wide.region_1.4_spmd.clone.sunk | while | flops 344504800 | bytes 15479899 | solution.py:113
  16.2 1.1 %copy.58 = bf16[2,640,256]{1,2,0:T(8,128)(2,1)S(1)} copy(bf16[2,640,256]{1,2,0:T(8,128)(2,1)} %get-tuple-element.478) | data formatting | bytes 1310720 | tf_op jit(solution)/shard_map/while
  17.3 1.6 %collective-permute-start = (bf16[2,640,256]{1,2,0:T(8,128)(2,1)S(1)}, bf16[2,640,256]{1,2,0:T(8,128)(2,1)}, u32[]{:S(2)}, u32[]{:S(2)}) collective-permute-start(bf16[2,640,256]{1,2,0:T(8,128)(2,1)S(1)} %copy.58), channel_id=1, source_target_pairs={{24,0},{0,8},{8,16},{16,24},{25,1},{1,9},{9,17},{17,25},{26,2},{2,... | collective-permute-start | bytes 1966088 | tf_op jit(solution)/shard_map/while/body/eval_jaxpr/ppermute | solution.py:26
  18.8 0.9 %fusion.66 = (bf16[1,640,256]{1,2,0:T(8,128)(2,1)}, bf16[1,640,256]{1,2,0:T(8,128)(2,1)}) fusion(bf16[2,640,256]{1,2,0:T(8,128)(2,1)S(1)} %copy.58), kind=kLoop, calls=%fused_computation.62.clone.1 | loop fusion | bytes 1310720 | tf_op jit(solution)/shard_map/while/body/eval_jaxpr/slice | solution.py:109
  19.8 0.7 constant_dynamic-slice_fusion.3
  20.5 0.1 pad_add_fusion.3
  20.6 0.1 broadcast_compare_fusion.3
  20.7 1.6 %fusion.67 = (f32[2,8,64]{2,1,0:T(8,128)S(1)}, f32[2,8,64,640]{3,2,1,0:T(8,128)S(1)}) fusion(pred[64,640]{1,0:T(8,128)(4,1)S(1)} %broadcast_compare_fusion.3, bf16[2,8,64,128]{3,2,1,0:T(8,128)(2,1)S(1)} %get-tuple-element.502, bf16[640,2,128,1]{0,2,3,1:T(8,128)(2,1)} %bitcast.84), kind=kOutput, calls=%fused_computation.3.clone.1 | convolution fusion | flops 169737216 | bytes 3256320 | tf_op jit(solution)/shard_map/while/body/eval_jaxpr/kgrd,nkd->kgrn/dot_general | solution.py:74
  22.3 0.0 copy-done
  22.3 1.4 %fusion.68 = f32[2,8,64]{2,1,0:T(8,128)} fusion(f32[2,8,64,640]{3,2,1,0:T(8,128)S(1)} %get-tuple-element.451, f32[2,8,64]{2,1,0:T(8,128)S(1)} %select_maximum_fusion.2, pred[64,640]{1,0:T(8,128)(4,1)S(1)} %broadcast_compare_fusion.3), kind=kLoop, calls=%fused_computation.5.clone.1 | loop fusion | flops 3275776 | bytes 2670592 | tf_op jit(solution)/shard_map/while/body/eval_jaxpr/reduce_sum | solution.py:82
  23.8 1.3 %fusion.69 = (f32[2,8,64]{2,1,0:T(8,128)}, f32[2,8,64]{2,1,0:T(8,128)S(1)}) fusion(f32[2,8,64]{2,1,0:T(8,128)} %fusion.68, f32[2,8,64]{2,1,0:T(8,128)} %get-tuple-element.476, pred[]{:T(512)S(6)} %compare.17, f32[2,8,64]{2,1,0:T(8,128)S(1)} %select_maximum_fusion.2, f32[2,8,64]{2,1,0:T(8,128)S(1)} %get-tuple-element.475), kind=kLoop, calls=%fused_computation.12.clone.1 | loop fusion | flops 5120 | bytes 24577 | tf_op jit(solution)/shard_map/while/body/eval_jaxpr/add | solution.py:82
  25.1 2.6 %fusion.70 = f32[2,8,64,128]{3,2,1,0:T(8,128)} fusion(bf16[640,2,128,1]{0,2,3,1:T(8,128)(2,1)} %bitcast.85, f32[2,8,64,640]{3,2,1,0:T(8,128)S(1)} %get-tuple-element.451, f32[2,8,64]{2,1,0:T(8,128)S(1)} %select_maximum_fusion.2, pred[64,640]{1,0:T(8,128)(4,1)} %copy-done, f32[2,8,64,128]{3,2,1,0:T(8,128)} %get-tuple-element.477, ...), kind=kOutput, calls=%fused_computation.8.clone.1 | convolution fusion | flops 171442176 | bytes 4046849 | tf_op jit(solution)/shard_map/while/body/eval_jaxpr/kgrn,nkd->kgrd/dot_general | solution.py:83
  27.7 7.7 %collective-permute-done = bf16[2,640,256]{1,2,0:T(8,128)(2,1)} collective-permute-done((bf16[2,640,256]{1,2,0:T(8,128)(2,1)S(1)}, bf16[2,640,256]{1,2,0:T(8,128)(2,1)}, u32[]{:S(2)}, u32[]{:S(2)}) %collective-permute-start) | collective-permute-done | bytes 655392 | tf_op jit(solution)/shard_map/while/body/eval_jaxpr/ppermute | solution.py:26
  35.4 1.1 %copy.58 = bf16[2,640,256]{1,2,0:T(8,128)(2,1)S(1)} copy(bf16[2,640,256]{1,2,0:T(8,128)(2,1)} %get-tuple-element.478) | data formatting | bytes 1310720 | tf_op jit(solution)/shard_map/while
  36.5 0.0 collective-permute-start
  36.5 0.9 %fusion.66 = (bf16[1,640,256]{1,2,0:T(8,128)(2,1)}, bf16[1,640,256]{1,2,0:T(8,128)(2,1)}) fusion(bf16[2,640,256]{1,2,0:T(8,128)(2,1)S(1)} %copy.58), kind=kLoop, calls=%fused_computation.62.clone.1 | loop fusion | bytes 1310720 | tf_op jit(solution)/shard_map/while/body/eval_jaxpr/slice | solution.py:109
  37.5 0.7 constant_dynamic-slice_fusion.3
  38.2 0.1 pad_add_fusion.3
  38.2 0.1 broadcast_compare_fusion.3
  38.4 1.6 %fusion.67 = (f32[2,8,64]{2,1,0:T(8,128)S(1)}, f32[2,8,64,640]{3,2,1,0:T(8,128)S(1)}) fusion(pred[64,640]{1,0:T(8,128)(4,1)S(1)} %broadcast_compare_fusion.3, bf16[2,8,64,128]{3,2,1,0:T(8,128)(2,1)S(1)} %get-tuple-element.502, bf16[640,2,128,1]{0,2,3,1:T(8,128)(2,1)} %bitcast.84), kind=kOutput, calls=%fused_computation.3.clone.1 | convolution fusion | flops 169737216 | bytes 3256320 | tf_op jit(solution)/shard_map/while/body/eval_jaxpr/kgrd,nkd->kgrn/dot_general | solution.py:74
  40.0 1.4 %fusion.68 = f32[2,8,64]{2,1,0:T(8,128)} fusion(f32[2,8,64,640]{3,2,1,0:T(8,128)S(1)} %get-tuple-element.451, f32[2,8,64]{2,1,0:T(8,128)S(1)} %select_maximum_fusion.2, pred[64,640]{1,0:T(8,128)(4,1)S(1)} %broadcast_compare_fusion.3), kind=kLoop, calls=%fused_computation.5.clone.1 | loop fusion | flops 3275776 | bytes 2670592 | tf_op jit(solution)/shard_map/while/body/eval_jaxpr/reduce_sum | solution.py:82
  41.4 1.3 %fusion.69 = (f32[2,8,64]{2,1,0:T(8,128)}, f32[2,8,64]{2,1,0:T(8,128)S(1)}) fusion(f32[2,8,64]{2,1,0:T(8,128)} %fusion.68, f32[2,8,64]{2,1,0:T(8,128)} %get-tuple-element.476, pred[]{:T(512)S(6)} %compare.17, f32[2,8,64]{2,1,0:T(8,128)S(1)} %select_maximum_fusion.2, f32[2,8,64]{2,1,0:T(8,128)S(1)} %get-tuple-element.475), kind=kLoop, calls=%fused_computation.12.clone.1 | loop fusion | flops 5120 | bytes 24577 | tf_op jit(solution)/shard_map/while/body/eval_jaxpr/add | solution.py:82
  42.8 2.8 %fusion.70 = f32[2,8,64,128]{3,2,1,0:T(8,128)} fusion(bf16[640,2,128,1]{0,2,3,1:T(8,128)(2,1)} %bitcast.85, f32[2,8,64,640]{3,2,1,0:T(8,128)S(1)} %get-tuple-element.451, f32[2,8,64]{2,1,0:T(8,128)S(1)} %select_maximum_fusion.2, pred[64,640]{1,0:T(8,128)(4,1)} %copy-done, f32[2,8,64,128]{3,2,1,0:T(8,128)} %get-tuple-element.477, ...), kind=kOutput, calls=%fused_computation.8.clone.1 | convolution fusion | flops 171442176 | bytes 4046849 | tf_op jit(solution)/shard_map/while/body/eval_jaxpr/kgrn,nkd->kgrd/dot_general | solution.py:83
  45.6 8.3 %collective-permute-done = bf16[2,640,256]{1,2,0:T(8,128)(2,1)} collective-permute-done((bf16[2,640,256]{1,2,0:T(8,128)(2,1)S(1)}, bf16[2,640,256]{1,2,0:T(8,128)(2,1)}, u32[]{:S(2)}, u32[]{:S(2)}) %collective-permute-start) | collective-permute-done | bytes 655392 | tf_op jit(solution)/shard_map/while/body/eval_jaxpr/ppermute | solution.py:26
  53.8 1.1 %copy.58 = bf16[2,640,256]{1,2,0:T(8,128)(2,1)S(1)} copy(bf16[2,640,256]{1,2,0:T(8,128)(2,1)} %get-tuple-element.478) | data formatting | bytes 1310720 | tf_op jit(solution)/shard_map/while
  54.9 0.0 collective-permute-start
  54.9 0.9 %fusion.66 = (bf16[1,640,256]{1,2,0:T(8,128)(2,1)}, bf16[1,640,256]{1,2,0:T(8,128)(2,1)}) fusion(bf16[2,640,256]{1,2,0:T(8,128)(2,1)S(1)} %copy.58), kind=kLoop, calls=%fused_computation.62.clone.1 | loop fusion | bytes 1310720 | tf_op jit(solution)/shard_map/while/body/eval_jaxpr/slice | solution.py:109
  55.8 0.7 constant_dynamic-slice_fusion.3
  56.6 0.1 pad_add_fusion.3
  56.6 0.1 broadcast_compare_fusion.3
  56.7 1.6 %fusion.67 = (f32[2,8,64]{2,1,0:T(8,128)S(1)}, f32[2,8,64,640]{3,2,1,0:T(8,128)S(1)}) fusion(pred[64,640]{1,0:T(8,128)(4,1)S(1)} %broadcast_compare_fusion.3, bf16[2,8,64,128]{3,2,1,0:T(8,128)(2,1)S(1)} %get-tuple-element.502, bf16[640,2,128,1]{0,2,3,1:T(8,128)(2,1)} %bitcast.84), kind=kOutput, calls=%fused_computation.3.clone.1 | convolution fusion | flops 169737216 | bytes 3256320 | tf_op jit(solution)/shard_map/while/body/eval_jaxpr/kgrd,nkd->kgrn/dot_general | solution.py:74
  58.4 1.4 %fusion.68 = f32[2,8,64]{2,1,0:T(8,128)} fusion(f32[2,8,64,640]{3,2,1,0:T(8,128)S(1)} %get-tuple-element.451, f32[2,8,64]{2,1,0:T(8,128)S(1)} %select_maximum_fusion.2, pred[64,640]{1,0:T(8,128)(4,1)S(1)} %broadcast_compare_fusion.3), kind=kLoop, calls=%fused_computation.5.clone.1 | loop fusion | flops 3275776 | bytes 2670592 | tf_op jit(solution)/shard_map/while/body/eval_jaxpr/reduce_sum | solution.py:82
  59.8 1.3 %fusion.69 = (f32[2,8,64]{2,1,0:T(8,128)}, f32[2,8,64]{2,1,0:T(8,128)S(1)}) fusion(f32[2,8,64]{2,1,0:T(8,128)} %fusion.68, f32[2,8,64]{2,1,0:T(8,128)} %get-tuple-element.476, pred[]{:T(512)S(6)} %compare.17, f32[2,8,64]{2,1,0:T(8,128)S(1)} %select_maximum_fusion.2, f32[2,8,64]{2,1,0:T(8,128)S(1)} %get-tuple-element.475), kind=kLoop, calls=%fused_computation.12.clone.1 | loop fusion | flops 5120 | bytes 24577 | tf_op jit(solution)/shard_map/while/body/eval_jaxpr/add | solution.py:82
  61.2 2.8 %fusion.70 = f32[2,8,64,128]{3,2,1,0:T(8,128)} fusion(bf16[640,2,128,1]{0,2,3,1:T(8,128)(2,1)} %bitcast.85, f32[2,8,64,640]{3,2,1,0:T(8,128)S(1)} %get-tuple-element.451, f32[2,8,64]{2,1,0:T(8,128)S(1)} %select_maximum_fusion.2, pred[64,640]{1,0:T(8,128)(4,1)} %copy-done, f32[2,8,64,128]{3,2,1,0:T(8,128)} %get-tuple-element.477, ...), kind=kOutput, calls=%fused_computation.8.clone.1 | convolution fusion | flops 171442176 | bytes 4046849 | tf_op jit(solution)/shard_map/while/body/eval_jaxpr/kgrn,nkd->kgrd/dot_general | solution.py:83
  63.9 7.4 %collective-permute-done = bf16[2,640,256]{1,2,0:T(8,128)(2,1)} collective-permute-done((bf16[2,640,256]{1,2,0:T(8,128)(2,1)S(1)}, bf16[2,640,256]{1,2,0:T(8,128)(2,1)}, u32[]{:S(2)}, u32[]{:S(2)}) %collective-permute-start) | collective-permute-done | bytes 655392 | tf_op jit(solution)/shard_map/while/body/eval_jaxpr/ppermute | solution.py:26
  71.3 1.1 %fusion.47 = (bf16[1,640,256]{1,2,0:T(8,128)(2,1)S(1)}, bf16[1,640,256]{1,2,0:T(8,128)(2,1)S(1)}) fusion(bf16[2,640,256]{1,2,0:T(8,128)(2,1)} %get-tuple-element.279), kind=kLoop, calls=%fused_computation.63 | loop fusion | bytes 1310720 | tf_op jit(solution)/shard_map/slice | solution.py:115
  72.5 1.7 %fusion.15 = (f32[2,8,64]{2,1,0:T(8,128)S(1)}, f32[2,640,8,64]{1,3,2,0:T(8,128)S(1)}) fusion(pred[64,640]{1,0:T(8,128)(4,1)} %broadcast_compare_fusion.1, bf16[640,2,128,1]{0,2,3,1:T(8,128)(2,1)S(1)} %bitcast.88, bf16[2,8,64,128]{3,1,0,2:T(8,128)(2,1)} %bitcast.87), kind=kOutput, calls=%fused_computation.24 | convolution fusion | flops 169737216 | bytes 3256320 | tf_op jit(solution)/shard_map/kgrd,nkd->kgrn/dot_general | solution.py:74
  74.2 0.9 %fusion.16 = f32[2,8,64]{2,1,0:T(8,128)S(1)} fusion(f32[2,640,8,64]{1,3,2,0:T(8,128)S(1)} %get-tuple-element.375, f32[2,8,64]{2,1,0:T(8,128)S(1)} %max.13, pred[64,640]{1,0:T(8,128)(4,1)S(1)} %copy-done.2), kind=kLoop, calls=%fused_computation.25 | loop fusion | flops 3275776 | bytes 2670592 | tf_op jit(solution)/shard_map/reduce_sum | solution.py:82
  75.1 0.9 %fusion.31 = bf16[64,2,8,128]{3,0,2,1:T(8,128)(2,1)S(1)} fusion(bf16[640,2,128,1]{0,2,3,1:T(8,128)(2,1)S(1)} %bitcast.89, f32[2,640,8,64]{1,3,2,0:T(8,128)S(1)} %get-tuple-element.375, f32[2,8,64]{2,1,0:T(8,128)S(1)} %max.13, pred[64,640]{1,0:T(8,128)(4,1)S(1)} %copy-done.2, f32[2,8,64,128]{3,2,1,0:T(8,128)S(1)} %copy-done.4, ...), kind=kOutput, calls=%fused_computation.34 | convolution fusion | flops 171573248 | bytes 3788800 | tf_op jit(solution)/shard_map/kgrn,nkd->kgrd/dot_general | solution.py:83
  76.1 0.2 copy.30
  76.2 0.8 %convert_element_type.50 = bf16[1,64,2048]{2,1,0:T(8,128)(2,1)} reshape(bf16[64,2,8,128]{3,2,1,0:T(8,128)(2,1)S(1)} %copy.30) | data formatting | bytes 524288 | tf_op jit(solution)/shard_map/convert_element_type | solution.py:120
  (39 shorter events, 0.1 us)
Async XLA Ops:
  1.8 13.4 %collective-permute-start.1 = (bf16[2,64,256]{1,2,0:T(8,128)(2,1)S(1)}, bf16[2,64,256]{1,2,0:T(8,128)(2,1)S(1)}, u32[]{:S(2)}, u32[]{:S(2)}) collective-permute-start(bf16[2,64,256]{1,2,0:T(8,128)(2,1)S(1)} %pad_maximum_fusion.1), channel_id=1, source_target_pairs={{0,1},{2,3},{4,5},{6,7},{8,9},{10,11},{12,13},{14,15},{16,17},{18,... | collective-permute-start | bytes 196616 | tf_op jit(solution)/shard_map/ppermute | solution.py:20
  15.1 1.0 %copy-start.1 = (bf16[8,8,16,128]{3,2,1,0:T(8,128)(2,1)}, bf16[8,8,16,128]{3,2,1,0:T(8,128)(2,1)S(1)}, u32[]{:S(2)}) copy-start(bf16[8,8,16,128]{3,2,1,0:T(8,128)(2,1)S(1)} %copy.44) | copy-start | bytes 786436
  17.3 18.2 %collective-permute-start = (bf16[2,640,256]{1,2,0:T(8,128)(2,1)S(1)}, bf16[2,640,256]{1,2,0:T(8,128)(2,1)}, u32[]{:S(2)}, u32[]{:S(2)}) collective-permute-start(bf16[2,640,256]{1,2,0:T(8,128)(2,1)S(1)} %copy.58), channel_id=1, source_target_pairs={{24,0},{0,8},{8,16},{16,24},{25,1},{1,9},{9,17},{17,25},{26,2},{2,... | collective-permute-start | bytes 1966088 | tf_op jit(solution)/shard_map/while/body/eval_jaxpr/ppermute | solution.py:26
  20.7 1.7 %copy-start = (pred[64,640]{1,0:T(8,128)(4,1)}, pred[64,640]{1,0:T(8,128)(4,1)S(1)}, u32[]{:S(2)}) copy-start(pred[64,640]{1,0:T(8,128)(4,1)S(1)} %broadcast_compare_fusion.3) | copy-start | bytes 122884 | tf_op jit(solution)/shard_map/while
  36.5 17.3 %collective-permute-start = (bf16[2,640,256]{1,2,0:T(8,128)(2,1)S(1)}, bf16[2,640,256]{1,2,0:T(8,128)(2,1)}, u32[]{:S(2)}, u32[]{:S(2)}) collective-permute-start(bf16[2,640,256]{1,2,0:T(8,128)(2,1)S(1)} %copy.58), channel_id=1, source_target_pairs={{24,0},{0,8},{8,16},{16,24},{25,1},{1,9},{9,17},{17,25},{26,2},{2,... | collective-permute-start | bytes 1966088 | tf_op jit(solution)/shard_map/while/body/eval_jaxpr/ppermute | solution.py:26
  38.3 1.7 %copy-start = (pred[64,640]{1,0:T(8,128)(4,1)}, pred[64,640]{1,0:T(8,128)(4,1)S(1)}, u32[]{:S(2)}) copy-start(pred[64,640]{1,0:T(8,128)(4,1)S(1)} %broadcast_compare_fusion.3) | copy-start | bytes 122884 | tf_op jit(solution)/shard_map/while
  54.9 16.4 %collective-permute-start = (bf16[2,640,256]{1,2,0:T(8,128)(2,1)S(1)}, bf16[2,640,256]{1,2,0:T(8,128)(2,1)}, u32[]{:S(2)}, u32[]{:S(2)}) collective-permute-start(bf16[2,640,256]{1,2,0:T(8,128)(2,1)S(1)} %copy.58), channel_id=1, source_target_pairs={{24,0},{0,8},{8,16},{16,24},{25,1},{1,9},{9,17},{17,25},{26,2},{2,... | collective-permute-start | bytes 1966088 | tf_op jit(solution)/shard_map/while/body/eval_jaxpr/ppermute | solution.py:26
  56.7 1.7 %copy-start = (pred[64,640]{1,0:T(8,128)(4,1)}, pred[64,640]{1,0:T(8,128)(4,1)S(1)}, u32[]{:S(2)}) copy-start(pred[64,640]{1,0:T(8,128)(4,1)S(1)} %broadcast_compare_fusion.3) | copy-start | bytes 122884 | tf_op jit(solution)/shard_map/while
  71.3 2.9 %copy-start.2 = (pred[64,640]{1,0:T(8,128)(4,1)S(1)}, pred[64,640]{1,0:T(8,128)(4,1)}, u32[]{:S(2)}) copy-start(pred[64,640]{1,0:T(8,128)(4,1)} %broadcast_compare_fusion.1) | copy-start | bytes 122884
  72.5 2.6 %copy-start.3 = (f32[2,8,64]{2,1,0:T(8,128)S(1)}, f32[2,8,64]{2,1,0:T(8,128)}, u32[]{:S(2)}) copy-start(f32[2,8,64]{2,1,0:T(8,128)} %get-tuple-element.280) | copy-start | bytes 12292
  72.5 2.6 %copy-start.4 = (f32[2,8,64,128]{3,2,1,0:T(8,128)S(1)}, f32[2,8,64,128]{3,2,1,0:T(8,128)}, u32[]{:S(2)}) copy-start(f32[2,8,64,128]{3,2,1,0:T(8,128)} %get-tuple-element.277) | copy-start | bytes 1572868
where the time goes:
time: 78.1 us; the launch traced here: 77.1 us
  waiting for transfers between devices  23.4 us (30%)
  matrix products  17.5 us (22%)
  local copies, waits for them, and re-layouts  16.5 us (21%)
  other arithmetic  12.8 us (16%)
  starting transfers between devices  6.49 us (8%)
    ppermute x3, waiting for transfers between devices, passed_along_2(): return lax.ppermute(block, axis, route)  23.4 us
    dot_general x4, matrix products, absorb_rows(): jnp.einsum('kgrn,nkd->kgrd', weights.astype(jnp.bfloat16), value_heads, p...  9.07 us
    dot_general x4, matrix products, absorb_rows(): jnp.einsum('kgrd,nkd->kgrn', query_heads, key_heads, preferred_element_ty...  6.58 us
    reduce_sum x4, other arithmetic, absorb_rows(): totals = totals * rescale + jnp.sum(weights, axis=-1)  5.17 us
    unnamed x14, local copies, waits for them, and re-layouts  5 us
    ppermute x1, starting transfers between devices, passed_along(): return lax.ppermute(block, axis, route)  4.91 us
    add x4, other arithmetic, absorb_rows(): totals = totals * rescale + jnp.sum(weights, axis=-1)  3.98 us
    while x12, local copies, waits for them, and re-layouts  3.28 us
  transfers between devices with their start and end apart: 4, of which 3 were waited for; matrix products, arithmetic and copies ran while one was open for 46% of the time, Pallas kernels for 0%

commit v1 on v0

--- a/solution.py
+++ b/solution.py
@@ -1,17 +1,320 @@
+import functools
 import math
 
 import jax
 import jax.numpy as jnp
 from jax import lax
+from jax.experimental import pallas as pl
+from jax.experimental.pallas import tpu as pltpu
 from jax.sharding import PartitionSpec as P
 
 HD = 128
 SPAN = 4
 PAGE = 64
-
+CAP = 8
 
 neg_floor = -1e30
 far_limit = 1 << 30
+log2_scale = math.log2(math.e) / math.sqrt(HD)
+
+ANY = pl.BlockSpec(memory_space=pl.ANY)
+VMEM = pl.BlockSpec(memory_space=pltpu.VMEM)
+SMEM = pl.BlockSpec(memory_space=pltpu.SMEM)
+
+
+def call(body, outs, in_specs, out_specs, scratch=(), flops=0, nbytes=0):
+    return pl.pallas_call(
+        body,
+        out_shape=outs,
+        in_specs=in_specs,
+        out_specs=out_specs,
+        scratch_shapes=scratch,
+        compiler_params=pltpu.CompilerParams(vmem_limit_bytes=40 << 20),
+        cost_estimate=pl.CostEstimate(flops=flops, bytes_accessed=nbytes, transcendentals=0),
+    )
+
+
+def sds(shape, dtype=jnp.bfloat16):
+    return jax.ShapeDtypeStruct(shape, dtype)
+
+
+def pack_body(
+    table, slot, length, nk, nv, pk, pv, pack0, pack1, fresh, limits, source, count, sem, *, cap
+):
+    position = lax.axis_index("ctx")
+    holders = lax.axis_size("ctx")
+    held = slot.shape[1] // holders
+    for i in range(holders * held):
+        limits[i] = 0
+        source[i] = 0
+    for i in range(holders):
+        count[i] = 0
+
+    @pl.loop(0, table.shape[2])
+    def _(i):
+        number = table[0, 0, i]
+        place = slot[0, number]
+        holder = place // held
+        nth = count[holder]
+        count[holder] = nth + 1
+        limits[holder * held + nth] = length[0, number]
+        source[holder * held + nth] = place - holder * held
+
+    copies = []
+    for j in range(cap):
+        first = pl.multiple_of(source[position * held + j] * PAGE, PAGE)
+        for g, pack in enumerate((pack0, pack1)):
+            for w, pages in enumerate((pk, pv)):
+                copy = pltpu.make_async_copy(
+                    pages.at[0, pl.ds(first, PAGE), pl.ds(g * HD, HD)],
+                    pack.at[w, pl.ds(j * PAGE, PAGE), :],
+                    sem.at[(j * 2 + g) * 2 + w],
+                )
+                copy.start()
+                copies.append(copy)
+    fresh[0] = nk[0]
+    fresh[1] = nv[0]
+    for copy in copies:
+        copy.wait()
+
+
+def holder_ids(position):
+    left = position < 2
+    return (
+        position,
+        position ^ 1,
+        jnp.where(left, 2, 1),
+        jnp.where(left, 3, 0),
+    )
+
+
+def is_inner(position):
+    return (position == 1) | (position == 2)
+
+
+def heads_of(ref, g, group):
+    return jnp.concatenate(
+        [ref[0, :, (g * group + i) * HD : (g * group + i + 1) * HD] for i in range(group)], axis=0
+    )
+
+
+def page_bias(limits, holder, held, cap):
+    column = lax.broadcasted_iota(jnp.int32, (1, cap * PAGE), 1)
+    page = column // PAGE
+    within = column - page * PAGE
+    limit = jnp.zeros((1, cap * PAGE), jnp.int32)
+    for j in range(cap):
+        limit = jnp.where(page == j, limits[holder * held + j], limit)
+    return jnp.where(within < limit, 0.0, neg_floor).astype(jnp.float32)
+
+
+def causal_bias(position, holder, rows, rows_dev):
+    row = lax.broadcasted_iota(jnp.int32, (rows, rows_dev), 0) % rows_dev
+    column = lax.broadcasted_iota(jnp.int32, (rows, rows_dev), 1)
+    allowed = position * rows_dev + row >= holder * rows_dev + column
+    return jnp.where(allowed, 0.0, neg_floor).astype(jnp.float32)
+
+
+def scored(q, k, bias):
+    s = lax.dot_general(q, k, (((1,), (1,)), ((), ())), preferred_element_type=jnp.float32)
+    return s * log2_scale + bias
+
+
+def attend(q, blocks, state=None):
+    scores = [scored(q, k, bias) for k, _, bias in blocks]
+    top = functools.reduce(jnp.maximum, [jnp.max(s, axis=1, keepdims=True) for s in scores])
+    if state is not None:
+        old_top, old_total, old_acc = state
+        top = jnp.maximum(top, old_top)
+        rescale = jnp.exp2(old_top - top)
+    total = 0.0
+    acc = 0.0
+    for s, (_, v, _) in zip(scores, blocks):
+        w = jnp.exp2(s - top)
+        total = total + jnp.sum(w, axis=1, keepdims=True)
+        acc = acc + jnp.dot(w.astype(jnp.bfloat16), v, preferred_element_type=jnp.float32)
+    if state is not None:
+        total = total + old_total * rescale
+        acc = acc + old_acc * rescale
+    return top, total, acc
+
+
+def save_state(stats, accs, g, state):
+    top, total, acc = state
+    lane = lax.broadcasted_iota(jnp.int32, acc.shape, 1)
+    stats[g] = jnp.where(lane == 0, top, total)
+    accs[g] = acc
+
+
+def load_state(stats, accs):
+    return stats[0][:, 0:1], stats[0][:, 1:2], accs[0]
+
+
+def first_body(
+    limits, q, own0, own1, near0, near1, far0, far1, n_own, n_near, n_far, n_last, stats, accs,
+    *, cap, shift
+):
+    position = lax.axis_index("ctx")
+    held = limits.shape[0] // lax.axis_size("ctx")
+    rows_dev = n_own.shape[1]
+    group = q.shape[2] // HD // 2
+
+    @pl.when(is_inner(position))
+    def _():
+        ids = holder_ids(position)
+        target = position ^ shift
+        biases = [page_bias(limits, ids[i], held, cap) for i in range(3)]
+        causal = [causal_bias(target, i, group * rows_dev, rows_dev) for i in ids]
+        fresh = jnp.concatenate(causal, axis=1)
+        for g, packs in enumerate(((own0, near0, far0), (own1, near1, far1))):
+            cols = slice(g * HD, (g + 1) * HD)
+            blocks = [(p[0], p[1], b) for p, b in zip(packs, biases)]
+            news = (n_own, n_near, n_far, n_last)
+            nk = jnp.concatenate([n[0, :, cols] for n in news], axis=0)
+            nv = jnp.concatenate([n[1, :, cols] for n in news], axis=0)
+            blocks.append((nk, nv, fresh))
+            save_state(stats, accs, g, attend(heads_of(q, g, group), blocks))
+
+
+def last_body(
+    limits, q_own, q_end, pack, taken, stats_own, acc_own, stats_end, acc_end, out_own, out_end,
+    *, cap, g
+):
+    position = lax.axis_index("ctx")
+    held = limits.shape[0] // lax.axis_size("ctx")
+    rows_dev = q_own.shape[1]
+    group = q_own.shape[2] // HD // 2
+
+    @pl.when(is_inner(position))
+    def _():
+        ids = holder_ids(position)
+        bias = page_bias(limits, ids[3], held, cap)
+        cols = slice(g * HD, (g + 1) * HD)
+        shut = jnp.where(lax.axis_index("grp") == 1, 0.0, neg_floor).astype(jnp.float32)
+        tk = jnp.concatenate([taken[i, 0, :, cols] for i in range(taken.shape[0])], axis=0)
+        tv = jnp.concatenate([taken[i, 1, :, cols] for i in range(taken.shape[0])], axis=0)
+        blocks = [
+            (pack[0], pack[1], bias),
+            (tk, tv, jnp.full((1, tk.shape[0]), shut, jnp.float32)),
+        ]
+        for q, stats, acc, out in (
+            (q_end, stats_end, acc_end, out_end),
+            (q_own, stats_own, acc_own, out_own),
+        ):
+            state = stats[g][:, 0:1], stats[g][:, 1:2], acc[g]
+            _, total, num = attend(heads_of(q, g, group), blocks, state)
+            result = (num / total).astype(jnp.bfloat16)
+            for i in range(group):
+                out[:, i * HD : (i + 1) * HD] = result[i * rows_dev : (i + 1) * rows_dev]
+
+
+def join_body(own0, own1, back0, back1, out):
+    inner = is_inner(lax.axis_index("ctx"))
+    half = own0.shape[1]
+
+    @pl.when(inner)
+    def _():
+        out[0, :, :half] = own0[...]
+        out[0, :, half:] = own1[...]
+
+    @pl.when(jnp.logical_not(inner))
+    def _():
+        out[0, :, :half] = back0[...]
+        out[0, :, half:] = back1[...]
+
+
+def chain_local(
+    queries, new_keys, new_values, page_keys, page_values, page_table, page_slot, page_length
+):
+    rows_dev = queries.shape[1]
+    width = new_keys.shape[2]
+    group = queries.shape[2] // width
+    holders = lax.axis_size("ctx")
+    heads = lax.axis_size("head")
+    held = page_slot.shape[1] // holders
+    cap = CAP
+    keys = cap * PAGE
+    side = [(i, i ^ 1) for i in range(holders)]
+    middle = []
+    for h in range(heads):
+        other = h ^ 1 if h ^ 1 < heads else h
+        for c in range(holders):
+            if c in (1, 2):
+                middle.append((c * heads + h, (3 - c) * heads + h))
+            else:
+                middle.append((c * heads + h, c * heads + other))
+
+    def swap_side(x):
+        return lax.ppermute(x, "ctx", side)
+
+    def swap_middle(x):
+        return lax.ppermute(x, ("ctx", "head"), middle)
+
+    pack0, pack1, fresh, limits = call(
+        functools.partial(pack_body, cap=cap),
+        (
+            sds((2, keys, HD)),
+            sds((2, keys, HD)),
+            sds((2, rows_dev, width)),
+            sds((holders * held,), jnp.int32),
+        ),
+        [SMEM, SMEM, SMEM, VMEM, VMEM, ANY, ANY],
+        (VMEM, VMEM, VMEM, SMEM),
+        [
+            pltpu.SMEM((holders * held,), jnp.int32),
+            pltpu.SMEM((holders,), jnp.int32),
+            pltpu.SemaphoreType.DMA((cap * 4,)),
+        ],
+        nbytes=2 << 20,
+    )(page_table, page_slot, page_length, new_keys, new_values, page_keys, page_values)
+
+    n_near = swap_side(fresh)
+    n_far = swap_middle(fresh)
+    near0 = swap_side(pack0)
+    far0 = swap_middle(pack0)
+    near1 = swap_side(pack1)
+    far1 = swap_middle(pack1)
+    q_end = swap_side(queries)
+    n_last = swap_middle(n_near)
+    last0 = swap_middle(near0)
+    last1 = swap_middle(near1)
+    taken = lax.ppermute(jnp.stack([fresh, n_near, n_far, n_last]), "grp", [(0, 1), (1, 0)])
+
+    rows = group * rows_dev
+    pair_flops = 4 * rows * HD
+    state = (sds((2, rows, HD), jnp.float32), sds((2, rows, HD), jnp.float32))
+    common = (pack0, pack1, near0, near1, far0, far1, fresh, n_near, n_far, n_last)
+
+    def first(q, shift):
+        return call(
+            functools.partial(first_body, cap=cap, shift=shift),
+            state,
+            [SMEM] + [VMEM] * 11,
+            (VMEM, VMEM),
+            flops=2 * pair_flops * (3 * keys + 4 * rows_dev),
+            nbytes=4 << 20,
+        )(limits, q, *common)
+
+    stats_own, acc_own = first(queries, 0)
+    stats_end, acc_end = first(q_end, 1)
+
+    def last(pack, g):
+        return call(
+            functools.partial(last_body, cap=cap, g=g),
+            (sds((rows_dev, group * HD)), sds((rows_dev, group * HD))),
+            [SMEM] + [VMEM] * 8,
+            (VMEM, VMEM),
+            flops=2 * pair_flops * (keys + 4 * rows_dev),
+            nbytes=3 << 20,
+        )(limits, queries, q_end, pack, taken, stats_own, acc_own, stats_end, acc_end)
+
+    own0, end0 = last(last0, 0)
+    back0 = swap_side(end0)
+    own1, end1 = last(last1, 1)
+    back1 = swap_side(end1)
+    return call(join_body, sds(queries.shape), [VMEM] * 4, VMEM, nbytes=1 << 20)(
+        own0, own1, back0, back1
+    )
 
 
 def passed_along(block, axis, distance):
@@ -26,7 +329,7 @@
     return lax.ppermute(block, axis, route)
 
 
-def local(
+def ring_local(
     queries, new_keys, new_values, page_keys, page_values, page_table, page_slot, page_length
 ):
     query_rows = queries[0]
@@ -131,5 +434,7 @@
         P("grp", None),
         P("grp", None),
     )
+    chain = mesh.shape["ctx"] == SPAN == 4 and mesh.shape["grp"] == 2
+    local = chain_local if chain else ring_local
     out_specs = P("grp", "ctx", "head")
     return jax.shard_map(local, mesh=mesh, in_specs=in_specs, out_specs=out_specs, check_vma=False)

time: 78.1 us -> 57.3 us (0.73)
  starting transfers between devices: 6.49 us -> 28.7 us
  matrix products: 17.5 us -> 0 us
  other arithmetic: 12.8 us -> 0.04 us
  local copies, waits for them, and re-layouts: 16.5 us -> 5.38 us
  waiting for transfers between devices: 23.4 us -> 17.7 us
  Pallas kernels: 0 us -> 5.06 us
    ppermute x4 -> x13, starting transfers between devices: 6.49 us -> 28.7 us  [the longest x6 25.6 us: swap_side(): return lax.ppermute(x, 'ctx', side)]
    dot_general x10 -> x0, matrix products: 17.5 us -> none  [the longest x4 9.07 us: absorb_rows(): jnp.einsum('kgrn,nkd->kgrd', weights.astype(jnp.bfloat16), value_heads, p...]
    ppermute x4 -> x13, waiting for transfers between devices: 23.4 us -> 17.7 us  [the longest x6 15.4 us: swap_side(): return lax.ppermute(x, 'ctx', side)]
    reduce_sum x4 -> x0, other arithmetic: 5.17 us -> none  [absorb_rows(): totals = totals * rescale + jnp.sum(weights, axis=-1)]
    pallas_call x0 -> x6, Pallas kernels: none -> 5.06 us  [the longest x1 1.94 us: chain_local(): call(functools.partial(pack_body, cap=cap), (sds((2, keys, HD)), sds((2,...]
    add x8 -> x0, other arithmetic: 3.99 us -> none  [the longest x4 3.98 us: absorb_rows(): totals = totals * rescale + jnp.sum(weights, axis=-1)]
    slice x4 -> x0, local copies, waits for them, and re-layouts: 3.96 us -> none  [the longest x3 2.83 us: advance(): travelling[1]]
    while x12 -> x0, local copies, waits for them, and re-layouts: 3.28 us -> none
  transfers between devices with their start and end apart: 4 -> 13, of which waited for: 3 -> 5; matrix products, arithmetic and copies ran while one was open for 46% -> 0% of each run, Pallas kernels for 0% -> 4%
where the time goes in v1:
time: 57.3 us; the launch traced here: 56.9 us
  starting transfers between devices  28.7 us (50%)
  waiting for transfers between devices  17.7 us (31%)
  local copies, waits for them, and re-layouts  5.38 us (9%)
  Pallas kernels  5.06 us (9%)
    ppermute x6, starting transfers between devices, swap_side(): return lax.ppermute(x, 'ctx', side)  25.6 us
    ppermute x6, waiting for transfers between devices, swap_side(): return lax.ppermute(x, 'ctx', side)  15.4 us
    unnamed x16, local copies, waits for them, and re-layouts  5.38 us
    pallas_call x1, Pallas kernels, chain_local(): call(functools.partial(pack_body, cap=cap), (sds((2, keys, HD)), sds((2,...  1.94 us
    ppermute x1, starting transfers between devices, chain_local(): lax.ppermute(jnp.stack([fresh, n_near, n_far, n_last]), 'grp', [(0, 1), (...  1.58 us
    ppermute x1, waiting for transfers between devices, chain_local(): lax.ppermute(jnp.stack([fresh, n_near, n_far, n_last]), 'grp', [(0, 1), (...  1.57 us
    ppermute x6, starting transfers between devices, swap_middle(): return lax.ppermute(x, ('ctx', 'head'), middle)  1.53 us
    pallas_call x2, Pallas kernels, last(): call(functools.partial(last_body, cap=cap, g=g), (sds((rows_dev, group *...  1.29 us
  transfers between devices with their start and end apart: 13, of which 5 were waited for; matrix products, arithmetic and copies ran while one was open for 0% of the time, Pallas kernels for 4%

profile of v1, /device:TPU:0, one launch (start us, length us, event | category | flops | bytes accessed | tf_op | source)
XLA Modules:
  0.0 56.9 jit_solution(12646344173974713582)
XLA Ops:
  0.0 0.0 copy-start.1
  0.0 0.9 %copy-done.1 = bf16[1,512,256]{2,1,0:T(8,128)(2,1)S(1)} copy-done((bf16[1,512,256]{2,1,0:T(8,128)(2,1)S(1)}, bf16[1,512,256]{2,1,0:T(8,128)(2,1)}, u32[]{:S(2)}) %copy-start.1) | copy-done | bytes 262168
  1.0 0.0 copy-start.2
  1.0 0.9 %copy-done.2 = bf16[1,512,256]{2,1,0:T(8,128)(2,1)S(1)} copy-done((bf16[1,512,256]{2,1,0:T(8,128)(2,1)S(1)}, bf16[1,512,256]{2,1,0:T(8,128)(2,1)}, u32[]{:S(2)}) %copy-start.2) | copy-done | bytes 262168
  1.9 0.0 copy-start.3
  1.9 0.8 %copy-done.3 = bf16[1,64,256]{2,1,0:T(8,128)(2,1)S(1)} copy-done((bf16[1,64,256]{2,1,0:T(8,128)(2,1)S(1)}, bf16[1,64,256]{2,1,0:T(8,128)(2,1)}, u32[]{:S(2)}) %copy-start.3) | copy-done | bytes 32792
  2.7 0.0 copy-start.4
  2.7 0.8 %copy-done.4 = bf16[1,64,256]{2,1,0:T(8,128)(2,1)S(1)} copy-done((bf16[1,64,256]{2,1,0:T(8,128)(2,1)S(1)}, bf16[1,64,256]{2,1,0:T(8,128)(2,1)}, u32[]{:S(2)}) %copy-start.4) | copy-done | bytes 32792
  3.4 0.0 copy-start.5
  3.4 0.7 %copy-done.5 = s32[1,1,16]{2,1,0:T(1,128)S(1)} copy-done((s32[1,1,16]{2,1,0:T(1,128)S(1)}, s32[1,1,16]{2,1,0:T(1,128)}, u32[]{:S(2)}) %copy-start.5) | copy-done | bytes 88
  4.1 0.0 copy-start.6
  4.1 0.7 %copy-done.6 = s32[1,32]{1,0:T(1,128)S(1)} copy-done((s32[1,32]{1,0:T(1,128)S(1)}, s32[1,32]{1,0:T(1,128)}, u32[]{:S(2)}) %copy-start.6) | copy-done | bytes 152
  4.7 0.0 copy-start.7
  4.7 0.7 %copy-done.7 = s32[1,32]{1,0:T(1,128)S(1)} copy-done((s32[1,32]{1,0:T(1,128)S(1)}, s32[1,32]{1,0:T(1,128)}, u32[]{:S(2)}) %copy-start.7) | copy-done | bytes 152
  5.4 0.0 copy-start
  5.4 1.9 %shard_map.82 = (bf16[2,512,128]{2,1,0:T(8,128)(2,1)S(1)}, bf16[2,512,128]{2,1,0:T(8,128)(2,1)S(1)}, bf16[2,64,256]{2,1,0:T(8,128)(2,1)S(1)}, s32[32]{0:T(128)S(1)}) custom-call(s32[1,1,16]{2,1,0:T(1,128)S(1)} %copy-done.5, s32[1,32]{1,0:T(1,128)S(1)} %copy-done.6, s32[1,32]{1,0:T(1,128)S(1)} %copy-done.7, bf16[1,64,256]{2,1,0:T(8,128)(2,1)S(1)} %copy-done.3, ...), custom_call_target="tpu_custom_call" | custom-call | bytes 2097152 | tf_op jit(solution)/shard_map/pallas_call | solution.py:253
  7.3 3.1 %collective-permute-start.1 = (bf16[2,512,128]{2,1,0:T(8,128)(2,1)S(1)}, bf16[2,512,128]{2,1,0:T(8,128)(2,1)S(1)}, u32[]{:S(2)}, u32[]{:S(2)}) collective-permute-start(bf16[2,512,128]{2,1,0:T(8,128)(2,1)S(1)} %get-tuple-element.18.own0), channel_id=1, source_target_pairs={{0,8},{8,0},{16,24},{24,16},{1,9},{9,1},{17,25},{25,17},{2,10},{10... | collective-permute-start | bytes 786440 | tf_op jit(solution)/shard_map/ppermute | solution.py:248
  10.5 0.1 collective-permute-start.7
  10.5 1.9 %collective-permute-start.3 = (bf16[2,64,256]{2,1,0:T(8,128)(2,1)S(1)}, bf16[2,64,256]{2,1,0:T(8,128)(2,1)S(1)}, u32[]{:S(2)}, u32[]{:S(2)}) collective-permute-start(bf16[2,64,256]{2,1,0:T(8,128)(2,1)S(1)} %get-tuple-element.19.n_own), channel_id=1, source_target_pairs={{0,8},{8,0},{16,24},{24,16},{1,9},{9,1},{17,25},{25,17},{2,10},{10... | collective-permute-start | bytes 196616 | tf_op jit(solution)/shard_map/ppermute | solution.py:248
  12.5 0.0 collective-permute-start.4
  12.5 0.5 collective-permute-start.8
  13.0 10.8 %collective-permute-done.3.n_near = bf16[2,64,256]{2,1,0:T(8,128)(2,1)S(1)} collective-permute-done((bf16[2,64,256]{2,1,0:T(8,128)(2,1)S(1)}, bf16[2,64,256]{2,1,0:T(8,128)(2,1)S(1)}, u32[]{:S(2)}, u32[]{:S(2)}) %collective-permute-start.3) | collective-permute-done | bytes 65568 | tf_op jit(solution)/shard_map/ppermute | solution.py:248
  23.8 0.0 collective-permute-start.5
  23.8 0.0 collective-permute-done.4.n_far
  23.8 0.5 collective-permute-start.9
  24.3 0.7 %collective-permute-done.5.n_last = bf16[2,64,256]{2,1,0:T(8,128)(2,1)S(1)} collective-permute-done((bf16[2,64,256]{2,1,0:T(8,128)(2,1)S(1)}, bf16[2,64,256]{2,1,0:T(8,128)(2,1)S(1)}, u32[]{:S(2)}, u32[]{:S(2)}) %collective-permute-start.5) | collective-permute-done | bytes 65568 | tf_op jit(solution)/shard_map/ppermute | solution.py:251
  25.0 0.0 copy-done
  25.0 5.4 %collective-permute-start = (bf16[1,64,2048]{2,1,0:T(8,128)(2,1)S(1)}, bf16[1,64,2048]{2,1,0:T(8,128)(2,1)S(1)}, u32[]{:S(2)}, u32[]{:S(2)}) collective-permute-start(bf16[1,64,2048]{2,1,0:T(8,128)(2,1)S(1)} %copy-done), channel_id=1, source_target_pairs={{0,8},{8,0},{16,24},{24,16},{1,9},{9,1},{17,25},{25,17},{2,10},{10... | collective-permute-start | bytes 786440 | tf_op jit(solution)/shard_map/ppermute | solution.py:248
  30.5 0.0 collective-permute-done.1.near0
  30.5 1.6 %collective-permute-start.6 = (bf16[4,2,64,256]{3,2,1,0:T(8,128)(2,1)S(1)}, bf16[4,2,64,256]{3,2,1,0:T(8,128)(2,1)S(1)}, u32[]{:S(2)}, u32[]{:S(2)}) collective-permute-start(bf16[4,2,64,256]{3,2,1,0:T(8,128)(2,1)S(1)} %pad_maximum_fusion), channel_id=1, source_target_pairs={{0,1},{1,0},{2,3},{3,2},{4,5},{5,4},{6,7},{7,6},{8,9},{9,8},{10,11... | collective-permute-start | bytes 786440 | tf_op jit(solution)/shard_map/ppermute | solution.py:281
  32.1 0.0 collective-permute-done.7.near1
  32.1 0.0 collective-permute-start.10
  32.1 0.0 collective-permute-done.8.far0
  32.1 0.5 collective-permute-start.2
  32.6 0.0 collective-permute-done.9.far1
  32.6 0.6 shard_map.83
  33.2 1.6 %collective-permute-done.q.q_end = bf16[1,64,2048]{2,1,0:T(8,128)(2,1)S(1)} collective-permute-done((bf16[1,64,2048]{2,1,0:T(8,128)(2,1)S(1)}, bf16[1,64,2048]{2,1,0:T(8,128)(2,1)S(1)}, u32[]{:S(2)}, u32[]{:S(2)}) %collective-permute-start) | collective-permute-done | bytes 262176 | tf_op jit(solution)/shard_map/ppermute | solution.py:248
  34.8 0.6 shard_map.84
  35.4 1.6 %collective-permute-done.6.taken = bf16[4,2,64,256]{3,2,1,0:T(8,128)(2,1)S(1)} collective-permute-done((bf16[4,2,64,256]{3,2,1,0:T(8,128)(2,1)S(1)}, bf16[4,2,64,256]{3,2,1,0:T(8,128)(2,1)S(1)}, u32[]{:S(2)}, u32[]{:S(2)}) %collective-permute-start.6) | collective-permute-done | bytes 262176 | tf_op jit(solution)/shard_map/ppermute | solution.py:281
  37.0 0.0 collective-permute-done.10.pack
  37.0 0.6 shard_map.86
  37.5 11.1 %collective-permute-start.12 = (bf16[64,1024]{1,0:T(8,128)(2,1)S(1)}, bf16[64,1024]{1,0:T(8,128)(2,1)S(1)}, u32[]{:S(2)}, u32[]{:S(2)}) collective-permute-start(bf16[64,1024]{1,0:T(8,128)(2,1)S(1)} %get-tuple-element.28), channel_id=1, source_target_pairs={{0,8},{8,0},{16,24},{24,16},{1,9},{9,1},{17,25},{25,17},{2,10},{10... | collective-permute-start | bytes 393224 | tf_op jit(solution)/shard_map/ppermute | solution.py:248
  48.7 0.0 collective-permute-done.2.pack
  48.7 0.7 %shard_map.85 = (bf16[64,1024]{1,0:T(8,128)(2,1)S(1)}, bf16[64,1024]{1,0:T(8,128)(2,1)S(1)}) custom-call(s32[32]{0:T(128)S(1)} %get-tuple-element.17.limits, bf16[1,64,2048]{2,1,0:T(8,128)(2,1)S(1)} %copy-done, bf16[1,64,2048]{2,1,0:T(8,128)(2,1)S(1)} %collective-permute-done.q.q_end, bf16[2,512,128]{2,1,0:T(8,128)(2,1)S(1)} %collective-permute-done.2.pack, ...), custom_call_target="tpu_custom_call" | custom-call | flops 402653184 | bytes 3145728 | tf_op jit(solution)/shard_map/pallas_call | solution.py:302
  49.4 3.9 %collective-permute-start.11 = (bf16[64,1024]{1,0:T(8,128)(2,1)S(1)}, bf16[64,1024]{1,0:T(8,128)(2,1)S(1)}, u32[]{:S(2)}, u32[]{:S(2)}) collective-permute-start(bf16[64,1024]{1,0:T(8,128)(2,1)S(1)} %get-tuple-element.27), channel_id=1, source_target_pairs={{0,8},{8,0},{16,24},{24,16},{1,9},{9,1},{17,25},{25,17},{2,10},{10... | collective-permute-start | bytes 393224 | tf_op jit(solution)/shard_map/ppermute | solution.py:248
  53.3 0.0 collective-permute-done.12.back1
  53.3 2.9 %collective-permute-done.11.back0 = bf16[64,1024]{1,0:T(8,128)(2,1)S(1)} collective-permute-done((bf16[64,1024]{1,0:T(8,128)(2,1)S(1)}, bf16[64,1024]{1,0:T(8,128)(2,1)S(1)}, u32[]{:S(2)}, u32[]{:S(2)}) %collective-permute-start.11) | collective-permute-done | bytes 131104 | tf_op jit(solution)/shard_map/ppermute | solution.py:248
  56.2 0.7 %shard_map.87 = bf16[1,64,2048]{2,1,0:T(8,128)(2,1)} custom-call(bf16[64,1024]{1,0:T(8,128)(2,1)S(1)} %get-tuple-element.25.own0, bf16[64,1024]{1,0:T(8,128)(2,1)S(1)} %get-tuple-element.26.own1, bf16[64,1024]{1,0:T(8,128)(2,1)S(1)} %collective-permute-done.11.back0, bf16[64,1024]{1,0:T(8,128)(2,1)S(1)} %collective-permute-done.12.back1), custom_call_target="tpu_custom_call" | custom-call | bytes 1048576 | tf_op jit(solution)/shard_map/pallas_call | solution.py:315
  (1 shorter events, 0.0 us)
Async XLA Ops:
  0.0 0.9 %copy-start.1 = (bf16[1,512,256]{2,1,0:T(8,128)(2,1)S(1)}, bf16[1,512,256]{2,1,0:T(8,128)(2,1)}, u32[]{:S(2)}) copy-start(bf16[1,512,256]{2,1,0:T(8,128)(2,1)} %pk.1) | copy-start | bytes 786436
  1.0 0.9 %copy-start.2 = (bf16[1,512,256]{2,1,0:T(8,128)(2,1)S(1)}, bf16[1,512,256]{2,1,0:T(8,128)(2,1)}, u32[]{:S(2)}) copy-start(bf16[1,512,256]{2,1,0:T(8,128)(2,1)} %pv.1) | copy-start | bytes 786436
  1.9 0.8 %copy-start.3 = (bf16[1,64,256]{2,1,0:T(8,128)(2,1)S(1)}, bf16[1,64,256]{2,1,0:T(8,128)(2,1)}, u32[]{:S(2)}) copy-start(bf16[1,64,256]{2,1,0:T(8,128)(2,1)} %nk.1) | copy-start | bytes 98308
  2.7 0.8 %copy-start.4 = (bf16[1,64,256]{2,1,0:T(8,128)(2,1)S(1)}, bf16[1,64,256]{2,1,0:T(8,128)(2,1)}, u32[]{:S(2)}) copy-start(bf16[1,64,256]{2,1,0:T(8,128)(2,1)} %nv.1) | copy-start | bytes 98308
  3.4 0.7 %copy-start.5 = (s32[1,1,16]{2,1,0:T(1,128)S(1)}, s32[1,1,16]{2,1,0:T(1,128)}, u32[]{:S(2)}) copy-start(s32[1,1,16]{2,1,0:T(1,128)} %table.1) | copy-start | bytes 196
  4.1 0.7 %copy-start.6 = (s32[1,32]{1,0:T(1,128)S(1)}, s32[1,32]{1,0:T(1,128)}, u32[]{:S(2)}) copy-start(s32[1,32]{1,0:T(1,128)} %slot.1) | copy-start | bytes 388
  4.7 0.7 %copy-start.7 = (s32[1,32]{1,0:T(1,128)S(1)}, s32[1,32]{1,0:T(1,128)}, u32[]{:S(2)}) copy-start(s32[1,32]{1,0:T(1,128)} %length.1) | copy-start | bytes 388
  5.4 19.7 %copy-start = (bf16[1,64,2048]{2,1,0:T(8,128)(2,1)S(1)}, bf16[1,64,2048]{2,1,0:T(8,128)(2,1)}, u32[]{:S(2)}) copy-start(bf16[1,64,2048]{2,1,0:T(8,128)(2,1)} %q_own.3) | copy-start | bytes 786436
  7.3 23.2 %collective-permute-start.1 = (bf16[2,512,128]{2,1,0:T(8,128)(2,1)S(1)}, bf16[2,512,128]{2,1,0:T(8,128)(2,1)S(1)}, u32[]{:S(2)}, u32[]{:S(2)}) collective-permute-start(bf16[2,512,128]{2,1,0:T(8,128)(2,1)S(1)} %get-tuple-element.18.own0), channel_id=1, source_target_pairs={{0,8},{8,0},{16,24},{24,16},{1,9},{9,1},{17,25},{25,17},{2,10},{10... | collective-permute-start | bytes 786440 | tf_op jit(solution)/shard_map/ppermute | solution.py:248
  10.5 21.7 %collective-permute-start.7 = (bf16[2,512,128]{2,1,0:T(8,128)(2,1)S(1)}, bf16[2,512,128]{2,1,0:T(8,128)(2,1)S(1)}, u32[]{:S(2)}, u32[]{:S(2)}) collective-permute-start(bf16[2,512,128]{2,1,0:T(8,128)(2,1)S(1)} %get-tuple-element.20.own1), channel_id=1, source_target_pairs={{0,8},{8,0},{16,24},{24,16},{1,9},{9,1},{17,25},{25,17},{2,10},{10... | collective-permute-start | bytes 786440 | tf_op jit(solution)/shard_map/ppermute | solution.py:248
  10.5 13.2 %collective-permute-start.3 = (bf16[2,64,256]{2,1,0:T(8,128)(2,1)S(1)}, bf16[2,64,256]{2,1,0:T(8,128)(2,1)S(1)}, u32[]{:S(2)}, u32[]{:S(2)}) collective-permute-start(bf16[2,64,256]{2,1,0:T(8,128)(2,1)S(1)} %get-tuple-element.19.n_own), channel_id=1, source_target_pairs={{0,8},{8,0},{16,24},{24,16},{1,9},{9,1},{17,25},{25,17},{2,10},{10... | collective-permute-start | bytes 196616 | tf_op jit(solution)/shard_map/ppermute | solution.py:248
  12.5 11.3 %collective-permute-start.4 = (bf16[2,64,256]{2,1,0:T(8,128)(2,1)S(1)}, bf16[2,64,256]{2,1,0:T(8,128)(2,1)S(1)}, u32[]{:S(2)}, u32[]{:S(2)}) collective-permute-start(bf16[2,64,256]{2,1,0:T(8,128)(2,1)S(1)} %get-tuple-element.19.n_own), channel_id=1, source_target_pairs={{0,2},{8,16},{16,8},{24,26},{2,0},{10,18},{18,10},{26,24},{4,6},{1... | collective-permute-start | bytes 196616 | tf_op jit(solution)/shard_map/ppermute | solution.py:251
  12.5 19.6 %collective-permute-start.8 = (bf16[2,512,128]{2,1,0:T(8,128)(2,1)S(1)}, bf16[2,512,128]{2,1,0:T(8,128)(2,1)S(1)}, u32[]{:S(2)}, u32[]{:S(2)}) collective-permute-start(bf16[2,512,128]{2,1,0:T(8,128)(2,1)S(1)} %get-tuple-element.18.own0), channel_id=1, source_target_pairs={{0,2},{8,16},{16,8},{24,26},{2,0},{10,18},{18,10},{26,24},{4,6},{1... | collective-permute-start | bytes 786440 | tf_op jit(solution)/shard_map/ppermute | solution.py:251
  23.8 1.3 %collective-permute-start.5 = (bf16[2,64,256]{2,1,0:T(8,128)(2,1)S(1)}, bf16[2,64,256]{2,1,0:T(8,128)(2,1)S(1)}, u32[]{:S(2)}, u32[]{:S(2)}) collective-permute-start(bf16[2,64,256]{2,1,0:T(8,128)(2,1)S(1)} %collective-permute-done.3.n_near), channel_id=1, source_target_pairs={{0,2},{8,16},{16,8},{24,26},{2,0},{10,18},{18,10},{26,24},{4,6},{1... | collective-permute-start | bytes 196616 | tf_op jit(solution)/shard_map/ppermute | solution.py:251
  23.8 8.9 %collective-permute-start.9 = (bf16[2,512,128]{2,1,0:T(8,128)(2,1)S(1)}, bf16[2,512,128]{2,1,0:T(8,128)(2,1)S(1)}, u32[]{:S(2)}, u32[]{:S(2)}) collective-permute-start(bf16[2,512,128]{2,1,0:T(8,128)(2,1)S(1)} %get-tuple-element.20.own1), channel_id=1, source_target_pairs={{0,2},{8,16},{16,8},{24,26},{2,0},{10,18},{18,10},{26,24},{4,6},{1... | collective-permute-start | bytes 786440 | tf_op jit(solution)/shard_map/ppermute | solution.py:251
  25.0 9.8 %collective-permute-start = (bf16[1,64,2048]{2,1,0:T(8,128)(2,1)S(1)}, bf16[1,64,2048]{2,1,0:T(8,128)(2,1)S(1)}, u32[]{:S(2)}, u32[]{:S(2)}) collective-permute-start(bf16[1,64,2048]{2,1,0:T(8,128)(2,1)S(1)} %copy-done), channel_id=1, source_target_pairs={{0,8},{8,0},{16,24},{24,16},{1,9},{9,1},{17,25},{25,17},{2,10},{10... | collective-permute-start | bytes 786440 | tf_op jit(solution)/shard_map/ppermute | solution.py:248
  30.5 6.4 %collective-permute-start.6 = (bf16[4,2,64,256]{3,2,1,0:T(8,128)(2,1)S(1)}, bf16[4,2,64,256]{3,2,1,0:T(8,128)(2,1)S(1)}, u32[]{:S(2)}, u32[]{:S(2)}) collective-permute-start(bf16[4,2,64,256]{3,2,1,0:T(8,128)(2,1)S(1)} %pad_maximum_fusion), channel_id=1, source_target_pairs={{0,1},{1,0},{2,3},{3,2},{4,5},{5,4},{6,7},{7,6},{8,9},{9,8},{10,11... | collective-permute-start | bytes 786440 | tf_op jit(solution)/shard_map/ppermute | solution.py:281
  32.1 4.9 %collective-permute-start.10 = (bf16[2,512,128]{2,1,0:T(8,128)(2,1)S(1)}, bf16[2,512,128]{2,1,0:T(8,128)(2,1)S(1)}, u32[]{:S(2)}, u32[]{:S(2)}) collective-permute-start(bf16[2,512,128]{2,1,0:T(8,128)(2,1)S(1)} %collective-permute-done.7.near1), channel_id=1, source_target_pairs={{0,2},{8,16},{16,8},{24,26},{2,0},{10,18},{18,10},{26,24},{4,6},{1... | collective-permute-start | bytes 786440 | tf_op jit(solution)/shard_map/ppermute | solution.py:251
  32.1 16.5 %collective-permute-start.2 = (bf16[2,512,128]{2,1,0:T(8,128)(2,1)S(1)}, bf16[2,512,128]{2,1,0:T(8,128)(2,1)S(1)}, u32[]{:S(2)}, u32[]{:S(2)}) collective-permute-start(bf16[2,512,128]{2,1,0:T(8,128)(2,1)S(1)} %collective-permute-done.1.near0), channel_id=1, source_target_pairs={{0,2},{8,16},{16,8},{24,26},{2,0},{10,18},{18,10},{26,24},{4,6},{1... | collective-permute-start | bytes 786440 | tf_op jit(solution)/shard_map/ppermute | solution.py:251
  37.5 15.7 %collective-permute-start.12 = (bf16[64,1024]{1,0:T(8,128)(2,1)S(1)}, bf16[64,1024]{1,0:T(8,128)(2,1)S(1)}, u32[]{:S(2)}, u32[]{:S(2)}) collective-permute-start(bf16[64,1024]{1,0:T(8,128)(2,1)S(1)} %get-tuple-element.28), channel_id=1, source_target_pairs={{0,8},{8,0},{16,24},{24,16},{1,9},{9,1},{17,25},{25,17},{2,10},{10... | collective-permute-start | bytes 393224 | tf_op jit(solution)/shard_map/ppermute | solution.py:248
  49.4 6.8 %collective-permute-start.11 = (bf16[64,1024]{1,0:T(8,128)(2,1)S(1)}, bf16[64,1024]{1,0:T(8,128)(2,1)S(1)}, u32[]{:S(2)}, u32[]{:S(2)}) collective-permute-start(bf16[64,1024]{1,0:T(8,128)(2,1)S(1)} %get-tuple-element.27), channel_id=1, source_target_pairs={{0,8},{8,0},{16,24},{24,16},{1,9},{9,1},{17,25},{25,17},{2,10},{10... | collective-permute-start | bytes 393224 | tf_op jit(solution)/shard_map/ppermute | solution.py:248

commit v2 on v1

--- a/solution.py
+++ b/solution.py
@@ -8,6 +8,7 @@
 from jax.experimental.pallas import tpu as pltpu
 from jax.sharding import PartitionSpec as P
 
+
 HD = 128
 SPAN = 4
 PAGE = 64
@@ -17,7 +18,7 @@
 far_limit = 1 << 30
 log2_scale = math.log2(math.e) / math.sqrt(HD)
 
-ANY = pl.BlockSpec(memory_space=pl.ANY)
+HBM = pl.BlockSpec(memory_space=pltpu.HBM)
 VMEM = pl.BlockSpec(memory_space=pltpu.VMEM)
 SMEM = pl.BlockSpec(memory_space=pltpu.SMEM)
 
@@ -38,20 +39,42 @@
     return jax.ShapeDtypeStruct(shape, dtype)
 
 
+def ready_body(nk, nv, q, fresh, q0, q1, sem):
+    half = q0.shape[1]
+    copies = [
+        pltpu.make_async_copy(nk.at[0], fresh.at[0], sem.at[0]),
+        pltpu.make_async_copy(nv.at[0], fresh.at[1], sem.at[1]),
+        pltpu.make_async_copy(q.at[0, :, pl.ds(0, half)], q0, sem.at[2]),
+        pltpu.make_async_copy(q.at[0, :, pl.ds(half, half)], q1, sem.at[3]),
+    ]
+    for copy in copies:
+        copy.start()
+    for copy in copies:
+        copy.wait()
+
+
 def pack_body(
-    table, slot, length, nk, nv, pk, pv, pack0, pack1, fresh, limits, source, count, sem, *, cap
+    table_in, slot_in, length_in, pk, pv, pack0, pack1, limits, table, slot, length, source, count,
+    sem, *, cap
 ):
     position = lax.axis_index("ctx")
     holders = lax.axis_size("ctx")
     held = slot.shape[1] // holders
+    reads = [
+        pltpu.make_async_copy(table_in, table, sem.at[0]),
+        pltpu.make_async_copy(slot_in, slot, sem.at[1]),
+        pltpu.make_async_copy(length_in, length, sem.at[2]),
+    ]
+    for copy in reads:
+        copy.start()
     for i in range(holders * held):
         limits[i] = 0
         source[i] = 0
     for i in range(holders):
         count[i] = 0
-
-    @pl.loop(0, table.shape[2])
-    def _(i):
+    for copy in reads:
+        copy.wait()
+    for i in range(table.shape[2]):
         number = table[0, 0, i]
         place = slot[0, number]
         holder = place // held
@@ -61,9 +84,9 @@
         source[holder * held + nth] = place - holder * held
 
     copies = []
-    for j in range(cap):
-        first = pl.multiple_of(source[position * held + j] * PAGE, PAGE)
-        for g, pack in enumerate((pack0, pack1)):
+    for g, pack in enumerate((pack0, pack1)):
+        for j in range(cap):
+            first = pl.multiple_of(source[position * held + j] * PAGE, PAGE)
             for w, pages in enumerate((pk, pv)):
                 copy = pltpu.make_async_copy(
                     pages.at[0, pl.ds(first, PAGE), pl.ds(g * HD, HD)],
@@ -72,8 +95,6 @@
                 )
                 copy.start()
                 copies.append(copy)
-    fresh[0] = nk[0]
-    fresh[1] = nv[0]
     for copy in copies:
         copy.wait()
 
@@ -92,9 +113,9 @@
     return (position == 1) | (position == 2)
 
 
-def heads_of(ref, g, group):
+def heads_of(ref):
     return jnp.concatenate(
-        [ref[0, :, (g * group + i) * HD : (g * group + i + 1) * HD] for i in range(group)], axis=0
+        [ref[:, i * HD : (i + 1) * HD] for i in range(ref.shape[1] // HD)], axis=0
     )
 
 
@@ -122,89 +143,74 @@
 
 def attend(q, blocks, state=None):
     scores = [scored(q, k, bias) for k, _, bias in blocks]
+    shape = (q.shape[0], HD)
     top = functools.reduce(jnp.maximum, [jnp.max(s, axis=1, keepdims=True) for s in scores])
     if state is not None:
         old_top, old_total, old_acc = state
-        top = jnp.maximum(top, old_top)
-        rescale = jnp.exp2(old_top - top)
+        wide = jnp.maximum(jnp.broadcast_to(top, shape), old_top)
+        rescale = jnp.exp2(old_top - wide)
+        top = wide[:, 0:1]
     total = 0.0
     acc = 0.0
     for s, (_, v, _) in zip(scores, blocks):
         w = jnp.exp2(s - top)
         total = total + jnp.sum(w, axis=1, keepdims=True)
         acc = acc + jnp.dot(w.astype(jnp.bfloat16), v, preferred_element_type=jnp.float32)
-    if state is not None:
-        total = total + old_total * rescale
-        acc = acc + old_acc * rescale
-    return top, total, acc
-
-
-def save_state(stats, accs, g, state):
-    top, total, acc = state
-    lane = lax.broadcasted_iota(jnp.int32, acc.shape, 1)
-    stats[g] = jnp.where(lane == 0, top, total)
-    accs[g] = acc
-
-
-def load_state(stats, accs):
-    return stats[0][:, 0:1], stats[0][:, 1:2], accs[0]
-
-
-def first_body(
-    limits, q, own0, own1, near0, near1, far0, far1, n_own, n_near, n_far, n_last, stats, accs,
-    *, cap, shift
+    if state is None:
+        return top, total, acc
+    total = jnp.broadcast_to(total, shape) + old_total * rescale
+    return total, acc + old_acc * rescale
+
+
+def early_body(
+    limits, q_own, q_end, own, near, far, n_own, n_near, n_far, n_last, tops, totals, accs, *, cap, g
 ):
     position = lax.axis_index("ctx")
     held = limits.shape[0] // lax.axis_size("ctx")
     rows_dev = n_own.shape[1]
-    group = q.shape[2] // HD // 2
+    rows = accs.shape[1]
 
     @pl.when(is_inner(position))
     def _():
         ids = holder_ids(position)
-        target = position ^ shift
-        biases = [page_bias(limits, ids[i], held, cap) for i in range(3)]
-        causal = [causal_bias(target, i, group * rows_dev, rows_dev) for i in ids]
-        fresh = jnp.concatenate(causal, axis=1)
-        for g, packs in enumerate(((own0, near0, far0), (own1, near1, far1))):
-            cols = slice(g * HD, (g + 1) * HD)
-            blocks = [(p[0], p[1], b) for p, b in zip(packs, biases)]
-            news = (n_own, n_near, n_far, n_last)
-            nk = jnp.concatenate([n[0, :, cols] for n in news], axis=0)
-            nv = jnp.concatenate([n[1, :, cols] for n in news], axis=0)
-            blocks.append((nk, nv, fresh))
-            save_state(stats, accs, g, attend(heads_of(q, g, group), blocks))
-
-
-def last_body(
-    limits, q_own, q_end, pack, taken, stats_own, acc_own, stats_end, acc_end, out_own, out_end,
-    *, cap, g
+        cols = slice(g * HD, (g + 1) * HD)
+        news = (n_own, n_near, n_far, n_last)
+        nk = jnp.concatenate([n[0, :, cols] for n in news], axis=0)
+        nv = jnp.concatenate([n[1, :, cols] for n in news], axis=0)
+        paged = [
+            (p[0], p[1], page_bias(limits, i, held, cap)) for p, i in zip((own, near, far), ids)
+        ]
+        for t, q in enumerate((q_own, q_end)):
+            causal = [causal_bias(position ^ t, i, rows, rows_dev) for i in ids]
+            fresh = (nk, nv, jnp.concatenate(causal, axis=1))
+            top, total, acc = attend(heads_of(q), paged + [fresh])
+            tops[t] = jnp.broadcast_to(top, acc.shape)
+            totals[t] = jnp.broadcast_to(total, acc.shape)
+            accs[t] = acc
+
+
+def late_body(
+    limits, q_own, q_end, pack, taken, tops, totals, accs, out_own, out_end, *, cap, g
 ):
     position = lax.axis_index("ctx")
     held = limits.shape[0] // lax.axis_size("ctx")
-    rows_dev = q_own.shape[1]
-    group = q_own.shape[2] // HD // 2
+    rows_dev = q_own.shape[0]
 
     @pl.when(is_inner(position))
     def _():
         ids = holder_ids(position)
-        bias = page_bias(limits, ids[3], held, cap)
         cols = slice(g * HD, (g + 1) * HD)
         shut = jnp.where(lax.axis_index("grp") == 1, 0.0, neg_floor).astype(jnp.float32)
         tk = jnp.concatenate([taken[i, 0, :, cols] for i in range(taken.shape[0])], axis=0)
         tv = jnp.concatenate([taken[i, 1, :, cols] for i in range(taken.shape[0])], axis=0)
         blocks = [
-            (pack[0], pack[1], bias),
+            (pack[0], pack[1], page_bias(limits, ids[3], held, cap)),
             (tk, tv, jnp.full((1, tk.shape[0]), shut, jnp.float32)),
         ]
-        for q, stats, acc, out in (
-            (q_end, stats_end, acc_end, out_end),
-            (q_own, stats_own, acc_own, out_own),
-        ):
-            state = stats[g][:, 0:1], stats[g][:, 1:2], acc[g]
-            _, total, num = attend(heads_of(q, g, group), blocks, state)
+        for t, q, out in ((1, q_end, out_end), (0, q_own, out_own)):
+            total, num = attend(heads_of(q), blocks, (tops[t], totals[t], accs[t]))
             result = (num / total).astype(jnp.bfloat16)
-            for i in range(group):
+            for i in range(out.shape[1] // HD):
                 out[:, i * HD : (i + 1) * HD] = result[i * rows_dev : (i + 1) * rows_dev]
 
 
@@ -223,7 +229,11 @@
         out[0, :, half:] = back1[...]
 
 
-def chain_local(
+def chain_local(*args):
+    return chain_steps(*args)
+
+
+def chain_steps(
     queries, new_keys, new_values, page_keys, page_values, page_table, page_slot, page_length
 ):
     rows_dev = queries.shape[1]
@@ -250,67 +260,76 @@
     def swap_middle(x):
         return lax.ppermute(x, ("ctx", "head"), middle)
 
-    pack0, pack1, fresh, limits = call(
+    def swap_pools(x):
+        return lax.ppermute(x, "grp", [(0, 1), (1, 0)])
+
+    half = sds((rows_dev, group * HD))
+    fresh, q0, q1 = call(
+        ready_body,
+        (sds((2, rows_dev, width)), half, half),
+        [HBM] * 3,
+        (VMEM,) * 3,
+        [pltpu.SemaphoreType.DMA((4,))],
+        nbytes=1 << 20,
+    )(new_keys, new_values, queries)
+    pack0, pack1, limits = call(
         functools.partial(pack_body, cap=cap),
-        (
-            sds((2, keys, HD)),
-            sds((2, keys, HD)),
-            sds((2, rows_dev, width)),
-            sds((holders * held,), jnp.int32),
-        ),
-        [SMEM, SMEM, SMEM, VMEM, VMEM, ANY, ANY],
-        (VMEM, VMEM, VMEM, SMEM),
+        (sds((2, keys, HD)), sds((2, keys, HD)), sds((holders * held,), jnp.int32)),
+        [HBM] * 5,
+        (VMEM, VMEM, SMEM),
         [
+            pltpu.SMEM(page_table.shape, jnp.int32),
+            pltpu.SMEM(page_slot.shape, jnp.int32),
+            pltpu.SMEM(page_length.shape, jnp.int32),
             pltpu.SMEM((holders * held,), jnp.int32),
             pltpu.SMEM((holders,), jnp.int32),
             pltpu.SemaphoreType.DMA((cap * 4,)),
         ],
         nbytes=2 << 20,
-    )(page_table, page_slot, page_length, new_keys, new_values, page_keys, page_values)
+    )(page_table, page_slot, page_length, page_keys, page_values)
 
     n_near = swap_side(fresh)
     n_far = swap_middle(fresh)
+    q0_end = swap_side(q0)
     near0 = swap_side(pack0)
     far0 = swap_middle(pack0)
+    n_last = swap_middle(n_near)
     near1 = swap_side(pack1)
     far1 = swap_middle(pack1)
-    q_end = swap_side(queries)
-    n_last = swap_middle(n_near)
+    q1_end = swap_side(q1)
+    taken = swap_pools(jnp.stack([fresh, n_near, n_far, n_last]))
     last0 = swap_middle(near0)
     last1 = swap_middle(near1)
-    taken = lax.ppermute(jnp.stack([fresh, n_near, n_far, n_last]), "grp", [(0, 1), (1, 0)])
 
     rows = group * rows_dev
     pair_flops = 4 * rows * HD
-    state = (sds((2, rows, HD), jnp.float32), sds((2, rows, HD), jnp.float32))
-    common = (pack0, pack1, near0, near1, far0, far1, fresh, n_near, n_far, n_last)
-
-    def first(q, shift):
+    state = (sds((2, rows, HD), jnp.float32),) * 3
+
+    def early(g, q, q_end, own, near, far):
         return call(
-            functools.partial(first_body, cap=cap, shift=shift),
+            functools.partial(early_body, cap=cap, g=g),
             state,
-            [SMEM] + [VMEM] * 11,
-            (VMEM, VMEM),
+            [SMEM] + [VMEM] * 9,
+            (VMEM,) * 3,
             flops=2 * pair_flops * (3 * keys + 4 * rows_dev),
             nbytes=4 << 20,
-        )(limits, q, *common)
-
-    stats_own, acc_own = first(queries, 0)
-    stats_end, acc_end = first(q_end, 1)
-
-    def last(pack, g):
+        )(limits, q, q_end, own, near, far, fresh, n_near, n_far, n_last)
+
+    def late(g, q, q_end, pack, carried):
         return call(
-            functools.partial(last_body, cap=cap, g=g),
-            (sds((rows_dev, group * HD)), sds((rows_dev, group * HD))),
-            [SMEM] + [VMEM] * 8,
+            functools.partial(late_body, cap=cap, g=g),
+            (half, half),
+            [SMEM] + [VMEM] * 7,
             (VMEM, VMEM),
             flops=2 * pair_flops * (keys + 4 * rows_dev),
             nbytes=3 << 20,
-        )(limits, queries, q_end, pack, taken, stats_own, acc_own, stats_end, acc_end)
-
-    own0, end0 = last(last0, 0)
+        )(limits, q, q_end, pack, taken, *carried)
+
+    carried0 = early(0, q0, q0_end, pack0, near0, far0)
+    carried1 = early(1, q1, q1_end, pack1, near1, far1)
+    own0, end0 = late(0, q0, q0_end, last0, carried0)
     back0 = swap_side(end0)
-    own1, end1 = last(last1, 1)
+    own1, end1 = late(1, q1, q1_end, last1, carried1)
     back1 = swap_side(end1)
     return call(join_body, sds(queries.shape), [VMEM] * 4, VMEM, nbytes=1 << 20)(
         own0, own1, back0, back1
@@ -417,7 +436,7 @@
     carried = absorb_rows(
         carried, moving_rows[0], moving_rows[1], block_limits((position + 1) % cycle_size)
     )
-    maxima, totals, accumulated = carried
+    _, totals, accumulated = carried
     attended = accumulated / totals[..., None]
     attended = attended.transpose(2, 0, 1, 3).reshape(rows_dev, query_count * HD)
     return attended.astype(jnp.bfloat16)[None]

time: 57.3 us -> 48.5 us (0.85)
  starting transfers between devices: 28.7 us -> 25 us
  waiting for transfers between devices: 17.7 us -> 14.3 us
  local copies, waits for them, and re-layouts: 5.38 us -> 3.87 us
    ppermute x6 -> x7, starting transfers between devices: 25.6 us -> 22.3 us  [swap_side(): return lax.ppermute(x, 'ctx', side)]
    ppermute x1, waiting for transfers between devices: 1.57 us -> 0.01 us  [swap_pools(): return lax.ppermute(x, 'grp', [(0, 1), (1, 0)])]
    unnamed x16, local copies, waits for them, and re-layouts: 5.38 us -> 3.87 us
    ppermute x6 -> x7, waiting for transfers between devices: 15.4 us -> 14.3 us  [swap_side(): return lax.ppermute(x, 'ctx', side)]
    ppermute x6, waiting for transfers between devices: 0.75 us -> 0.02 us  [swap_middle(): return lax.ppermute(x, ('ctx', 'head'), middle)]
    pallas_call x6 -> x7, Pallas kernels: 5.06 us -> 4.91 us  [the longest x1 1.8 us: chain_steps(): call(functools.partial(pack_body, cap=cap), (sds((2, keys, HD)), sds((2,...]
  transfers between devices with their start and end apart: 13 -> 14, of which waited for: 5 -> 5; matrix products, arithmetic and copies ran while one was open for 0% -> 0% of each run, Pallas kernels for 4% -> 5%
where the time goes in v2:
time: 48.5 us; the launch traced here: 48.3 us
  starting transfers between devices  25 us (52%)
  waiting for transfers between devices  14.3 us (29%)
  Pallas kernels  4.91 us (10%)
  local copies, waits for them, and re-layouts  3.87 us (8%)
    ppermute x7, starting transfers between devices, swap_side(): return lax.ppermute(x, 'ctx', side)  22.3 us
    ppermute x7, waiting for transfers between devices, swap_side(): return lax.ppermute(x, 'ctx', side)  14.3 us
    unnamed x16, local copies, waits for them, and re-layouts  3.87 us
    pallas_call x1, Pallas kernels, chain_steps(): call(functools.partial(pack_body, cap=cap), (sds((2, keys, HD)), sds((2,...  1.8 us
    ppermute x1, starting transfers between devices, swap_pools(): return lax.ppermute(x, 'grp', [(0, 1), (1, 0)])  1.68 us
    pallas_call x2, Pallas kernels, late(): call(functools.partial(late_body, cap=cap, g=g), (half, half), [SMEM] + [...  1.11 us
    pallas_call x2, Pallas kernels, early(): call(functools.partial(early_body, cap=cap, g=g), state, [SMEM] + [VMEM]...  1.11 us
    ppermute x6, starting transfers between devices, swap_middle(): return lax.ppermute(x, ('ctx', 'head'), middle)  1.02 us
  transfers between devices with their start and end apart: 14, of which 5 were waited for; matrix products, arithmetic and copies ran while one was open for 0% of the time, Pallas kernels for 5%

profile of v2, /device:TPU:0, one launch (start us, length us, event | category | flops | bytes accessed | tf_op | source)
XLA Modules:
  0.0 48.3 jit_solution(5569302530321090940)
XLA Ops:
  0.0 0.0 copy-start
  0.0 0.9 %copy-done = bf16[1,512,256]{2,1,0:T(8,128)(2,1)S(1)} copy-done((bf16[1,512,256]{2,1,0:T(8,128)(2,1)S(1)}, bf16[1,512,256]{2,1,0:T(8,128)(2,1)}, u32[]{:S(2)}) %copy-start) | copy-done | bytes 262168
  1.0 0.0 copy-start.1
  1.0 0.9 %copy-done.1 = bf16[1,512,256]{2,1,0:T(8,128)(2,1)S(1)} copy-done((bf16[1,512,256]{2,1,0:T(8,128)(2,1)S(1)}, bf16[1,512,256]{2,1,0:T(8,128)(2,1)}, u32[]{:S(2)}) %copy-start.1) | copy-done | bytes 262168
  1.9 0.0 copy-start.5
  1.9 0.7 %copy-done.5 = s32[1,1,16]{2,1,0:T(1,128)S(1)} copy-done((s32[1,1,16]{2,1,0:T(1,128)S(1)}, s32[1,1,16]{2,1,0:T(1,128)}, u32[]{:S(2)}) %copy-start.5) | copy-done | bytes 88
  2.6 0.0 copy-start.6
  2.6 0.7 %copy-done.6 = s32[1,32]{1,0:T(1,128)S(1)} copy-done((s32[1,32]{1,0:T(1,128)S(1)}, s32[1,32]{1,0:T(1,128)}, u32[]{:S(2)}) %copy-start.6) | copy-done | bytes 152
  3.2 0.0 copy-start.7
  3.2 0.7 %copy-done.7 = s32[1,32]{1,0:T(1,128)S(1)} copy-done((s32[1,32]{1,0:T(1,128)S(1)}, s32[1,32]{1,0:T(1,128)}, u32[]{:S(2)}) %copy-start.7) | copy-done | bytes 152
  3.9 0.0 copy-start.2
  3.9 0.0 copy-start.3
  3.9 0.0 copy-start.4
  3.9 1.8 %shard_map.82 = (bf16[2,512,128]{2,1,0:T(8,128)(2,1)S(1)}, bf16[2,512,128]{2,1,0:T(8,128)(2,1)S(1)}, s32[32]{0:T(128)S(1)}) custom-call(s32[1,1,16]{2,1,0:T(1,128)S(1)} %copy-done.5, s32[1,32]{1,0:T(1,128)S(1)} %copy-done.6, s32[1,32]{1,0:T(1,128)S(1)} %copy-done.7, bf16[1,512,256]{2,1,0:T(8,128)(2,1)S(1)} %copy-done, bf16[1,512,256]{2,1,0:T(8,128)(2,1)S(1)} %copy-done.1), custom_call_target="tpu_custom_call" | custom-call | bytes 2097152 | tf_op jit(solution)/shard_map/pallas_call | solution.py:275
  5.7 3.1 %collective-permute-start.9 = (bf16[2,512,128]{2,1,0:T(8,128)(2,1)S(1)}, bf16[2,512,128]{2,1,0:T(8,128)(2,1)S(1)}, u32[]{:S(2)}, u32[]{:S(2)}) collective-permute-start(bf16[2,512,128]{2,1,0:T(8,128)(2,1)S(1)} %get-tuple-element.30.own), channel_id=1, source_target_pairs={{0,8},{8,0},{16,24},{24,16},{1,9},{9,1},{17,25},{25,17},{2,10},{10... | collective-permute-start | bytes 786440 | tf_op jit(solution)/shard_map/ppermute | solution.py:258
  8.8 0.0 copy-done.2
  8.8 0.0 copy-done.3
  8.8 0.0 copy-done.4
  8.8 0.2 shard_map.83
  9.0 0.1 collective-permute-start.3
  9.1 2.0 %collective-permute-start.1 = (bf16[2,512,128]{2,1,0:T(8,128)(2,1)S(1)}, bf16[2,512,128]{2,1,0:T(8,128)(2,1)S(1)}, u32[]{:S(2)}, u32[]{:S(2)}) collective-permute-start(bf16[2,512,128]{2,1,0:T(8,128)(2,1)S(1)} %get-tuple-element.23.own), channel_id=1, source_target_pairs={{0,8},{8,0},{16,24},{24,16},{1,9},{9,1},{17,25},{25,17},{2,10},{10... | collective-permute-start | bytes 786440 | tf_op jit(solution)/shard_map/ppermute | solution.py:258
  11.1 0.0 collective-permute-start.11
  11.1 0.5 %collective-permute-start.4 = (bf16[2,64,256]{2,1,0:T(8,128)(2,1)S(1)}, bf16[2,64,256]{2,1,0:T(8,128)(2,1)S(1)}, u32[]{:S(2)}, u32[]{:S(2)}) collective-permute-start(bf16[2,64,256]{2,1,0:T(8,128)(2,1)S(1)} %get-tuple-element.24.n_own), channel_id=1, source_target_pairs={{0,2},{8,16},{16,8},{24,26},{2,0},{10,18},{18,10},{26,24},{4,6},{1... | collective-permute-start | bytes 196616 | tf_op jit(solution)/shard_map/ppermute | solution.py:261
  11.6 5.8 %collective-permute-done.3.n_near = bf16[2,64,256]{2,1,0:T(8,128)(2,1)S(1)} collective-permute-done((bf16[2,64,256]{2,1,0:T(8,128)(2,1)S(1)}, bf16[2,64,256]{2,1,0:T(8,128)(2,1)S(1)}, u32[]{:S(2)}, u32[]{:S(2)}) %collective-permute-start.3) | collective-permute-done | bytes 65568 | tf_op jit(solution)/shard_map/ppermute | solution.py:258
  17.4 0.0 collective-permute-start.5
  17.4 0.0 collective-permute-done.4.n_far
  17.4 4.4 %collective-permute-start.8 = (bf16[64,1024]{1,0:T(8,128)(2,1)S(1)}, bf16[64,1024]{1,0:T(8,128)(2,1)S(1)}, u32[]{:S(2)}, u32[]{:S(2)}) collective-permute-start(bf16[64,1024]{1,0:T(8,128)(2,1)S(1)} %get-tuple-element.29.q_own), channel_id=1, source_target_pairs={{0,8},{8,0},{16,24},{24,16},{1,9},{9,1},{17,25},{25,17},{2,10},{10... | collective-permute-start | bytes 393224 | tf_op jit(solution)/shard_map/ppermute | solution.py:258
  21.8 0.0 collective-permute-done.5.n_last
  21.8 0.0 collective-permute-start.7
  21.8 3.1 %collective-permute-done.8.q_end = bf16[64,1024]{1,0:T(8,128)(2,1)S(1)} collective-permute-done((bf16[64,1024]{1,0:T(8,128)(2,1)S(1)}, bf16[64,1024]{1,0:T(8,128)(2,1)S(1)}, u32[]{:S(2)}, u32[]{:S(2)}) %collective-permute-start.8) | collective-permute-done | bytes 131104 | tf_op jit(solution)/shard_map/ppermute | solution.py:258
  24.9 1.7 %collective-permute-start.6 = (bf16[4,2,64,256]{3,2,1,0:T(8,128)(2,1)S(1)}, bf16[4,2,64,256]{3,2,1,0:T(8,128)(2,1)S(1)}, u32[]{:S(2)}, u32[]{:S(2)}) collective-permute-start(bf16[4,2,64,256]{3,2,1,0:T(8,128)(2,1)S(1)} %pad_maximum_fusion), channel_id=1, source_target_pairs={{0,1},{1,0},{2,3},{3,2},{4,5},{5,4},{6,7},{7,6},{8,9},{9,8},{10,11... | collective-permute-start | bytes 786440 | tf_op jit(solution)/shard_map/ppermute | solution.py:264
  26.6 0.0 collective-permute-done.9.near
  26.6 0.0 collective-permute-start.10
  26.6 0.0 collective-permute-done.1.near
  26.6 0.5 %collective-permute-start.2 = (bf16[2,512,128]{2,1,0:T(8,128)(2,1)S(1)}, bf16[2,512,128]{2,1,0:T(8,128)(2,1)S(1)}, u32[]{:S(2)}, u32[]{:S(2)}) collective-permute-start(bf16[2,512,128]{2,1,0:T(8,128)(2,1)S(1)} %collective-permute-done.1.near), channel_id=1, source_target_pairs={{0,2},{8,16},{16,8},{24,26},{2,0},{10,18},{18,10},{26,24},{4,6},{1... | collective-permute-start | bytes 786440 | tf_op jit(solution)/shard_map/ppermute | solution.py:261
  27.1 0.0 collective-permute-done.11.far
  27.1 3.2 %collective-permute-start = (bf16[64,1024]{1,0:T(8,128)(2,1)S(1)}, bf16[64,1024]{1,0:T(8,128)(2,1)S(1)}, u32[]{:S(2)}, u32[]{:S(2)}) collective-permute-start(bf16[64,1024]{1,0:T(8,128)(2,1)S(1)} %get-tuple-element.22.q_own), channel_id=1, source_target_pairs={{0,8},{8,0},{16,24},{24,16},{1,9},{9,1},{17,25},{25,17},{2,10},{10... | collective-permute-start | bytes 393224 | tf_op jit(solution)/shard_map/ppermute | solution.py:258
  30.3 0.6 %shard_map.86 = (f32[2,512,128]{2,1,0:T(8,128)S(1)}, f32[2,512,128]{2,1,0:T(8,128)S(1)}, f32[2,512,128]{2,1,0:T(8,128)S(1)}) custom-call(s32[32]{0:T(128)S(1)} %get-tuple-element.21.limits, bf16[64,1024]{1,0:T(8,128)(2,1)S(1)} %get-tuple-element.29.q_own, bf16[64,1024]{1,0:T(8,128)(2,1)S(1)} %collective-permute-done.8.q_end, ...), custom_call_target="tpu_custom_call" | custom-call | flops 939524096 | bytes 4194304 | tf_op jit(solution)/shard_map/pallas_call | solution.py:309
  30.9 2.4 %collective-permute-done.q_end = bf16[64,1024]{1,0:T(8,128)(2,1)S(1)} collective-permute-done((bf16[64,1024]{1,0:T(8,128)(2,1)S(1)}, bf16[64,1024]{1,0:T(8,128)(2,1)S(1)}, u32[]{:S(2)}, u32[]{:S(2)}) %collective-permute-start) | collective-permute-done | bytes 131104 | tf_op jit(solution)/shard_map/ppermute | solution.py:258
  33.3 0.0 collective-permute-done.7.far
  33.3 0.6 %shard_map.84 = (f32[2,512,128]{2,1,0:T(8,128)S(1)}, f32[2,512,128]{2,1,0:T(8,128)S(1)}, f32[2,512,128]{2,1,0:T(8,128)S(1)}) custom-call(s32[32]{0:T(128)S(1)} %get-tuple-element.21.limits, bf16[64,1024]{1,0:T(8,128)(2,1)S(1)} %get-tuple-element.22.q_own, bf16[64,1024]{1,0:T(8,128)(2,1)S(1)} %collective-permute-done.q_end, ...), custom_call_target="tpu_custom_call" | custom-call | flops 939524096 | bytes 4194304 | tf_op jit(solution)/shard_map/pallas_call | solution.py:309
  33.8 0.0 collective-permute-done.6.taken
  33.8 0.0 collective-permute-done.10.pack
  33.9 0.6 %shard_map.87 = (bf16[64,1024]{1,0:T(8,128)(2,1)S(1)}, bf16[64,1024]{1,0:T(8,128)(2,1)S(1)}) custom-call(s32[32]{0:T(128)S(1)} %get-tuple-element.21.limits, bf16[64,1024]{1,0:T(8,128)(2,1)S(1)} %get-tuple-element.29.q_own, bf16[64,1024]{1,0:T(8,128)(2,1)S(1)} %collective-permute-done.8.q_end, bf16[2,512,128]{2,1,0:T(8,128)(2,1)S(1)} %collective-permute-done.10.pack, ...), custom_call_target="tpu_custom_call" | custom-call | flops 402653184 | bytes 3145728 | tf_op jit(solution)/shard_map/pallas_call | solution.py:319
  34.4 7.5 %collective-permute-start.13 = (bf16[64,1024]{1,0:T(8,128)(2,1)S(1)}, bf16[64,1024]{1,0:T(8,128)(2,1)S(1)}, u32[]{:S(2)}, u32[]{:S(2)}) collective-permute-start(bf16[64,1024]{1,0:T(8,128)(2,1)S(1)} %get-tuple-element.36), channel_id=1, source_target_pairs={{0,8},{8,0},{16,24},{24,16},{1,9},{9,1},{17,25},{25,17},{2,10},{10... | collective-permute-start | bytes 393224 | tf_op jit(solution)/shard_map/ppermute | solution.py:258
  41.9 0.0 collective-permute-done.2.pack
  41.9 0.6 %shard_map.85 = (bf16[64,1024]{1,0:T(8,128)(2,1)S(1)}, bf16[64,1024]{1,0:T(8,128)(2,1)S(1)}) custom-call(s32[32]{0:T(128)S(1)} %get-tuple-element.21.limits, bf16[64,1024]{1,0:T(8,128)(2,1)S(1)} %get-tuple-element.22.q_own, bf16[64,1024]{1,0:T(8,128)(2,1)S(1)} %collective-permute-done.q_end, bf16[2,512,128]{2,1,0:T(8,128)(2,1)S(1)} %collective-permute-done.2.pack, ...), custom_call_target="tpu_custom_call" | custom-call | flops 402653184 | bytes 3145728 | tf_op jit(solution)/shard_map/pallas_call | solution.py:319
  42.5 2.0 %collective-permute-start.12 = (bf16[64,1024]{1,0:T(8,128)(2,1)S(1)}, bf16[64,1024]{1,0:T(8,128)(2,1)S(1)}, u32[]{:S(2)}, u32[]{:S(2)}) collective-permute-start(bf16[64,1024]{1,0:T(8,128)(2,1)S(1)} %get-tuple-element.35), channel_id=1, source_target_pairs={{0,8},{8,0},{16,24},{24,16},{1,9},{9,1},{17,25},{25,17},{2,10},{10... | collective-permute-start | bytes 393224 | tf_op jit(solution)/shard_map/ppermute | solution.py:258
  44.5 1.4 %collective-permute-done.13.back1 = bf16[64,1024]{1,0:T(8,128)(2,1)S(1)} collective-permute-done((bf16[64,1024]{1,0:T(8,128)(2,1)S(1)}, bf16[64,1024]{1,0:T(8,128)(2,1)S(1)}, u32[]{:S(2)}, u32[]{:S(2)}) %collective-permute-start.13) | collective-permute-done | bytes 131104 | tf_op jit(solution)/shard_map/ppermute | solution.py:258
  45.9 1.6 %collective-permute-done.12.back0 = bf16[64,1024]{1,0:T(8,128)(2,1)S(1)} collective-permute-done((bf16[64,1024]{1,0:T(8,128)(2,1)S(1)}, bf16[64,1024]{1,0:T(8,128)(2,1)S(1)}, u32[]{:S(2)}, u32[]{:S(2)}) %collective-permute-start.12) | collective-permute-done | bytes 131104 | tf_op jit(solution)/shard_map/ppermute | solution.py:258
  47.5 0.7 %shard_map.88 = bf16[1,64,2048]{2,1,0:T(8,128)(2,1)} custom-call(bf16[64,1024]{1,0:T(8,128)(2,1)S(1)} %get-tuple-element.28.own0, bf16[64,1024]{1,0:T(8,128)(2,1)S(1)} %get-tuple-element.34.own1, bf16[64,1024]{1,0:T(8,128)(2,1)S(1)} %collective-permute-done.12.back0, bf16[64,1024]{1,0:T(8,128)(2,1)S(1)} %collective-permute-done.13.back1), custom_call_target="tpu_custom_call" | custom-call | bytes 1048576 | tf_op jit(solution)/shard_map/pallas_call | solution.py:334
  (1 shorter events, 0.0 us)
Async XLA Ops:
  0.0 0.9 %copy-start = (bf16[1,512,256]{2,1,0:T(8,128)(2,1)S(1)}, bf16[1,512,256]{2,1,0:T(8,128)(2,1)}, u32[]{:S(2)}) copy-start(bf16[1,512,256]{2,1,0:T(8,128)(2,1)} %pk.1) | copy-start | bytes 786436
  1.0 0.9 %copy-start.1 = (bf16[1,512,256]{2,1,0:T(8,128)(2,1)S(1)}, bf16[1,512,256]{2,1,0:T(8,128)(2,1)}, u32[]{:S(2)}) copy-start(bf16[1,512,256]{2,1,0:T(8,128)(2,1)} %pv.1) | copy-start | bytes 786436
  1.9 0.7 %copy-start.5 = (s32[1,1,16]{2,1,0:T(1,128)S(1)}, s32[1,1,16]{2,1,0:T(1,128)}, u32[]{:S(2)}) copy-start(s32[1,1,16]{2,1,0:T(1,128)} %table_in.1) | copy-start | bytes 196
  2.6 0.7 %copy-start.6 = (s32[1,32]{1,0:T(1,128)S(1)}, s32[1,32]{1,0:T(1,128)}, u32[]{:S(2)}) copy-start(s32[1,32]{1,0:T(1,128)} %slot_in.1) | copy-start | bytes 388
  3.2 0.7 %copy-start.7 = (s32[1,32]{1,0:T(1,128)S(1)}, s32[1,32]{1,0:T(1,128)}, u32[]{:S(2)}) copy-start(s32[1,32]{1,0:T(1,128)} %length_in.1) | copy-start | bytes 388
  3.9 4.9 %copy-start.2 = (bf16[1,64,2048]{2,1,0:T(8,128)(2,1)S(1)}, bf16[1,64,2048]{2,1,0:T(8,128)(2,1)}, u32[]{:S(2)}) copy-start(bf16[1,64,2048]{2,1,0:T(8,128)(2,1)} %q.1) | copy-start | bytes 786436
  3.9 4.9 %copy-start.3 = (bf16[1,64,256]{2,1,0:T(8,128)(2,1)S(1)}, bf16[1,64,256]{2,1,0:T(8,128)(2,1)}, u32[]{:S(2)}) copy-start(bf16[1,64,256]{2,1,0:T(8,128)(2,1)} %nk.1) | copy-start | bytes 98308
  3.9 4.9 %copy-start.4 = (bf16[1,64,256]{2,1,0:T(8,128)(2,1)S(1)}, bf16[1,64,256]{2,1,0:T(8,128)(2,1)}, u32[]{:S(2)}) copy-start(bf16[1,64,256]{2,1,0:T(8,128)(2,1)} %nv.1) | copy-start | bytes 98308
  5.7 20.9 %collective-permute-start.9 = (bf16[2,512,128]{2,1,0:T(8,128)(2,1)S(1)}, bf16[2,512,128]{2,1,0:T(8,128)(2,1)S(1)}, u32[]{:S(2)}, u32[]{:S(2)}) collective-permute-start(bf16[2,512,128]{2,1,0:T(8,128)(2,1)S(1)} %get-tuple-element.30.own), channel_id=1, source_target_pairs={{0,8},{8,0},{16,24},{24,16},{1,9},{9,1},{17,25},{25,17},{2,10},{10... | collective-permute-start | bytes 786440 | tf_op jit(solution)/shard_map/ppermute | solution.py:258
  9.0 8.4 %collective-permute-start.3 = (bf16[2,64,256]{2,1,0:T(8,128)(2,1)S(1)}, bf16[2,64,256]{2,1,0:T(8,128)(2,1)S(1)}, u32[]{:S(2)}, u32[]{:S(2)}) collective-permute-start(bf16[2,64,256]{2,1,0:T(8,128)(2,1)S(1)} %get-tuple-element.24.n_own), channel_id=1, source_target_pairs={{0,8},{8,0},{16,24},{24,16},{1,9},{9,1},{17,25},{25,17},{2,10},{10... | collective-permute-start | bytes 196616 | tf_op jit(solution)/shard_map/ppermute | solution.py:258
  9.1 17.5 %collective-permute-start.1 = (bf16[2,512,128]{2,1,0:T(8,128)(2,1)S(1)}, bf16[2,512,128]{2,1,0:T(8,128)(2,1)S(1)}, u32[]{:S(2)}, u32[]{:S(2)}) collective-permute-start(bf16[2,512,128]{2,1,0:T(8,128)(2,1)S(1)} %get-tuple-element.23.own), channel_id=1, source_target_pairs={{0,8},{8,0},{16,24},{24,16},{1,9},{9,1},{17,25},{25,17},{2,10},{10... | collective-permute-start | bytes 786440 | tf_op jit(solution)/shard_map/ppermute | solution.py:258
  11.1 16.1 %collective-permute-start.11 = (bf16[2,512,128]{2,1,0:T(8,128)(2,1)S(1)}, bf16[2,512,128]{2,1,0:T(8,128)(2,1)S(1)}, u32[]{:S(2)}, u32[]{:S(2)}) collective-permute-start(bf16[2,512,128]{2,1,0:T(8,128)(2,1)S(1)} %get-tuple-element.30.own), channel_id=1, source_target_pairs={{0,2},{8,16},{16,8},{24,26},{2,0},{10,18},{18,10},{26,24},{4,6},{1... | collective-permute-start | bytes 786440 | tf_op jit(solution)/shard_map/ppermute | solution.py:261
  11.1 6.3 %collective-permute-start.4 = (bf16[2,64,256]{2,1,0:T(8,128)(2,1)S(1)}, bf16[2,64,256]{2,1,0:T(8,128)(2,1)S(1)}, u32[]{:S(2)}, u32[]{:S(2)}) collective-permute-start(bf16[2,64,256]{2,1,0:T(8,128)(2,1)S(1)} %get-tuple-element.24.n_own), channel_id=1, source_target_pairs={{0,2},{8,16},{16,8},{24,26},{2,0},{10,18},{18,10},{26,24},{4,6},{1... | collective-permute-start | bytes 196616 | tf_op jit(solution)/shard_map/ppermute | solution.py:261
  17.4 4.4 %collective-permute-start.5 = (bf16[2,64,256]{2,1,0:T(8,128)(2,1)S(1)}, bf16[2,64,256]{2,1,0:T(8,128)(2,1)S(1)}, u32[]{:S(2)}, u32[]{:S(2)}) collective-permute-start(bf16[2,64,256]{2,1,0:T(8,128)(2,1)S(1)} %collective-permute-done.3.n_near), channel_id=1, source_target_pairs={{0,2},{8,16},{16,8},{24,26},{2,0},{10,18},{18,10},{26,24},{4,6},{1... | collective-permute-start | bytes 196616 | tf_op jit(solution)/shard_map/ppermute | solution.py:261
  17.4 7.6 %collective-permute-start.8 = (bf16[64,1024]{1,0:T(8,128)(2,1)S(1)}, bf16[64,1024]{1,0:T(8,128)(2,1)S(1)}, u32[]{:S(2)}, u32[]{:S(2)}) collective-permute-start(bf16[64,1024]{1,0:T(8,128)(2,1)S(1)} %get-tuple-element.29.q_own), channel_id=1, source_target_pairs={{0,8},{8,0},{16,24},{24,16},{1,9},{9,1},{17,25},{25,17},{2,10},{10... | collective-permute-start | bytes 393224 | tf_op jit(solution)/shard_map/ppermute | solution.py:258
  21.8 11.5 %collective-permute-start.7 = (bf16[2,512,128]{2,1,0:T(8,128)(2,1)S(1)}, bf16[2,512,128]{2,1,0:T(8,128)(2,1)S(1)}, u32[]{:S(2)}, u32[]{:S(2)}) collective-permute-start(bf16[2,512,128]{2,1,0:T(8,128)(2,1)S(1)} %get-tuple-element.23.own), channel_id=1, source_target_pairs={{0,2},{8,16},{16,8},{24,26},{2,0},{10,18},{18,10},{26,24},{4,6},{1... | collective-permute-start | bytes 786440 | tf_op jit(solution)/shard_map/ppermute | solution.py:261
  24.9 8.9 %collective-permute-start.6 = (bf16[4,2,64,256]{3,2,1,0:T(8,128)(2,1)S(1)}, bf16[4,2,64,256]{3,2,1,0:T(8,128)(2,1)S(1)}, u32[]{:S(2)}, u32[]{:S(2)}) collective-permute-start(bf16[4,2,64,256]{3,2,1,0:T(8,128)(2,1)S(1)} %pad_maximum_fusion), channel_id=1, source_target_pairs={{0,1},{1,0},{2,3},{3,2},{4,5},{5,4},{6,7},{7,6},{8,9},{9,8},{10,11... | collective-permute-start | bytes 786440 | tf_op jit(solution)/shard_map/ppermute | solution.py:264
  26.6 7.2 %collective-permute-start.10 = (bf16[2,512,128]{2,1,0:T(8,128)(2,1)S(1)}, bf16[2,512,128]{2,1,0:T(8,128)(2,1)S(1)}, u32[]{:S(2)}, u32[]{:S(2)}) collective-permute-start(bf16[2,512,128]{2,1,0:T(8,128)(2,1)S(1)} %collective-permute-done.9.near), channel_id=1, source_target_pairs={{0,2},{8,16},{16,8},{24,26},{2,0},{10,18},{18,10},{26,24},{4,6},{1... | collective-permute-start | bytes 786440 | tf_op jit(solution)/shard_map/ppermute | solution.py:261
  26.6 15.3 %collective-permute-start.2 = (bf16[2,512,128]{2,1,0:T(8,128)(2,1)S(1)}, bf16[2,512,128]{2,1,0:T(8,128)(2,1)S(1)}, u32[]{:S(2)}, u32[]{:S(2)}) collective-permute-start(bf16[2,512,128]{2,1,0:T(8,128)(2,1)S(1)} %collective-permute-done.1.near), channel_id=1, source_target_pairs={{0,2},{8,16},{16,8},{24,26},{2,0},{10,18},{18,10},{26,24},{4,6},{1... | collective-permute-start | bytes 786440 | tf_op jit(solution)/shard_map/ppermute | solution.py:261
  27.1 6.1 %collective-permute-start = (bf16[64,1024]{1,0:T(8,128)(2,1)S(1)}, bf16[64,1024]{1,0:T(8,128)(2,1)S(1)}, u32[]{:S(2)}, u32[]{:S(2)}) collective-permute-start(bf16[64,1024]{1,0:T(8,128)(2,1)S(1)} %get-tuple-element.22.q_own), channel_id=1, source_target_pairs={{0,8},{8,0},{16,24},{24,16},{1,9},{9,1},{17,25},{25,17},{2,10},{10... | collective-permute-start | bytes 393224 | tf_op jit(solution)/shard_map/ppermute | solution.py:258
  34.4 11.5 %collective-permute-start.13 = (bf16[64,1024]{1,0:T(8,128)(2,1)S(1)}, bf16[64,1024]{1,0:T(8,128)(2,1)S(1)}, u32[]{:S(2)}, u32[]{:S(2)}) collective-permute-start(bf16[64,1024]{1,0:T(8,128)(2,1)S(1)} %get-tuple-element.36), channel_id=1, source_target_pairs={{0,8},{8,0},{16,24},{24,16},{1,9},{9,1},{17,25},{25,17},{2,10},{10... | collective-permute-start | bytes 393224 | tf_op jit(solution)/shard_map/ppermute | solution.py:258
  42.5 5.0 %collective-permute-start.12 = (bf16[64,1024]{1,0:T(8,128)(2,1)S(1)}, bf16[64,1024]{1,0:T(8,128)(2,1)S(1)}, u32[]{:S(2)}, u32[]{:S(2)}) collective-permute-start(bf16[64,1024]{1,0:T(8,128)(2,1)S(1)} %get-tuple-element.35), channel_id=1, source_target_pairs={{0,8},{8,0},{16,24},{24,16},{1,9},{9,1},{17,25},{25,17},{2,10},{10... | collective-permute-start | bytes 393224 | tf_op jit(solution)/shard_map/ppermute | solution.py:258

commit v3 on v2

--- a/solution.py
+++ b/solution.py
@@ -12,7 +12,8 @@
 HD = 128
 SPAN = 4
 PAGE = 64
-CAP = 8
+CAP = 6
+
 
 neg_floor = -1e30
 far_limit = 1 << 30
@@ -39,31 +40,13 @@
     return jax.ShapeDtypeStruct(shape, dtype)
 
 
-def ready_body(nk, nv, q, fresh, q0, q1, sem):
-    half = q0.shape[1]
-    copies = [
-        pltpu.make_async_copy(nk.at[0], fresh.at[0], sem.at[0]),
-        pltpu.make_async_copy(nv.at[0], fresh.at[1], sem.at[1]),
-        pltpu.make_async_copy(q.at[0, :, pl.ds(0, half)], q0, sem.at[2]),
-        pltpu.make_async_copy(q.at[0, :, pl.ds(half, half)], q1, sem.at[3]),
-    ]
-    for copy in copies:
-        copy.start()
-    for copy in copies:
-        copy.wait()
-
-
-def pack_body(
-    table_in, slot_in, length_in, pk, pv, pack0, pack1, limits, table, slot, length, source, count,
-    sem, *, cap
-):
-    position = lax.axis_index("ctx")
+def listed_pages(tables, places, limits, source, count, most, sem):
+    table, slot, length = places
     holders = lax.axis_size("ctx")
     held = slot.shape[1] // holders
     reads = [
-        pltpu.make_async_copy(table_in, table, sem.at[0]),
-        pltpu.make_async_copy(slot_in, slot, sem.at[1]),
-        pltpu.make_async_copy(length_in, length, sem.at[2]),
+        pltpu.make_async_copy(wide, near, sem.at[i])
+        for i, (wide, near) in enumerate(zip(tables, places))
     ]
     for copy in reads:
         copy.start()
@@ -82,21 +65,68 @@
         count[holder] = nth + 1
         limits[holder * held + nth] = length[0, number]
         source[holder * held + nth] = place - holder * held
-
+    most[0] = functools.reduce(jnp.maximum, [count[i] for i in range(holders)])
+
+
+def page_copies(packs, pages, source, first, cap, sem):
+    position = lax.axis_index("ctx")
+    held = source.shape[0] // lax.axis_size("ctx")
     copies = []
-    for g, pack in enumerate((pack0, pack1)):
+    for g, pack in enumerate(packs):
         for j in range(cap):
-            first = pl.multiple_of(source[position * held + j] * PAGE, PAGE)
-            for w, pages in enumerate((pk, pv)):
+            row = pl.multiple_of(source[position * held + first + j] * PAGE, PAGE)
+            for w, wide in enumerate(pages):
                 copy = pltpu.make_async_copy(
-                    pages.at[0, pl.ds(first, PAGE), pl.ds(g * HD, HD)],
+                    wide.at[0, pl.ds(row, PAGE), pl.ds(g * HD, HD)],
                     pack.at[w, pl.ds(j * PAGE, PAGE), :],
                     sem.at[(j * 2 + g) * 2 + w],
                 )
                 copy.start()
                 copies.append(copy)
+    return copies
+
+
+def pack_body(
+    table_in, slot_in, length_in, pk, pv, nk, nv, q, pack0, pack1, q0, q1, limits, most,
+    table, slot, length, source, count, sem, sem_new, *, cap
+):
+    half = q0.shape[1]
+    rows_dev = nk.shape[1]
+    copies = []
+    for i, (wide, near) in enumerate(((0, q0), (half, q1))):
+        copies.append(pltpu.make_async_copy(q.at[0, :, pl.ds(wide, half)], near, sem_new.at[i]))
+    for w, new in enumerate((nk, nv)):
+        for g in range(2):
+            copies.append(
+                pltpu.make_async_copy(
+                    new.at[0, :, pl.ds(g * HD, HD)],
+                    pack0.at[w, pl.ds(cap * PAGE + g * rows_dev, rows_dev), :],
+                    sem_new.at[2 + w * 2 + g],
+                )
+            )
+    for copy in copies:
+        copy.start()
+    listed_pages(
+        (table_in, slot_in, length_in), (table, slot, length), limits, source, count, most, sem
+    )
+    copies += page_copies((pack0, pack1), (pk, pv), source, 0, cap, sem)
     for copy in copies:
         copy.wait()
+
+
+def spare_body(
+    table_in, slot_in, length_in, pk, pv, rest, table, slot, length, source, count, limits, most,
+    sem, *, first, cap
+):
+    listed_pages(
+        (table_in, slot_in, length_in), (table, slot, length), limits, source, count, most, sem
+    )
+    for copy in page_copies((rest.at[0], rest.at[1]), (pk, pv), source, first, cap, sem):
+        copy.wait()
+
+
+def blank_body(*refs):
+    pass
 
 
 def holder_ids(position):
@@ -119,21 +149,26 @@
     )
 
 
-def page_bias(limits, holder, held, cap):
+def page_bias(limits, holder, held, first, cap):
     column = lax.broadcasted_iota(jnp.int32, (1, cap * PAGE), 1)
     page = column // PAGE
     within = column - page * PAGE
     limit = jnp.zeros((1, cap * PAGE), jnp.int32)
     for j in range(cap):
-        limit = jnp.where(page == j, limits[holder * held + j], limit)
+        limit = jnp.where(page == j, limits[holder * held + first + j], limit)
     return jnp.where(within < limit, 0.0, neg_floor).astype(jnp.float32)
 
 
-def causal_bias(position, holder, rows, rows_dev):
-    row = lax.broadcasted_iota(jnp.int32, (rows, rows_dev), 0) % rows_dev
-    column = lax.broadcasted_iota(jnp.int32, (rows, rows_dev), 1)
-    allowed = position * rows_dev + row >= holder * rows_dev + column
-    return jnp.where(allowed, 0.0, neg_floor).astype(jnp.float32)
+def causal_bias(position, ids, rows, rows_dev):
+    shape = (rows_dev, len(ids) * rows_dev)
+    row = lax.broadcasted_iota(jnp.int32, shape, 0)
+    column = lax.broadcasted_iota(jnp.int32, (1, shape[1]), 1)
+    key = jnp.zeros_like(column)
+    for i, holder in enumerate(ids):
+        key = jnp.where(column // rows_dev == i, column + (holder - i) * rows_dev, key)
+    allowed = position * rows_dev + row >= key
+    bias = jnp.where(allowed, 0.0, neg_floor).astype(jnp.float32)
+    return jnp.concatenate([bias] * (rows // rows_dev), axis=0)
 
 
 def scored(q, k, bias):
@@ -162,56 +197,84 @@
     return total, acc + old_acc * rescale
 
 
-def early_body(
-    limits, q_own, q_end, own, near, far, n_own, n_near, n_far, n_last, tops, totals, accs, *, cap, g
-):
+def early_body(limits, q_own, q_end, *refs, cap, g):
+    packs = refs[:3]
+    news = refs[3:7] if len(refs) == 10 else packs + refs[3:4]
+    tops, totals, accs = refs[-3:]
     position = lax.axis_index("ctx")
     held = limits.shape[0] // lax.axis_size("ctx")
-    rows_dev = n_own.shape[1]
+    rows_dev = q_own.shape[0]
     rows = accs.shape[1]
+    pages = cap * PAGE
 
     @pl.when(is_inner(position))
     def _():
         ids = holder_ids(position)
-        cols = slice(g * HD, (g + 1) * HD)
-        news = (n_own, n_near, n_far, n_last)
-        nk = jnp.concatenate([n[0, :, cols] for n in news], axis=0)
-        nv = jnp.concatenate([n[1, :, cols] for n in news], axis=0)
+        firsts = [n.shape[1] - 2 * rows_dev + g * rows_dev for n in news]
+        nk = jnp.concatenate([n[0, i : i + rows_dev] for n, i in zip(news, firsts)], axis=0)
+        nv = jnp.concatenate([n[1, i : i + rows_dev] for n, i in zip(news, firsts)], axis=0)
         paged = [
-            (p[0], p[1], page_bias(limits, i, held, cap)) for p, i in zip((own, near, far), ids)
+            (p[0, :pages], p[1, :pages], page_bias(limits, i, held, 0, cap))
+            for p, i in zip(packs, ids)
         ]
         for t, q in enumerate((q_own, q_end)):
-            causal = [causal_bias(position ^ t, i, rows, rows_dev) for i in ids]
-            fresh = (nk, nv, jnp.concatenate(causal, axis=1))
+            fresh = (nk, nv, causal_bias(position ^ t, ids, rows, rows_dev))
             top, total, acc = attend(heads_of(q), paged + [fresh])
             tops[t] = jnp.broadcast_to(top, acc.shape)
             totals[t] = jnp.broadcast_to(total, acc.shape)
             accs[t] = acc
 
 
-def late_body(
-    limits, q_own, q_end, pack, taken, tops, totals, accs, out_own, out_end, *, cap, g
-):
+def late_body(*refs, cap, g, tasks):
+    n = len(tasks)
+    limits, most = refs[:2]
+    queries = refs[2 : 2 + n]
+    pack, taken, tops, totals, accs = refs[2 + n : 7 + n]
+    spilled = refs[7 + n : 11 + n]
+    outs = refs[11 + n : 11 + 2 * n]
+    extra, sem = refs[11 + 2 * n :]
     position = lax.axis_index("ctx")
     held = limits.shape[0] // lax.axis_size("ctx")
-    rows_dev = q_own.shape[0]
-
-    @pl.when(is_inner(position))
-    def _():
+
+    def finish(more):
         ids = holder_ids(position)
-        cols = slice(g * HD, (g + 1) * HD)
+        rows_dev = queries[0].shape[0]
+        new = slice(g * rows_dev, (g + 1) * rows_dev)
         shut = jnp.where(lax.axis_index("grp") == 1, 0.0, neg_floor).astype(jnp.float32)
-        tk = jnp.concatenate([taken[i, 0, :, cols] for i in range(taken.shape[0])], axis=0)
-        tv = jnp.concatenate([taken[i, 1, :, cols] for i in range(taken.shape[0])], axis=0)
+        tk = jnp.concatenate([taken[i, 0, new] for i in range(taken.shape[0])], axis=0)
+        tv = jnp.concatenate([taken[i, 1, new] for i in range(taken.shape[0])], axis=0)
         blocks = [
-            (pack[0], pack[1], page_bias(limits, ids[3], held, cap)),
+            (pack[0], pack[1], page_bias(limits, ids[3], held, 0, cap)),
             (tk, tv, jnp.full((1, tk.shape[0]), shut, jnp.float32)),
         ]
-        for t, q, out in ((1, q_end, out_end), (0, q_own, out_own)):
+        if more:
+            copies = [
+                pltpu.make_async_copy(ref.at[g], extra.at[i], sem.at[i])
+                for i, ref in enumerate(spilled)
+            ]
+            for copy in copies:
+                copy.start()
+            for copy in copies:
+                copy.wait()
+            for i, holder in enumerate(ids):
+                bias = page_bias(limits, holder, held, cap, held - cap)
+                blocks.append((extra[i, 0], extra[i, 1], bias))
+        for t, q, out in zip(tasks, queries, outs):
             total, num = attend(heads_of(q), blocks, (tops[t], totals[t], accs[t]))
             result = (num / total).astype(jnp.bfloat16)
             for i in range(out.shape[1] // HD):
                 out[:, i * HD : (i + 1) * HD] = result[i * rows_dev : (i + 1) * rows_dev]
+
+    inner = is_inner(position)
+    over = most[0] > cap
+
+    @pl.when(inner & jnp.logical_not(over))
+    def _():
+        finish(False)
+
+    @pl.when(inner & over)
+    def _():
+        finish(True)
 
 
 def join_body(own0, own1, back0, back1, out):
@@ -263,74 +326,106 @@
     def swap_pools(x):
         return lax.ppermute(x, "grp", [(0, 1), (1, 0)])
 
+    new_keys, new_values, queries, page_table, page_slot, page_length, page_keys, page_values = [
+        pltpu.with_memory_space_constraint(x, pltpu.HBM)
+        for x in (
+            new_keys, new_values, queries, page_table, page_slot, page_length, page_keys,
+            page_values,
+        )
+    ]
     half = sds((rows_dev, group * HD))
-    fresh, q0, q1 = call(
-        ready_body,
-        (sds((2, rows_dev, width)), half, half),
-        [HBM] * 3,
-        (VMEM,) * 3,
-        [pltpu.SemaphoreType.DMA((4,))],
-        nbytes=1 << 20,
-    )(new_keys, new_values, queries)
-    pack0, pack1, limits = call(
+    tables = (page_table, page_slot, page_length, page_keys, page_values)
+    scalars = [
+        pltpu.SMEM(page_table.shape, jnp.int32),
+        pltpu.SMEM(page_slot.shape, jnp.int32),
+        pltpu.SMEM(page_length.shape, jnp.int32),
+        pltpu.SMEM((holders * held,), jnp.int32),
+        pltpu.SMEM((holders,), jnp.int32),
+    ]
+    pack0, pack1, q0, q1, limits, most = call(
         functools.partial(pack_body, cap=cap),
-        (sds((2, keys, HD)), sds((2, keys, HD)), sds((holders * held,), jnp.int32)),
-        [HBM] * 5,
-        (VMEM, VMEM, SMEM),
-        [
-            pltpu.SMEM(page_table.shape, jnp.int32),
-            pltpu.SMEM(page_slot.shape, jnp.int32),
-            pltpu.SMEM(page_length.shape, jnp.int32),
-            pltpu.SMEM((holders * held,), jnp.int32),
-            pltpu.SMEM((holders,), jnp.int32),
-            pltpu.SemaphoreType.DMA((cap * 4,)),
-        ],
-        nbytes=2 << 20,
-    )(page_table, page_slot, page_length, page_keys, page_values)
-
-    n_near = swap_side(fresh)
-    n_far = swap_middle(fresh)
-    q0_end = swap_side(q0)
+        (
+            sds((2, keys + 2 * rows_dev, HD)),
+            sds((2, keys, HD)),
+            half,
+            half,
+            sds((holders * held,), jnp.int32),
+            sds((1,), jnp.int32),
+        ),
+        [HBM] * 8,
+        (VMEM, VMEM, VMEM, VMEM, SMEM, SMEM),
+        scalars + [pltpu.SemaphoreType.DMA((cap * 4,)), pltpu.SemaphoreType.DMA((6,))],
+        nbytes=3 << 20,
+    )(*tables, new_keys, new_values, queries)
+
     near0 = swap_side(pack0)
     far0 = swap_middle(pack0)
-    n_last = swap_middle(n_near)
+    q0_end = swap_side(q0)
+    n_last = swap_middle(near0[:, keys:])
     near1 = swap_side(pack1)
     far1 = swap_middle(pack1)
     q1_end = swap_side(q1)
-    taken = swap_pools(jnp.stack([fresh, n_near, n_far, n_last]))
-    last0 = swap_middle(near0)
+    last0 = swap_middle(near0[:, :keys])
+    fresh = [pack0[:, keys:], near0[:, keys:], far0[:, keys:], n_last]
+    taken = swap_pools(jnp.stack(fresh))
     last1 = swap_middle(near1)
+    spare = sds((2, 2, (held - cap) * PAGE, HD))
+
+    def fetch():
+        rest = call(
+            functools.partial(spare_body, first=cap, cap=held - cap),
+            spare,
+            [HBM] * 5,
+            VMEM,
+            scalars
+            + [
+                pltpu.SMEM((holders * held,), jnp.int32),
+                pltpu.SMEM((1,), jnp.int32),
+                pltpu.SemaphoreType.DMA((max(held - cap, 1) * 4,)),
+            ],
+            nbytes=1 << 20,
+        )(*tables)
+        near = swap_side(rest)
+        far = swap_middle(rest)
+        return rest, near, far, swap_middle(near)
+
+    def skip():
+        return tuple(call(blank_body, (spare,) * 4, [], (HBM,) * 4)())
+
+    spilled = lax.cond(most[0] > cap, fetch, skip)
 
     rows = group * rows_dev
     pair_flops = 4 * rows * HD
     state = (sds((2, rows, HD), jnp.float32),) * 3
 
-    def early(g, q, q_end, own, near, far):
+    def early(g, q, q_end, packs, news):
         return call(
             functools.partial(early_body, cap=cap, g=g),
             state,
-            [SMEM] + [VMEM] * 9,
+            [SMEM] + [VMEM] * (5 + len(news)),
             (VMEM,) * 3,
             flops=2 * pair_flops * (3 * keys + 4 * rows_dev),
             nbytes=4 << 20,
-        )(limits, q, q_end, own, near, far, fresh, n_near, n_far, n_last)
-
-    def late(g, q, q_end, pack, carried):
+        )(limits, q, q_end, *packs, *news)
+
+    def late(g, tasks, queries, pack, carried):
         return call(
-            functools.partial(late_body, cap=cap, g=g),
-            (half, half),
-            [SMEM] + [VMEM] * 7,
-            (VMEM, VMEM),
-            flops=2 * pair_flops * (keys + 4 * rows_dev),
-            nbytes=3 << 20,
-        )(limits, q, q_end, pack, taken, *carried)
-
-    carried0 = early(0, q0, q0_end, pack0, near0, far0)
-    carried1 = early(1, q1, q1_end, pack1, near1, far1)
-    own0, end0 = late(0, q0, q0_end, last0, carried0)
+            functools.partial(late_body, cap=cap, g=g, tasks=tasks),
+            (half,) * len(tasks),
+            [SMEM, SMEM] + [VMEM] * (5 + len(tasks)) + [HBM] * 4,
+            (VMEM,) * len(tasks),
+            [pltpu.VMEM((4, 2, (held - cap) * PAGE, HD), jnp.bfloat16), pltpu.SemaphoreType.DMA((4,))],
+            flops=len(tasks) * pair_flops * (keys + 4 * rows_dev),
+            nbytes=len(tasks) << 20,
+        )(limits, most, *queries, pack, taken, *carried, *spilled)
+
+    carried0 = early(0, q0, q0_end, (pack0, near0, far0), (n_last,))
+    carried1 = early(1, q1, q1_end, (pack1, near1, far1), (pack0, near0, far0, n_last))
+    end0, own0 = late(0, (1, 0), (q0_end, q0), last0, carried0)
     back0 = swap_side(end0)
-    own1, end1 = late(1, q1, q1_end, last1, carried1)
+    (end1,) = late(1, (1,), (q1_end,), last1, carried1)
     back1 = swap_side(end1)
+    (own1,) = late(1, (0,), (q1,), last1, carried1)
     return call(join_body, sds(queries.shape), [VMEM] * 4, VMEM, nbytes=1 << 20)(
         own0, own1, back0, back1
     )

time: 48.5 us -> 40.2 us (0.83)
  waiting for transfers between devices: 14.3 us -> 7.89 us
  local copies, waits for them, and re-layouts: 3.87 us -> 0.04 us
  Pallas kernels: 4.91 us -> 8.19 us
  starting transfers between devices: 25 us -> 23.1 us
  between operations: 0.09 us -> 0.7 us
    ppermute x7 -> x6, waiting for transfers between devices: 14.3 us -> 6.66 us  [swap_side(): return lax.ppermute(x, 'ctx', side)]
    unnamed x16 -> x0, local copies, waits for them, and re-layouts: 3.87 us -> none
    pallas_call x4 -> x5, Pallas kernels: 3.08 us -> 6.36 us  [the longest x3 3.61 us: late(): call(functools.partial(late_body, cap=cap, g=g, tasks=tasks), (half,) * l...]
    ppermute x7 -> x6, starting transfers between devices: 22.3 us -> 20.3 us  [swap_side(): return lax.ppermute(x, 'ctx', side)]
    ppermute x6 -> x5, waiting for transfers between devices: 0.02 us -> 1.23 us  [swap_middle(): return lax.ppermute(x, ('ctx', 'head'), middle)]
    ppermute x6 -> x5, starting transfers between devices: 1.02 us -> 0.72 us  [swap_middle(): return lax.ppermute(x, ('ctx', 'head'), middle)]
  transfers between devices with their start and end apart: 14 -> 12, of which waited for: 5 -> 4; matrix products, arithmetic and copies ran while one was open for 0% -> 0% of each run, Pallas kernels for 5% -> 12%
where the time goes in v3:
time: 40.2 us; the launch traced here: 39.9 us
  starting transfers between devices  23.1 us (57%)
  Pallas kernels  8.19 us (20%)
  waiting for transfers between devices  7.89 us (20%)
  between operations  0.7 us (2%)
    ppermute x6, starting transfers between devices, swap_side(): return lax.ppermute(x, 'ctx', side)  20.3 us
    ppermute x6, waiting for transfers between devices, swap_side(): return lax.ppermute(x, 'ctx', side)  6.66 us
    pallas_call x3, Pallas kernels, late(): call(functools.partial(late_body, cap=cap, g=g, tasks=tasks), (half,) * l...  3.61 us
    pallas_call x1, Pallas kernels, chain_steps(): call(functools.partial(pack_body, cap=cap), (sds((2, keys + 2 * rows_dev,...  2.76 us
    ppermute x1, starting transfers between devices, swap_pools(): return lax.ppermute(x, 'grp', [(0, 1), (1, 0)])  2.02 us
    ppermute x5, waiting for transfers between devices, swap_middle(): return lax.ppermute(x, ('ctx', 'head'), middle)  1.23 us
    pallas_call x2, Pallas kernels, early(): call(functools.partial(early_body, cap=cap, g=g), state, [SMEM] + [VMEM]...  1.11 us
  transfers between devices with their start and end apart: 12, of which 4 were waited for; matrix products, arithmetic and copies ran while one was open for 0% of the time, Pallas kernels for 12%

profile of v3, /device:TPU:0, one launch (start us, length us, event | category | flops | bytes accessed | tf_op | source)
XLA Modules:
  0.0 39.9 jit_solution(5036827040356709302)
XLA Ops:
  0.0 2.8 %shard_map.82 = (bf16[2,512,128]{2,1,0:T(8,128)(2,1)S(1)}, bf16[2,384,128]{2,1,0:T(8,128)(2,1)S(1)}, bf16[64,1024]{1,0:T(8,128)(2,1)S(1)}, bf16[64,1024]{1,0:T(8...) custom-call(s32[1,1,16]{2,1,0:T(1,128)} %table_in.1, s32[1,32]{1,0:T(1,128)} %slot_in.1, s32[1,32]{1,0:T(1,128)} %length_in.1, ...), custom_call_target="tpu_custom_call" | custom-call | bytes 3145728 | tf_op jit(solution)/shard_map/pallas_call | solution.py:345
  2.8 3.1 %collective-permute-start.4 = (bf16[2,512,128]{2,1,0:T(8,128)(2,1)S(1)}, bf16[2,512,128]{2,1,0:T(8,128)(2,1)S(1)}, u32[]{:S(2)}, u32[]{:S(2)}) collective-permute-start(bf16[2,512,128]{2,1,0:T(8,128)(2,1)S(1)} %get-tuple-element.41.refs_0_.refs_3_), channel_id=1, source_target_pairs={{0,8},{8,0},{16,24},{24,16},{1,9},{9,1},{17,25},{25,17},{2,10},{10... | collective-permute-start | bytes 786440 | tf_op jit(solution)/shard_map/ppermute | solution.py:321
  5.9 0.0 collective-permute-start.6
  5.9 3.1 %collective-permute-start.9 = (bf16[2,384,128]{2,1,0:T(8,128)(2,1)S(1)}, bf16[2,384,128]{2,1,0:T(8,128)(2,1)S(1)}, u32[]{:S(2)}, u32[]{:S(2)}) collective-permute-start(bf16[2,384,128]{2,1,0:T(8,128)(2,1)S(1)} %get-tuple-element.51.refs_0_), channel_id=1, source_target_pairs={{0,8},{8,0},{16,24},{24,16},{1,9},{9,1},{17,25},{25,17},{2,10},{10... | collective-permute-start | bytes 589832 | tf_op jit(solution)/shard_map/ppermute | solution.py:321
  9.6 0.1 collective-permute-start.12
  9.7 0.4 %collective-permute-start.3 = (bf16[64,1024]{1,0:T(8,128)(2,1)S(1)}, bf16[64,1024]{1,0:T(8,128)(2,1)S(1)}, u32[]{:S(2)}, u32[]{:S(2)}) collective-permute-start(bf16[64,1024]{1,0:T(8,128)(2,1)S(1)} %get-tuple-element.40.q_own.refs_3_), channel_id=1, source_target_pairs={{0,8},{8,0},{16,24},{24,16},{1,9},{9,1},{17,25},{25,17},{2,10},{10... | collective-permute-start | bytes 393224 | tf_op jit(solution)/shard_map/ppermute | solution.py:321
  10.2 2.9 %collective-permute-done.4.refs_1_.refs_4_ = bf16[2,512,128]{2,1,0:T(8,128)(2,1)S(1)} collective-permute-done((bf16[2,512,128]{2,1,0:T(8,128)(2,1)S(1)}, bf16[2,512,128]{2,1,0:T(8,128)(2,1)S(1)}, u32[]{:S(2)}, u32[]{:S(2)}) %collective-permute-start.4) | collective-permute-done | bytes 262176 | tf_op jit(solution)/shard_map/ppermute | solution.py:321
  13.1 0.1 collective-permute-start.7
  13.1 0.0 collective-permute-done.6.refs_2_.refs_5_
  13.2 1.2 %collective-permute-done.7.refs_3_.refs_6_ = bf16[2,128,128]{2,1,0:T(8,128)(2,1)S(1)} collective-permute-done((bf16[2,128,128]{2,1,0:T(8,128)(2,1)S(1)}, bf16[2,128,128]{2,1,0:T(8,128)(2,1)S(1)}, u32[]{:S(2)}, u32[]{:S(2)}) %collective-permute-start.7) | collective-permute-done | bytes 65568 | tf_op jit(solution)/shard_map/ppermute | solution.py:324
  14.4 2.0 %collective-permute-start.8 = (bf16[4,2,128,128]{3,2,1,0:T(8,128)(2,1)S(1)}, bf16[4,2,128,128]{3,2,1,0:T(8,128)(2,1)S(1)}, u32[]{:S(2)}, u32[]{:S(2)}) collective-permute-start(bf16[4,2,128,128]{3,2,1,0:T(8,128)(2,1)S(1)} %pad_maximum_fusion), channel_id=1, source_target_pairs={{0,1},{1,0},{2,3},{3,2},{4,5},{5,4},{6,7},{7,6},{8,9},{9,8},{10,11... | collective-permute-start | bytes 786440 | tf_op jit(solution)/shard_map/ppermute | solution.py:327
  16.4 5.9 %collective-permute-start.11 = (bf16[64,1024]{1,0:T(8,128)(2,1)S(1)}, bf16[64,1024]{1,0:T(8,128)(2,1)S(1)}, u32[]{:S(2)}, u32[]{:S(2)}) collective-permute-start(bf16[64,1024]{1,0:T(8,128)(2,1)S(1)} %get-tuple-element.50.q_own.refs_2_), channel_id=1, source_target_pairs={{0,8},{8,0},{16,24},{24,16},{1,9},{9,1},{17,25},{25,17},{2,10},{10... | collective-permute-start | bytes 393224 | tf_op jit(solution)/shard_map/ppermute | solution.py:321
  22.3 0.0 collective-permute-done.9.refs_1_
  22.4 0.0 collective-permute-start.10
  22.4 0.0 collective-permute-done.3.q_end.refs_2_
  22.4 0.6 %collective-permute-start.5 = (bf16[2,384,128]{2,1,0:T(8,128)(2,1)S(1)}, bf16[2,384,128]{2,1,0:T(8,128)(2,1)S(1)}, u32[]{:S(2)}, u32[]{:S(2)}) collective-permute-start(bf16[2,384,128]{2,1,0:T(8,128)(2,1)S(1)} %slice.17), channel_id=1, source_target_pairs={{0,2},{8,16},{16,8},{24,26},{2,0},{10,18},{18,10},{26,24},{4,6},{1... | collective-permute-start | bytes 589832 | tf_op jit(solution)/shard_map/ppermute | solution.py:324
  23.0 0.6 %shard_map.83 = (f32[2,512,128]{2,1,0:T(8,128)S(1)}, f32[2,512,128]{2,1,0:T(8,128)S(1)}, f32[2,512,128]{2,1,0:T(8,128)S(1)}) custom-call(s32[32]{0:T(128)S(1)} %get-tuple-element.38.limits.refs_0_, bf16[64,1024]{1,0:T(8,128)(2,1)S(1)} %get-tuple-element.40.q_own.refs_3_, bf16[64,1024]{1,0:T(8,128)(2,1)S(1)} %collective-permute-done.3.q_end.refs_2_, ...), custom_call_target="tpu_custom_call" | custom-call | flops 738197504 | bytes 4194304 | tf_op jit(solution)/shard_map/pallas_call | solution.py:402
  23.5 1.8 %collective-permute-done.11.q_end.refs_2_ = bf16[64,1024]{1,0:T(8,128)(2,1)S(1)} collective-permute-done((bf16[64,1024]{1,0:T(8,128)(2,1)S(1)}, bf16[64,1024]{1,0:T(8,128)(2,1)S(1)}, u32[]{:S(2)}, u32[]{:S(2)}) %collective-permute-start.11) | collective-permute-done | bytes 131104 | tf_op jit(solution)/shard_map/ppermute | solution.py:321
  25.3 0.0 collective-permute-done.12.refs_2_
  25.3 0.6 %shard_map.85 = (f32[2,512,128]{2,1,0:T(8,128)S(1)}, f32[2,512,128]{2,1,0:T(8,128)S(1)}, f32[2,512,128]{2,1,0:T(8,128)S(1)}) custom-call(s32[32]{0:T(128)S(1)} %get-tuple-element.38.limits.refs_0_, bf16[64,1024]{1,0:T(8,128)(2,1)S(1)} %get-tuple-element.50.q_own.refs_2_, bf16[64,1024]{1,0:T(8,128)(2,1)S(1)} %collective-permute-done.11.q_end.refs_2_, ...), custom_call_target="tpu_custom_call" | custom-call | flops 738197504 | bytes 4194304 | tf_op jit(solution)/shard_map/pallas_call | solution.py:402
  25.9 0.0 collective-permute-done.10.refs_3_
  25.9 0.0 collective-permute-done.8.refs_5_.refs_4_
  25.9 1.1 %shard_map.87 = bf16[64,1024]{1,0:T(8,128)(2,1)S(1)} custom-call(s32[32]{0:T(128)S(1)} %get-tuple-element.38.limits.refs_0_, s32[1]{0:T(128)} %get-tuple-element.39.refs_1_, bf16[64,1024]{1,0:T(8,128)(2,1)S(1)} %collective-permute-done.11.q_end.refs_2_, bf16[2,384,128]{2,1,0:T(8,128)(2,1)S(1)} %collective-permute-done.10.refs_3_, ...), custom_call_target="tpu_custom_call" | custom-call | flops 167772160 | bytes 1048576 | tf_op jit(solution)/shard_map/pallas_call | solution.py:412
  27.0 5.8 %collective-permute-start.14 = (bf16[64,1024]{1,0:T(8,128)(2,1)S(1)}, bf16[64,1024]{1,0:T(8,128)(2,1)S(1)}, u32[]{:S(2)}, u32[]{:S(2)}) collective-permute-start(bf16[64,1024]{1,0:T(8,128)(2,1)S(1)} %shard_map.87), channel_id=1, source_target_pairs={{0,8},{8,0},{16,24},{24,16},{1,9},{9,1},{17,25},{25,17},{2,10},{10... | collective-permute-start | bytes 393224 | tf_op jit(solution)/shard_map/ppermute | solution.py:321
  32.8 0.0 collective-permute-done.5.refs_4_
  32.8 1.3 %shard_map.84 = (bf16[64,1024]{1,0:T(8,128)(2,1)S(1)}, bf16[64,1024]{1,0:T(8,128)(2,1)S(1)}) custom-call(s32[32]{0:T(128)S(1)} %get-tuple-element.38.limits.refs_0_, s32[1]{0:T(128)} %get-tuple-element.39.refs_1_, bf16[64,1024]{1,0:T(8,128)(2,1)S(1)} %collective-permute-done.3.q_end.refs_2_, bf16[64,1024]{1,0:T(8,128)(2,1)S(1)} %get-tuple-element.40.q_own.refs_3_, ...), custom_call_target="tpu_custom_call" | custom-call | flops 335544320 | bytes 2097152 | tf_op jit(solution)/shard_map/pallas_call | solution.py:412
  34.2 1.9 %collective-permute-start.13 = (bf16[64,1024]{1,0:T(8,128)(2,1)S(1)}, bf16[64,1024]{1,0:T(8,128)(2,1)S(1)}, u32[]{:S(2)}, u32[]{:S(2)}) collective-permute-start(bf16[64,1024]{1,0:T(8,128)(2,1)S(1)} %get-tuple-element.55), channel_id=1, source_target_pairs={{0,8},{8,0},{16,24},{24,16},{1,9},{9,1},{17,25},{25,17},{2,10},{10... | collective-permute-start | bytes 393224 | tf_op jit(solution)/shard_map/ppermute | solution.py:321
  36.1 1.1 %shard_map.86.own1 = bf16[64,1024]{1,0:T(8,128)(2,1)S(1)} custom-call(s32[32]{0:T(128)S(1)} %get-tuple-element.38.limits.refs_0_, s32[1]{0:T(128)} %get-tuple-element.39.refs_1_, bf16[64,1024]{1,0:T(8,128)(2,1)S(1)} %get-tuple-element.50.q_own.refs_2_, bf16[2,384,128]{2,1,0:T(8,128)(2,1)S(1)} %collective-permute-done.10.refs_3_, ...), custom_call_target="tpu_custom_call" | custom-call | flops 167772160 | bytes 1048576 | tf_op jit(solution)/shard_map/pallas_call | solution.py:412
  37.2 0.0 collective-permute-done.14.back1
  37.2 2.0 %collective-permute-done.13.back0 = bf16[64,1024]{1,0:T(8,128)(2,1)S(1)} collective-permute-done((bf16[64,1024]{1,0:T(8,128)(2,1)S(1)}, bf16[64,1024]{1,0:T(8,128)(2,1)S(1)}, u32[]{:S(2)}, u32[]{:S(2)}) %collective-permute-start.13) | collective-permute-done | bytes 131104 | tf_op jit(solution)/shard_map/ppermute | solution.py:321
  39.2 0.7 %shard_map.88 = bf16[1,64,2048]{2,1,0:T(8,128)(2,1)} custom-call(bf16[64,1024]{1,0:T(8,128)(2,1)S(1)} %get-tuple-element.49.own0, bf16[64,1024]{1,0:T(8,128)(2,1)S(1)} %shard_map.86.own1, bf16[64,1024]{1,0:T(8,128)(2,1)S(1)} %collective-permute-done.13.back0, bf16[64,1024]{1,0:T(8,128)(2,1)S(1)} %collective-permute-done.14.back1), custom_call_target="tpu_custom_call" | custom-call | bytes 1048576 | tf_op jit(solution)/shard_map/pallas_call | solution.py:429
  (7 shorter events, 0.1 us)
Async XLA Ops:
  2.8 10.3 %collective-permute-start.4 = (bf16[2,512,128]{2,1,0:T(8,128)(2,1)S(1)}, bf16[2,512,128]{2,1,0:T(8,128)(2,1)S(1)}, u32[]{:S(2)}, u32[]{:S(2)}) collective-permute-start(bf16[2,512,128]{2,1,0:T(8,128)(2,1)S(1)} %get-tuple-element.41.refs_0_.refs_3_), channel_id=1, source_target_pairs={{0,8},{8,0},{16,24},{24,16},{1,9},{9,1},{17,25},{25,17},{2,10},{10... | collective-permute-start | bytes 786440 | tf_op jit(solution)/shard_map/ppermute | solution.py:321
  5.9 7.3 %collective-permute-start.6 = (bf16[2,512,128]{2,1,0:T(8,128)(2,1)S(1)}, bf16[2,512,128]{2,1,0:T(8,128)(2,1)S(1)}, u32[]{:S(2)}, u32[]{:S(2)}) collective-permute-start(bf16[2,512,128]{2,1,0:T(8,128)(2,1)S(1)} %get-tuple-element.41.refs_0_.refs_3_), channel_id=1, source_target_pairs={{0,2},{8,16},{16,8},{24,26},{2,0},{10,18},{18,10},{26,24},{4,6},{1... | collective-permute-start | bytes 786440 | tf_op jit(solution)/shard_map/ppermute | solution.py:324
  5.9 16.5 %collective-permute-start.9 = (bf16[2,384,128]{2,1,0:T(8,128)(2,1)S(1)}, bf16[2,384,128]{2,1,0:T(8,128)(2,1)S(1)}, u32[]{:S(2)}, u32[]{:S(2)}) collective-permute-start(bf16[2,384,128]{2,1,0:T(8,128)(2,1)S(1)} %get-tuple-element.51.refs_0_), channel_id=1, source_target_pairs={{0,8},{8,0},{16,24},{24,16},{1,9},{9,1},{17,25},{25,17},{2,10},{10... | collective-permute-start | bytes 589832 | tf_op jit(solution)/shard_map/ppermute | solution.py:321
  9.6 15.7 %collective-permute-start.12 = (bf16[2,384,128]{2,1,0:T(8,128)(2,1)S(1)}, bf16[2,384,128]{2,1,0:T(8,128)(2,1)S(1)}, u32[]{:S(2)}, u32[]{:S(2)}) collective-permute-start(bf16[2,384,128]{2,1,0:T(8,128)(2,1)S(1)} %get-tuple-element.51.refs_0_), channel_id=1, source_target_pairs={{0,2},{8,16},{16,8},{24,26},{2,0},{10,18},{18,10},{26,24},{4,6},{1... | collective-permute-start | bytes 589832 | tf_op jit(solution)/shard_map/ppermute | solution.py:324
  9.7 12.7 %collective-permute-start.3 = (bf16[64,1024]{1,0:T(8,128)(2,1)S(1)}, bf16[64,1024]{1,0:T(8,128)(2,1)S(1)}, u32[]{:S(2)}, u32[]{:S(2)}) collective-permute-start(bf16[64,1024]{1,0:T(8,128)(2,1)S(1)} %get-tuple-element.40.q_own.refs_3_), channel_id=1, source_target_pairs={{0,8},{8,0},{16,24},{24,16},{1,9},{9,1},{17,25},{25,17},{2,10},{10... | collective-permute-start | bytes 393224 | tf_op jit(solution)/shard_map/ppermute | solution.py:321
  13.1 1.3 %collective-permute-start.7 = (bf16[2,128,128]{2,1,0:T(8,128)(2,1)S(1)}, bf16[2,128,128]{2,1,0:T(8,128)(2,1)S(1)}, u32[]{:S(2)}, u32[]{:S(2)}) collective-permute-start(bf16[2,128,128]{2,1,0:T(8,128)(2,1)S(1)} %get-tuple-element.57), channel_id=1, source_target_pairs={{0,2},{8,16},{16,8},{24,26},{2,0},{10,18},{18,10},{26,24},{4,6},{1... | collective-permute-start | bytes 196616 | tf_op jit(solution)/shard_map/ppermute | solution.py:324
  14.4 11.4 %collective-permute-start.8 = (bf16[4,2,128,128]{3,2,1,0:T(8,128)(2,1)S(1)}, bf16[4,2,128,128]{3,2,1,0:T(8,128)(2,1)S(1)}, u32[]{:S(2)}, u32[]{:S(2)}) collective-permute-start(bf16[4,2,128,128]{3,2,1,0:T(8,128)(2,1)S(1)} %pad_maximum_fusion), channel_id=1, source_target_pairs={{0,1},{1,0},{2,3},{3,2},{4,5},{5,4},{6,7},{7,6},{8,9},{9,8},{10,11... | collective-permute-start | bytes 786440 | tf_op jit(solution)/shard_map/ppermute | solution.py:327
  16.4 8.8 %collective-permute-start.11 = (bf16[64,1024]{1,0:T(8,128)(2,1)S(1)}, bf16[64,1024]{1,0:T(8,128)(2,1)S(1)}, u32[]{:S(2)}, u32[]{:S(2)}) collective-permute-start(bf16[64,1024]{1,0:T(8,128)(2,1)S(1)} %get-tuple-element.50.q_own.refs_2_), channel_id=1, source_target_pairs={{0,8},{8,0},{16,24},{24,16},{1,9},{9,1},{17,25},{25,17},{2,10},{10... | collective-permute-start | bytes 393224 | tf_op jit(solution)/shard_map/ppermute | solution.py:321
  22.4 3.5 %collective-permute-start.10 = (bf16[2,384,128]{2,1,0:T(8,128)(2,1)S(1)}, bf16[2,384,128]{2,1,0:T(8,128)(2,1)S(1)}, u32[]{:S(2)}, u32[]{:S(2)}) collective-permute-start(bf16[2,384,128]{2,1,0:T(8,128)(2,1)S(1)} %collective-permute-done.9.refs_1_), channel_id=1, source_target_pairs={{0,2},{8,16},{16,8},{24,26},{2,0},{10,18},{18,10},{26,24},{4,6},{1... | collective-permute-start | bytes 589832 | tf_op jit(solution)/shard_map/ppermute | solution.py:324
  22.4 10.5 %collective-permute-start.5 = (bf16[2,384,128]{2,1,0:T(8,128)(2,1)S(1)}, bf16[2,384,128]{2,1,0:T(8,128)(2,1)S(1)}, u32[]{:S(2)}, u32[]{:S(2)}) collective-permute-start(bf16[2,384,128]{2,1,0:T(8,128)(2,1)S(1)} %slice.17), channel_id=1, source_target_pairs={{0,2},{8,16},{16,8},{24,26},{2,0},{10,18},{18,10},{26,24},{4,6},{1... | collective-permute-start | bytes 589832 | tf_op jit(solution)/shard_map/ppermute | solution.py:324
  27.0 10.2 %collective-permute-start.14 = (bf16[64,1024]{1,0:T(8,128)(2,1)S(1)}, bf16[64,1024]{1,0:T(8,128)(2,1)S(1)}, u32[]{:S(2)}, u32[]{:S(2)}) collective-permute-start(bf16[64,1024]{1,0:T(8,128)(2,1)S(1)} %shard_map.87), channel_id=1, source_target_pairs={{0,8},{8,0},{16,24},{24,16},{1,9},{9,1},{17,25},{25,17},{2,10},{10... | collective-permute-start | bytes 393224 | tf_op jit(solution)/shard_map/ppermute | solution.py:321
  34.2 5.0 %collective-permute-start.13 = (bf16[64,1024]{1,0:T(8,128)(2,1)S(1)}, bf16[64,1024]{1,0:T(8,128)(2,1)S(1)}, u32[]{:S(2)}, u32[]{:S(2)}) collective-permute-start(bf16[64,1024]{1,0:T(8,128)(2,1)S(1)} %get-tuple-element.55), channel_id=1, source_target_pairs={{0,8},{8,0},{16,24},{24,16},{1,9},{9,1},{17,25},{25,17},{2,10},{10... | collective-permute-start | bytes 393224 | tf_op jit(solution)/shard_map/ppermute | solution.py:321

commit v4 on v3

--- a/solution.py
+++ b/solution.py
@@ -65,6 +65,8 @@
         count[holder] = nth + 1
         limits[holder * held + nth] = length[0, number]
         source[holder * held + nth] = place - holder * held
+    for i in range(holders):
+        limits[holders * held + i] = count[i]
     most[0] = functools.reduce(jnp.maximum, [count[i] for i in range(holders)])
 
 
@@ -87,7 +89,7 @@
 
 
 def pack_body(
-    table_in, slot_in, length_in, pk, pv, nk, nv, q, pack0, pack1, q0, q1, limits, most,
+    table_in, slot_in, length_in, pk, pv, nk, nv, q, pack0, pack1, fresh, q0, q1, limits, most,
     table, slot, length, source, count, sem, sem_new, *, cap
 ):
     half = q0.shape[1]
@@ -97,13 +99,14 @@
         copies.append(pltpu.make_async_copy(q.at[0, :, pl.ds(wide, half)], near, sem_new.at[i]))
     for w, new in enumerate((nk, nv)):
         for g in range(2):
-            copies.append(
-                pltpu.make_async_copy(
-                    new.at[0, :, pl.ds(g * HD, HD)],
-                    pack0.at[w, pl.ds(cap * PAGE + g * rows_dev, rows_dev), :],
-                    sem_new.at[2 + w * 2 + g],
+            for n, (pack, row) in enumerate(((pack0, cap * PAGE), (fresh, 0))):
+                copies.append(
+                    pltpu.make_async_copy(
+                        new.at[0, :, pl.ds(g * HD, HD)],
+                        pack.at[w, pl.ds(row + g * rows_dev, rows_dev), :],
+                        sem_new.at[2 + (n * 2 + w) * 2 + g],
+                    )
                 )
-            )
     for copy in copies:
         copy.start()
     listed_pages(
@@ -149,14 +152,65 @@
     )
 
 
-def page_bias(limits, holder, held, first, cap):
-    column = lax.broadcasted_iota(jnp.int32, (1, cap * PAGE), 1)
+def page_bias(limits, first, count):
+    column = lax.broadcasted_iota(jnp.int32, (1, count * PAGE), 1)
     page = column // PAGE
     within = column - page * PAGE
-    limit = jnp.zeros((1, cap * PAGE), jnp.int32)
+    limit = jnp.zeros((1, count * PAGE), jnp.int32)
+    for j in range(count):
+        limit = jnp.where(page == j, limits[first + j], limit)
+    return jnp.where(within < limit, 0.0, neg_floor).astype(jnp.float32)
+
+
+def held_pages(limits):
+    holders = lax.axis_size("ctx")
+    return limits.shape[0] // holders - 1
+
+
+def join_limits(limits, ids, cap, joined):
+    holders = lax.axis_size("ctx")
+    held = held_pages(limits)
+    for i in range(joined.shape[0]):
+        joined[i] = 0
+    offsets = []
+    offset = jnp.int32(0)
+    for holder in ids:
+        offsets.append(offset)
+        for j in range(cap):
+            joined[offset + j] = limits[holder * held + j]
+        offset = offset + jnp.minimum(limits[holders * held + holder], cap)
+    return offsets, offset
+
+
+def plan_body(limits, marks, bias_early, bias_late, bias_spare, joined, last, *, cap, early):
+    holders = lax.axis_size("ctx")
+    held = held_pages(limits)
+    ids = holder_ids(lax.axis_index("ctx"))
+    offsets, total = join_limits(limits, ids[:3], cap, joined)
+    more = jnp.maximum(total - early, 0)
     for j in range(cap):
-        limit = jnp.where(page == j, limits[holder * held + first + j], limit)
-    return jnp.where(within < limit, 0.0, neg_floor).astype(jnp.float32)
+        last[j] = joined[early + j]
+    for j in range(cap):
+        last[more + j] = limits[ids[3] * held + j]
+    most = functools.reduce(jnp.maximum, [limits[holders * held + i] for i in range(holders)])
+    for i, mark in enumerate((offsets[1], offsets[2], more, most)):
+        marks[i] = mark
+    for ref, bias in (
+        (bias_early, page_bias(joined, 0, early)),
+        (bias_late, page_bias(last, 0, cap)),
+    ):
+        ref[...] = jnp.broadcast_to(bias, ref.shape)
+    for i, holder in enumerate(ids):
+        bias = page_bias(limits, holder * held + cap, held - cap)
+        bias_spare[i] = jnp.broadcast_to(bias, bias_spare.shape[1:])
+
+
+def place_pages(dense, packs, offsets, cap):
+    for b, pack in enumerate(packs):
+        dense[:, b * cap * PAGE : (b + 1) * cap * PAGE, :] = pack[:, : cap * PAGE, :]
+    for pack, offset in list(zip(packs, offsets))[1:]:
+        row = pl.multiple_of(offset * PAGE, PAGE)
+        dense[:, pl.ds(row, cap * PAGE), :] = pack[:, : cap * PAGE, :]
 
 
 def causal_bias(position, ids, rows, rows_dev):
@@ -197,29 +251,27 @@
     return total, acc + old_acc * rescale
 
 
-def early_body(limits, q_own, q_end, *refs, cap, g):
+def early_body(marks, bias_early, q_own, q_end, *refs, cap, early, g):
+    tops, totals, accs, left, dense = refs[-5:]
     packs = refs[:3]
-    news = refs[3:7] if len(refs) == 10 else packs + refs[3:4]
-    tops, totals, accs = refs[-3:]
+    news = refs[3:7] if len(refs) == 12 else packs + refs[3:4]
     position = lax.axis_index("ctx")
-    held = limits.shape[0] // lax.axis_size("ctx")
     rows_dev = q_own.shape[0]
     rows = accs.shape[1]
-    pages = cap * PAGE
 
     @pl.when(is_inner(position))
     def _():
         ids = holder_ids(position)
+        place_pages(dense, packs, (0, marks[0], marks[1]), cap)
         firsts = [n.shape[1] - 2 * rows_dev + g * rows_dev for n in news]
         nk = jnp.concatenate([n[0, i : i + rows_dev] for n, i in zip(news, firsts)], axis=0)
         nv = jnp.concatenate([n[1, i : i + rows_dev] for n, i in zip(news, firsts)], axis=0)
-        paged = [
-            (p[0, :pages], p[1, :pages], page_bias(limits, i, held, 0, cap))
-            for p, i in zip(packs, ids)
-        ]
+        split = early * PAGE
+        left[...] = dense[:, split : split + left.shape[1], :]
+        paged = (dense[0, :split], dense[1, :split], bias_early[0:1, :])
         for t, q in enumerate((q_own, q_end)):
             fresh = (nk, nv, causal_bias(position ^ t, ids, rows, rows_dev))
-            top, total, acc = attend(heads_of(q), paged + [fresh])
+            top, total, acc = attend(heads_of(q), [paged, fresh])
             tops[t] = jnp.broadcast_to(top, acc.shape)
             totals[t] = jnp.broadcast_to(total, acc.shape)
             accs[t] = acc
@@ -227,24 +279,22 @@
 
 def late_body(*refs, cap, g, tasks):
     n = len(tasks)
-    limits, most = refs[:2]
-    queries = refs[2 : 2 + n]
-    pack, taken, tops, totals, accs = refs[2 + n : 7 + n]
-    spilled = refs[7 + n : 11 + n]
-    outs = refs[11 + n : 11 + 2 * n]
-    extra, sem = refs[11 + 2 * n :]
-    position = lax.axis_index("ctx")
-    held = limits.shape[0] // lax.axis_size("ctx")
+    marks, bias_late, bias_spare = refs[:3]
+    queries = refs[3 : 3 + n]
+    pack, taken, left, tops, totals, accs = refs[3 + n : 9 + n]
+    spilled = refs[9 + n : 13 + n]
+    outs = refs[13 + n : 13 + 2 * n]
+    extra, sem, dense = refs[13 + 2 * n :]
 
     def finish(more):
-        ids = holder_ids(position)
         rows_dev = queries[0].shape[0]
+        place_pages(dense, (left, pack), (0, marks[2]), cap)
         new = slice(g * rows_dev, (g + 1) * rows_dev)
         shut = jnp.where(lax.axis_index("grp") == 1, 0.0, neg_floor).astype(jnp.float32)
         tk = jnp.concatenate([taken[i, 0, new] for i in range(taken.shape[0])], axis=0)
         tv = jnp.concatenate([taken[i, 1, new] for i in range(taken.shape[0])], axis=0)
         blocks = [
-            (pack[0], pack[1], page_bias(limits, ids[3], held, 0, cap)),
+            (dense[0, : cap * PAGE], dense[1, : cap * PAGE], bias_late[0:1, :]),
             (tk, tv, jnp.full((1, tk.shape[0]), shut, jnp.float32)),
         ]
         if more:
@@ -256,17 +306,16 @@
                 copy.start()
             for copy in copies:
                 copy.wait()
-            for i, holder in enumerate(ids):
-                bias = page_bias(limits, holder, held, cap, held - cap)
-                blocks.append((extra[i, 0], extra[i, 1], bias))
+            for i in range(len(spilled)):
+                blocks.append((extra[i, 0], extra[i, 1], bias_spare[i, 0:1, :]))
         for t, q, out in zip(tasks, queries, outs):
             total, num = attend(heads_of(q), blocks, (tops[t], totals[t], accs[t]))
             result = (num / total).astype(jnp.bfloat16)
             for i in range(out.shape[1] // HD):
                 out[:, i * HD : (i + 1) * HD] = result[i * rows_dev : (i + 1) * rows_dev]
 
-    inner = is_inner(position)
-    over = most[0] > cap
+    inner = is_inner(lax.axis_index("ctx"))
+    over = marks[3] > cap
 
     @pl.when(inner & jnp.logical_not(over))
     def _():
@@ -342,33 +391,47 @@
         pltpu.SMEM((holders * held,), jnp.int32),
         pltpu.SMEM((holders,), jnp.int32),
     ]
-    pack0, pack1, q0, q1, limits, most = call(
+    pack0, pack1, fresh, q0, q1, limits, most = call(
         functools.partial(pack_body, cap=cap),
         (
             sds((2, keys + 2 * rows_dev, HD)),
             sds((2, keys, HD)),
+            sds((2, 2 * rows_dev, HD)),
             half,
             half,
-            sds((holders * held,), jnp.int32),
+            sds((holders * held + holders,), jnp.int32),
             sds((1,), jnp.int32),
         ),
         [HBM] * 8,
-        (VMEM, VMEM, VMEM, VMEM, SMEM, SMEM),
-        scalars + [pltpu.SemaphoreType.DMA((cap * 4,)), pltpu.SemaphoreType.DMA((6,))],
+        (VMEM,) * 5 + (SMEM, SMEM),
+        scalars + [pltpu.SemaphoreType.DMA((cap * 4,)), pltpu.SemaphoreType.DMA((10,))],
         nbytes=3 << 20,
     )(*tables, new_keys, new_values, queries)
 
     near0 = swap_side(pack0)
     far0 = swap_middle(pack0)
+    n_last = lax.ppermute(fresh, "ctx", [(0, 2), (2, 3), (3, 1), (1, 0)])
     q0_end = swap_side(q0)
-    n_last = swap_middle(near0[:, keys:])
+    far1 = swap_middle(pack1)
     near1 = swap_side(pack1)
-    far1 = swap_middle(pack1)
+    last0 = swap_middle(near0[:, :keys])
     q1_end = swap_side(q1)
-    last0 = swap_middle(near0[:, :keys])
-    fresh = [pack0[:, keys:], near0[:, keys:], far0[:, keys:], n_last]
-    taken = swap_pools(jnp.stack(fresh))
+    taken = swap_pools(jnp.stack([fresh, near0[:, keys:], far0[:, keys:], n_last]))
     last1 = swap_middle(near1)
+    early_pages = page_table.shape[2] - cap
+    marks, bias_early, bias_late, bias_spare = call(
+        functools.partial(plan_body, cap=cap, early=early_pages),
+        (
+            sds((8,), jnp.int32),
+            sds((8, early_pages * PAGE), jnp.float32),
+            sds((8, keys), jnp.float32),
+            sds((holders, 8, (held - cap) * PAGE), jnp.float32),
+        ),
+        [SMEM],
+        (SMEM, VMEM, VMEM, VMEM),
+        [pltpu.SMEM((early_pages + 2 * cap,), jnp.int32), pltpu.SMEM((2 * cap,), jnp.int32)],
+        nbytes=1 << 19,
+    )(limits)
     spare = sds((2, 2, (held - cap) * PAGE, HD))
 
     def fetch():
@@ -379,7 +442,7 @@
             VMEM,
             scalars
             + [
-                pltpu.SMEM((holders * held,), jnp.int32),
+                pltpu.SMEM((holders * held + holders,), jnp.int32),
                 pltpu.SMEM((1,), jnp.int32),
                 pltpu.SemaphoreType.DMA((max(held - cap, 1) * 4,)),
             ],
@@ -396,28 +459,34 @@
 
     rows = group * rows_dev
     pair_flops = 4 * rows * HD
-    state = (sds((2, rows, HD), jnp.float32),) * 3
+    state = (sds((2, rows, HD), jnp.float32),) * 3 + (sds((2, keys, HD)),)
 
     def early(g, q, q_end, packs, news):
         return call(
-            functools.partial(early_body, cap=cap, g=g),
+            functools.partial(early_body, cap=cap, early=early_pages, g=g),
             state,
-            [SMEM] + [VMEM] * (5 + len(news)),
-            (VMEM,) * 3,
-            flops=2 * pair_flops * (3 * keys + 4 * rows_dev),
+            [SMEM] + [VMEM] * (6 + len(news)),
+            (VMEM,) * 4,
+            [pltpu.VMEM((2, (early_pages + 2 * cap) * PAGE, HD), jnp.bfloat16)],
+            flops=2 * pair_flops * (early_pages * PAGE + 4 * rows_dev),
             nbytes=4 << 20,
-        )(limits, q, q_end, *packs, *news)
+        )(marks, bias_early, q, q_end, *packs, *news)
 
     def late(g, tasks, queries, pack, carried):
+        tops, totals, accs, left = carried
         return call(
             functools.partial(late_body, cap=cap, g=g, tasks=tasks),
             (half,) * len(tasks),
-            [SMEM, SMEM] + [VMEM] * (5 + len(tasks)) + [HBM] * 4,
+            [SMEM] + [VMEM] * (8 + len(tasks)) + [HBM] * 4,
             (VMEM,) * len(tasks),
-            [pltpu.VMEM((4, 2, (held - cap) * PAGE, HD), jnp.bfloat16), pltpu.SemaphoreType.DMA((4,))],
+            [
+                pltpu.VMEM((4, 2, (held - cap) * PAGE, HD), jnp.bfloat16),
+                pltpu.SemaphoreType.DMA((4,)),
+                pltpu.VMEM((2, 2 * keys, HD), jnp.bfloat16),
+            ],
             flops=len(tasks) * pair_flops * (keys + 4 * rows_dev),
             nbytes=len(tasks) << 20,
-        )(limits, most, *queries, pack, taken, *carried, *spilled)
+        )(marks, bias_late, bias_spare, *queries, pack, taken, left, tops, totals, accs, *spilled)
 
     carried0 = early(0, q0, q0_end, (pack0, near0, far0), (n_last,))
     carried1 = early(1, q1, q1_end, (pack1, near1, far1), (pack0, near0, far0, n_last))

time: 40.2 us -> 43.2 us (1.075)
  waiting for transfers between devices: 7.89 us -> 11.1 us
    ppermute x0 -> x1, waiting for transfers between devices: none -> 5.59 us  [chain_steps(): n_last = lax.ppermute(fresh, 'ctx', [(0, 2), (2, 3), (3, 1), (1, 0)])]
    pallas_call x3, Pallas kernels: 3.61 us -> 1.97 us  [late(): call(functools.partial(late_body, cap=cap, g=g, tasks=tasks), (half,) * l...]
    ppermute x5 -> x4, waiting for transfers between devices: 1.23 us -> 0.01 us  [swap_middle(): return lax.ppermute(x, ('ctx', 'head'), middle)]
    pallas_call x2 -> x3, Pallas kernels: 1.11 us -> 2.31 us  [the longest x1 1.19 us: chain_steps(): call(functools.partial(plan_body, cap=cap, early=early_pages), (sds((8,),...]
    ppermute x6, waiting for transfers between devices: 6.66 us -> 5.5 us  [swap_side(): return lax.ppermute(x, 'ctx', side)]
  transfers between devices with their start and end apart: 12 -> 12, of which waited for: 4 -> 4; matrix products, arithmetic and copies ran while one was open for 0% -> 0% of each run, Pallas kernels for 12% -> 10%
where the time goes in v4:
time: 43.2 us; the launch traced here: 43 us
  starting transfers between devices  23.2 us (54%)
  waiting for transfers between devices  11.1 us (26%)
  Pallas kernels  7.79 us (18%)
  between operations  0.79 us (2%)
    ppermute x6, starting transfers between devices, swap_side(): return lax.ppermute(x, 'ctx', side)  20.5 us
    ppermute x1, waiting for transfers between devices, chain_steps(): n_last = lax.ppermute(fresh, 'ctx', [(0, 2), (2, 3), (3, 1), (1, 0)])  5.59 us
    ppermute x6, waiting for transfers between devices, swap_side(): return lax.ppermute(x, 'ctx', side)  5.5 us
    pallas_call x1, Pallas kernels, chain_steps(): call(functools.partial(pack_body, cap=cap), (sds((2, keys + 2 * rows_dev,...  2.79 us
    ppermute x1, starting transfers between devices, swap_pools(): return lax.ppermute(x, 'grp', [(0, 1), (1, 0)])  2.02 us
    pallas_call x3, Pallas kernels, late(): call(functools.partial(late_body, cap=cap, g=g, tasks=tasks), (half,) * l...  1.97 us
    pallas_call x1, Pallas kernels, chain_steps(): call(functools.partial(plan_body, cap=cap, early=early_pages), (sds((8,),...  1.19 us
    pallas_call x2, Pallas kernels, early(): call(functools.partial(early_body, cap=cap, early=early_pages, g=g), stat...  1.11 us
  transfers between devices with their start and end apart: 12, of which 4 were waited for; matrix products, arithmetic and copies ran while one was open for 0% of the time, Pallas kernels for 10%

profile of v4, /device:TPU:0, one launch (start us, length us, event | category | flops | bytes accessed | tf_op | source)
XLA Modules:
  0.0 43.0 jit_solution(12048834616175930083)
XLA Ops:
  0.0 2.8 %shard_map.82 = (bf16[2,512,128]{2,1,0:T(8,128)(2,1)S(1)}, bf16[2,384,128]{2,1,0:T(8,128)(2,1)S(1)}, bf16[2,128,128]{2,1,0:T(8,128)(2,1)S(1)}, bf16[64,1024]{1,0...) custom-call(s32[1,1,16]{2,1,0:T(1,128)} %table_in.1, s32[1,32]{1,0:T(1,128)} %slot_in.1, ...), custom_call_target="tpu_custom_call" | custom-call | bytes 3145728 | tf_op jit(solution)/shard_map/pallas_call | solution.py:394
  2.8 3.1 %collective-permute-start.4 = (bf16[2,512,128]{2,1,0:T(8,128)(2,1)S(1)}, bf16[2,512,128]{2,1,0:T(8,128)(2,1)S(1)}, u32[]{:S(2)}, u32[]{:S(2)}) collective-permute-start(bf16[2,512,128]{2,1,0:T(8,128)(2,1)S(1)} %get-tuple-element.50.refs_0_.refs_3_), channel_id=1, source_target_pairs={{0,8},{8,0},{16,24},{24,16},{1,9},{9,1},{17,25},{25,17},{2,10},{10... | collective-permute-start | bytes 786440 | tf_op jit(solution)/shard_map/ppermute | solution.py:370
  5.9 0.0 collective-permute-start.6
  5.9 3.1 %collective-permute-start.9 = (bf16[2,384,128]{2,1,0:T(8,128)(2,1)S(1)}, bf16[2,384,128]{2,1,0:T(8,128)(2,1)S(1)}, u32[]{:S(2)}, u32[]{:S(2)}) collective-permute-start(bf16[2,384,128]{2,1,0:T(8,128)(2,1)S(1)} %get-tuple-element.64.refs_0_), channel_id=1, source_target_pairs={{0,8},{8,0},{16,24},{24,16},{1,9},{9,1},{17,25},{25,17},{2,10},{10... | collective-permute-start | bytes 589832 | tf_op jit(solution)/shard_map/ppermute | solution.py:370
  9.1 0.0 collective-permute-start.7
  9.1 2.0 %collective-permute-start.3 = (bf16[64,1024]{1,0:T(8,128)(2,1)S(1)}, bf16[64,1024]{1,0:T(8,128)(2,1)S(1)}, u32[]{:S(2)}, u32[]{:S(2)}) collective-permute-start(bf16[64,1024]{1,0:T(8,128)(2,1)S(1)} %get-tuple-element.49.q_own.refs_4_), channel_id=1, source_target_pairs={{0,8},{8,0},{16,24},{24,16},{1,9},{9,1},{17,25},{25,17},{2,10},{10... | collective-permute-start | bytes 393224 | tf_op jit(solution)/shard_map/ppermute | solution.py:370
  11.1 2.0 %collective-permute-done.4.refs_1_.refs_4_ = bf16[2,512,128]{2,1,0:T(8,128)(2,1)S(1)} collective-permute-done((bf16[2,512,128]{2,1,0:T(8,128)(2,1)S(1)}, bf16[2,512,128]{2,1,0:T(8,128)(2,1)S(1)}, u32[]{:S(2)}, u32[]{:S(2)}) %collective-permute-start.4) | collective-permute-done | bytes 262176 | tf_op jit(solution)/shard_map/ppermute | solution.py:370
  13.1 0.0 collective-permute-done.6.refs_2_.refs_5_
  13.1 5.6 %collective-permute-done.7.refs_3_.refs_6_ = bf16[2,128,128]{2,1,0:T(8,128)(2,1)S(1)} collective-permute-done((bf16[2,128,128]{2,1,0:T(8,128)(2,1)S(1)}, bf16[2,128,128]{2,1,0:T(8,128)(2,1)S(1)}, u32[]{:S(2)}, u32[]{:S(2)}) %collective-permute-start.7) | collective-permute-done | bytes 65568 | tf_op jit(solution)/shard_map/ppermute | solution.py:413
  18.7 2.0 %collective-permute-start.8 = (bf16[4,2,128,128]{3,2,1,0:T(8,128)(2,1)S(1)}, bf16[4,2,128,128]{3,2,1,0:T(8,128)(2,1)S(1)}, u32[]{:S(2)}, u32[]{:S(2)}) collective-permute-start(bf16[4,2,128,128]{3,2,1,0:T(8,128)(2,1)S(1)} %pad_maximum_fusion), channel_id=1, source_target_pairs={{0,1},{1,0},{2,3},{3,2},{4,5},{5,4},{6,7},{7,6},{8,9},{9,8},{10,11... | collective-permute-start | bytes 786440 | tf_op jit(solution)/shard_map/ppermute | solution.py:376
  21.4 0.1 collective-permute-start.12
  21.5 0.0 collective-permute-done.9.refs_1_
  21.5 0.5 %collective-permute-start.10 = (bf16[2,384,128]{2,1,0:T(8,128)(2,1)S(1)}, bf16[2,384,128]{2,1,0:T(8,128)(2,1)S(1)}, u32[]{:S(2)}, u32[]{:S(2)}) collective-permute-start(bf16[2,384,128]{2,1,0:T(8,128)(2,1)S(1)} %collective-permute-done.9.refs_1_), channel_id=1, source_target_pairs={{0,2},{8,16},{16,8},{24,26},{2,0},{10,18},{18,10},{26,24},{4,6},{1... | collective-permute-start | bytes 589832 | tf_op jit(solution)/shard_map/ppermute | solution.py:373
  22.0 0.2 collective-permute-start.5
  22.2 0.0 collective-permute-done.3.q_end.refs_3_
  22.2 4.5 %collective-permute-start.11 = (bf16[64,1024]{1,0:T(8,128)(2,1)S(1)}, bf16[64,1024]{1,0:T(8,128)(2,1)S(1)}, u32[]{:S(2)}, u32[]{:S(2)}) collective-permute-start(bf16[64,1024]{1,0:T(8,128)(2,1)S(1)} %get-tuple-element.63.q_own.refs_3_), channel_id=1, source_target_pairs={{0,8},{8,0},{16,24},{24,16},{1,9},{9,1},{17,25},{25,17},{2,10},{10... | collective-permute-start | bytes 393224 | tf_op jit(solution)/shard_map/ppermute | solution.py:370
  26.7 1.2 %shard_map.83 = (s32[8]{0:T(128)S(1)}, f32[8,640]{1,0:T(8,128)S(1)}, f32[8,384]{1,0:T(8,128)S(1)}, f32[4,8,128]{2,1,0:T(8,128)S(1)}) custom-call(s32[36]{0:T(128)S(1)} %get-tuple-element.45.limits), custom_call_target="tpu_custom_call" | custom-call | bytes 524288 | tf_op jit(solution)/shard_map/pallas_call | solution.py:422
  27.9 0.6 %shard_map.84 = (f32[2,512,128]{2,1,0:T(8,128)S(1)}, f32[2,512,128]{2,1,0:T(8,128)S(1)}, f32[2,512,128]{2,1,0:T(8,128)S(1)}, bf16[2,384,128]{2,1,0:T(8,128)(2,1)S(1)}) custom-call(s32[8]{0:T(128)S(1)} %get-tuple-element.46.marks.refs_0_, f32[8,640]{1,0:T(8,128)S(1)} %get-tuple-element.52.bias_early, bf16[64,1024]{1,0:T(8,128)(2,1)S(1)} %get-tuple-element.49.q_own.refs_4_, ...), custom_call_target="tpu_custom_call" | custom-call | flops 469762048 | bytes 4194304 | tf_op jit(solution)/shard_map/pallas_call | solution.py:465
  28.4 1.2 %collective-permute-done.11.q_end.refs_3_ = bf16[64,1024]{1,0:T(8,128)(2,1)S(1)} collective-permute-done((bf16[64,1024]{1,0:T(8,128)(2,1)S(1)}, bf16[64,1024]{1,0:T(8,128)(2,1)S(1)}, u32[]{:S(2)}, u32[]{:S(2)}) %collective-permute-start.11) | collective-permute-done | bytes 131104 | tf_op jit(solution)/shard_map/ppermute | solution.py:370
  29.6 0.0 collective-permute-done.12.refs_2_
  29.6 0.6 %shard_map.86 = (f32[2,512,128]{2,1,0:T(8,128)S(1)}, f32[2,512,128]{2,1,0:T(8,128)S(1)}, f32[2,512,128]{2,1,0:T(8,128)S(1)}, bf16[2,384,128]{2,1,0:T(8,128)(2,1)S(1)}) custom-call(s32[8]{0:T(128)S(1)} %get-tuple-element.46.marks.refs_0_, f32[8,640]{1,0:T(8,128)S(1)} %get-tuple-element.52.bias_early, bf16[64,1024]{1,0:T(8,128)(2,1)S(1)} %get-tuple-element.63.q_own.refs_3_, ...), custom_call_target="tpu_custom_call" | custom-call | flops 469762048 | bytes 4194304 | tf_op jit(solution)/shard_map/pallas_call | solution.py:465
  30.2 0.0 collective-permute-done.10.refs_4_
  30.2 0.0 collective-permute-done.8.refs_6_.refs_5_
  30.2 0.6 %shard_map.88 = bf16[64,1024]{1,0:T(8,128)(2,1)S(1)} custom-call(s32[8]{0:T(128)S(1)} %get-tuple-element.46.marks.refs_0_, f32[8,384]{1,0:T(8,128)S(1)} %get-tuple-element.47.refs_1_, f32[4,8,128]{2,1,0:T(8,128)S(1)} %get-tuple-element.48.refs_2_, bf16[64,1024]{1,0:T(8,128)(2,1)S(1)} %collective-permute-done.11.q_end.refs_3_, ...), custom_call_target="tpu_custom_call" | custom-call | flops 167772160 | bytes 1048576 | tf_op jit(solution)/shard_map/pallas_call | solution.py:477
  30.8 5.5 %collective-permute-start.14 = (bf16[64,1024]{1,0:T(8,128)(2,1)S(1)}, bf16[64,1024]{1,0:T(8,128)(2,1)S(1)}, u32[]{:S(2)}, u32[]{:S(2)}) collective-permute-start(bf16[64,1024]{1,0:T(8,128)(2,1)S(1)} %shard_map.88), channel_id=1, source_target_pairs={{0,8},{8,0},{16,24},{24,16},{1,9},{9,1},{17,25},{25,17},{2,10},{10... | collective-permute-start | bytes 393224 | tf_op jit(solution)/shard_map/ppermute | solution.py:370
  36.3 0.0 collective-permute-done.5.refs_5_
  36.3 0.8 %shard_map.85 = (bf16[64,1024]{1,0:T(8,128)(2,1)S(1)}, bf16[64,1024]{1,0:T(8,128)(2,1)S(1)}) custom-call(s32[8]{0:T(128)S(1)} %get-tuple-element.46.marks.refs_0_, f32[8,384]{1,0:T(8,128)S(1)} %get-tuple-element.47.refs_1_, f32[4,8,128]{2,1,0:T(8,128)S(1)} %get-tuple-element.48.refs_2_, bf16[64,1024]{1,0:T(8,128)(2,1)S(1)} %collective-permute-done.3.q_end.refs_3_, ...), custom_call_target="tpu_custom_call" | custom-call | flops 335544320 | bytes 2097152 | tf_op jit(solution)/shard_map/pallas_call | solution.py:477
  37.1 2.2 %collective-permute-start.13 = (bf16[64,1024]{1,0:T(8,128)(2,1)S(1)}, bf16[64,1024]{1,0:T(8,128)(2,1)S(1)}, u32[]{:S(2)}, u32[]{:S(2)}) collective-permute-start(bf16[64,1024]{1,0:T(8,128)(2,1)S(1)} %get-tuple-element.69), channel_id=1, source_target_pairs={{0,8},{8,0},{16,24},{24,16},{1,9},{9,1},{17,25},{25,17},{2,10},{10... | collective-permute-start | bytes 393224 | tf_op jit(solution)/shard_map/ppermute | solution.py:370
  39.3 0.6 %shard_map.87.own1 = bf16[64,1024]{1,0:T(8,128)(2,1)S(1)} custom-call(s32[8]{0:T(128)S(1)} %get-tuple-element.46.marks.refs_0_, f32[8,384]{1,0:T(8,128)S(1)} %get-tuple-element.47.refs_1_, f32[4,8,128]{2,1,0:T(8,128)S(1)} %get-tuple-element.48.refs_2_, bf16[64,1024]{1,0:T(8,128)(2,1)S(1)} %get-tuple-element.63.q_own.refs_3_, ...), custom_call_target="tpu_custom_call" | custom-call | flops 167772160 | bytes 1048576 | tf_op jit(solution)/shard_map/pallas_call | solution.py:477
  39.9 0.0 collective-permute-done.14.back1
  40.0 2.3 %collective-permute-done.13.back0 = bf16[64,1024]{1,0:T(8,128)(2,1)S(1)} collective-permute-done((bf16[64,1024]{1,0:T(8,128)(2,1)S(1)}, bf16[64,1024]{1,0:T(8,128)(2,1)S(1)}, u32[]{:S(2)}, u32[]{:S(2)}) %collective-permute-start.13) | collective-permute-done | bytes 131104 | tf_op jit(solution)/shard_map/ppermute | solution.py:370
  42.3 0.7 %shard_map.89 = bf16[1,64,2048]{2,1,0:T(8,128)(2,1)} custom-call(bf16[64,1024]{1,0:T(8,128)(2,1)S(1)} %get-tuple-element.62.own0, bf16[64,1024]{1,0:T(8,128)(2,1)S(1)} %shard_map.87.own1, bf16[64,1024]{1,0:T(8,128)(2,1)S(1)} %collective-permute-done.13.back0, bf16[64,1024]{1,0:T(8,128)(2,1)S(1)} %collective-permute-done.14.back1), custom_call_target="tpu_custom_call" | custom-call | bytes 1048576 | tf_op jit(solution)/shard_map/pallas_call | solution.py:498
  (6 shorter events, 0.1 us)
Async XLA Ops:
  2.8 10.3 %collective-permute-start.4 = (bf16[2,512,128]{2,1,0:T(8,128)(2,1)S(1)}, bf16[2,512,128]{2,1,0:T(8,128)(2,1)S(1)}, u32[]{:S(2)}, u32[]{:S(2)}) collective-permute-start(bf16[2,512,128]{2,1,0:T(8,128)(2,1)S(1)} %get-tuple-element.50.refs_0_.refs_3_), channel_id=1, source_target_pairs={{0,8},{8,0},{16,24},{24,16},{1,9},{9,1},{17,25},{25,17},{2,10},{10... | collective-permute-start | bytes 786440 | tf_op jit(solution)/shard_map/ppermute | solution.py:370
  5.9 7.2 %collective-permute-start.6 = (bf16[2,512,128]{2,1,0:T(8,128)(2,1)S(1)}, bf16[2,512,128]{2,1,0:T(8,128)(2,1)S(1)}, u32[]{:S(2)}, u32[]{:S(2)}) collective-permute-start(bf16[2,512,128]{2,1,0:T(8,128)(2,1)S(1)} %get-tuple-element.50.refs_0_.refs_3_), channel_id=1, source_target_pairs={{0,2},{8,16},{16,8},{24,26},{2,0},{10,18},{18,10},{26,24},{4,6},{1... | collective-permute-start | bytes 786440 | tf_op jit(solution)/shard_map/ppermute | solution.py:373
  5.9 15.6 %collective-permute-start.9 = (bf16[2,384,128]{2,1,0:T(8,128)(2,1)S(1)}, bf16[2,384,128]{2,1,0:T(8,128)(2,1)S(1)}, u32[]{:S(2)}, u32[]{:S(2)}) collective-permute-start(bf16[2,384,128]{2,1,0:T(8,128)(2,1)S(1)} %get-tuple-element.64.refs_0_), channel_id=1, source_target_pairs={{0,8},{8,0},{16,24},{24,16},{1,9},{9,1},{17,25},{25,17},{2,10},{10... | collective-permute-start | bytes 589832 | tf_op jit(solution)/shard_map/ppermute | solution.py:370
  9.1 9.6 %collective-permute-start.7 = (bf16[2,128,128]{2,1,0:T(8,128)(2,1)S(1)}, bf16[2,128,128]{2,1,0:T(8,128)(2,1)S(1)}, u32[]{:S(2)}, u32[]{:S(2)}) collective-permute-start(bf16[2,128,128]{2,1,0:T(8,128)(2,1)S(1)} %get-tuple-element.51), channel_id=1, source_target_pairs={{0,16},{16,24},{24,8},{8,0},{1,17},{17,25},{25,9},{9,1},{2,18},{18... | collective-permute-start | bytes 196616 | tf_op jit(solution)/shard_map/ppermute | solution.py:413
  9.1 13.1 %collective-permute-start.3 = (bf16[64,1024]{1,0:T(8,128)(2,1)S(1)}, bf16[64,1024]{1,0:T(8,128)(2,1)S(1)}, u32[]{:S(2)}, u32[]{:S(2)}) collective-permute-start(bf16[64,1024]{1,0:T(8,128)(2,1)S(1)} %get-tuple-element.49.q_own.refs_4_), channel_id=1, source_target_pairs={{0,8},{8,0},{16,24},{24,16},{1,9},{9,1},{17,25},{25,17},{2,10},{10... | collective-permute-start | bytes 393224 | tf_op jit(solution)/shard_map/ppermute | solution.py:370
  18.7 11.5 %collective-permute-start.8 = (bf16[4,2,128,128]{3,2,1,0:T(8,128)(2,1)S(1)}, bf16[4,2,128,128]{3,2,1,0:T(8,128)(2,1)S(1)}, u32[]{:S(2)}, u32[]{:S(2)}) collective-permute-start(bf16[4,2,128,128]{3,2,1,0:T(8,128)(2,1)S(1)} %pad_maximum_fusion), channel_id=1, source_target_pairs={{0,1},{1,0},{2,3},{3,2},{4,5},{5,4},{6,7},{7,6},{8,9},{9,8},{10,11... | collective-permute-start | bytes 786440 | tf_op jit(solution)/shard_map/ppermute | solution.py:376
  21.4 8.2 %collective-permute-start.12 = (bf16[2,384,128]{2,1,0:T(8,128)(2,1)S(1)}, bf16[2,384,128]{2,1,0:T(8,128)(2,1)S(1)}, u32[]{:S(2)}, u32[]{:S(2)}) collective-permute-start(bf16[2,384,128]{2,1,0:T(8,128)(2,1)S(1)} %get-tuple-element.64.refs_0_), channel_id=1, source_target_pairs={{0,2},{8,16},{16,8},{24,26},{2,0},{10,18},{18,10},{26,24},{4,6},{1... | collective-permute-start | bytes 589832 | tf_op jit(solution)/shard_map/ppermute | solution.py:373
  21.5 8.6 %collective-permute-start.10 = (bf16[2,384,128]{2,1,0:T(8,128)(2,1)S(1)}, bf16[2,384,128]{2,1,0:T(8,128)(2,1)S(1)}, u32[]{:S(2)}, u32[]{:S(2)}) collective-permute-start(bf16[2,384,128]{2,1,0:T(8,128)(2,1)S(1)} %collective-permute-done.9.refs_1_), channel_id=1, source_target_pairs={{0,2},{8,16},{16,8},{24,26},{2,0},{10,18},{18,10},{26,24},{4,6},{1... | collective-permute-start | bytes 589832 | tf_op jit(solution)/shard_map/ppermute | solution.py:373
  22.0 14.3 %collective-permute-start.5 = (bf16[2,384,128]{2,1,0:T(8,128)(2,1)S(1)}, bf16[2,384,128]{2,1,0:T(8,128)(2,1)S(1)}, u32[]{:S(2)}, u32[]{:S(2)}) collective-permute-start(bf16[2,384,128]{2,1,0:T(8,128)(2,1)S(1)} %slice.12), channel_id=1, source_target_pairs={{0,2},{8,16},{16,8},{24,26},{2,0},{10,18},{18,10},{26,24},{4,6},{1... | collective-permute-start | bytes 589832 | tf_op jit(solution)/shard_map/ppermute | solution.py:373
  22.2 7.4 %collective-permute-start.11 = (bf16[64,1024]{1,0:T(8,128)(2,1)S(1)}, bf16[64,1024]{1,0:T(8,128)(2,1)S(1)}, u32[]{:S(2)}, u32[]{:S(2)}) collective-permute-start(bf16[64,1024]{1,0:T(8,128)(2,1)S(1)} %get-tuple-element.63.q_own.refs_3_), channel_id=1, source_target_pairs={{0,8},{8,0},{16,24},{24,16},{1,9},{9,1},{17,25},{25,17},{2,10},{10... | collective-permute-start | bytes 393224 | tf_op jit(solution)/shard_map/ppermute | solution.py:370
  30.8 9.1 %collective-permute-start.14 = (bf16[64,1024]{1,0:T(8,128)(2,1)S(1)}, bf16[64,1024]{1,0:T(8,128)(2,1)S(1)}, u32[]{:S(2)}, u32[]{:S(2)}) collective-permute-start(bf16[64,1024]{1,0:T(8,128)(2,1)S(1)} %shard_map.88), channel_id=1, source_target_pairs={{0,8},{8,0},{16,24},{24,16},{1,9},{9,1},{17,25},{25,17},{2,10},{10... | collective-permute-start | bytes 393224 | tf_op jit(solution)/shard_map/ppermute | solution.py:370
  37.1 5.2 %collective-permute-start.13 = (bf16[64,1024]{1,0:T(8,128)(2,1)S(1)}, bf16[64,1024]{1,0:T(8,128)(2,1)S(1)}, u32[]{:S(2)}, u32[]{:S(2)}) collective-permute-start(bf16[64,1024]{1,0:T(8,128)(2,1)S(1)} %get-tuple-element.69), channel_id=1, source_target_pairs={{0,8},{8,0},{16,24},{24,16},{1,9},{9,1},{17,25},{25,17},{2,10},{10... | collective-permute-start | bytes 393224 | tf_op jit(solution)/shard_map/ppermute | solution.py:370

commit v5 on v4

--- a/solution.py
+++ b/solution.py
@@ -89,14 +89,11 @@
 
 
 def pack_body(
-    table_in, slot_in, length_in, pk, pv, nk, nv, q, pack0, pack1, fresh, q0, q1, limits, most,
+    table_in, slot_in, length_in, pk, pv, nk, nv, pack0, pack1, fresh, limits, most,
     table, slot, length, source, count, sem, sem_new, *, cap
 ):
-    half = q0.shape[1]
     rows_dev = nk.shape[1]
     copies = []
-    for i, (wide, near) in enumerate(((0, q0), (half, q1))):
-        copies.append(pltpu.make_async_copy(q.at[0, :, pl.ds(wide, half)], near, sem_new.at[i]))
     for w, new in enumerate((nk, nv)):
         for g in range(2):
             for n, (pack, row) in enumerate(((pack0, cap * PAGE), (fresh, 0))):
@@ -104,7 +101,7 @@
                     pltpu.make_async_copy(
                         new.at[0, :, pl.ds(g * HD, HD)],
                         pack.at[w, pl.ds(row + g * rows_dev, rows_dev), :],
-                        sem_new.at[2 + (n * 2 + w) * 2 + g],
+                        sem_new.at[(n * 2 + w) * 2 + g],
                     )
                 )
     for copy in copies:
@@ -146,9 +143,10 @@
     return (position == 1) | (position == 2)
 
 
-def heads_of(ref):
+def heads_of(ref, g):
+    group = ref.shape[2] // HD // 2
     return jnp.concatenate(
-        [ref[:, i * HD : (i + 1) * HD] for i in range(ref.shape[1] // HD)], axis=0
+        [ref[0, :, i * HD : (i + 1) * HD] for i in range(g * group, (g + 1) * group)], axis=0
     )
 
 
@@ -225,14 +223,16 @@
     return jnp.concatenate([bias] * (rows // rows_dev), axis=0)
 
 
-def scored(q, k, bias):
-    s = lax.dot_general(q, k, (((1,), (1,)), ((), ())), preferred_element_type=jnp.float32)
-    return s * log2_scale + bias
-
-
-def attend(q, blocks, state=None):
-    scores = [scored(q, k, bias) for k, _, bias in blocks]
-    shape = (q.shape[0], HD)
+def scores_of(q, blocks):
+    return [
+        lax.dot_general(q, k, (((1,), (1,)), ((), ())), preferred_element_type=jnp.float32)
+        for k, _, _ in blocks
+    ]
+
+
+def softmax_of(raw, blocks, state=None):
+    scores = [s * log2_scale + bias for s, (_, _, bias) in zip(raw, blocks)]
+    shape = (raw[0].shape[0], HD)
     top = functools.reduce(jnp.maximum, [jnp.max(s, axis=1, keepdims=True) for s in scores])
     if state is not None:
         old_top, old_total, old_acc = state
@@ -251,55 +251,72 @@
     return total, acc + old_acc * rescale
 
 
-def early_body(marks, bias_early, q_own, q_end, *refs, cap, early, g):
-    tops, totals, accs, left, dense = refs[-5:]
-    packs = refs[:3]
-    news = refs[3:7] if len(refs) == 12 else packs + refs[3:4]
+def in_turn(units):
+    pending = None
+    for queries, blocks, use in units:
+        raw = scores_of(queries(), blocks)
+        if pending is not None:
+            pending()
+        pending = functools.partial(use, raw, blocks)
+    pending()
+
+
+def early_body(marks, bias_early, q, *refs, cap, early, gs, t):
+    news = refs[:4]
+    packs = {0: news[:3], 1: refs[4:7] if 1 in gs else None}
+    refs = refs[7 if 1 in gs else 4 :]
+    tops, totals, accs = refs[:3]
+    left = refs[3] if t else None
+    dense = refs[-1]
     position = lax.axis_index("ctx")
-    rows_dev = q_own.shape[0]
+    rows_dev = q.shape[1]
     rows = accs.shape[1]
-
-    @pl.when(is_inner(position))
-    def _():
+    split = early * PAGE
+
+    def blocks_of(u, g):
         ids = holder_ids(position)
-        place_pages(dense, packs, (0, marks[0], marks[1]), cap)
+        place_pages(dense.at[u], packs[g], (0, marks[0], marks[1]), cap)
         firsts = [n.shape[1] - 2 * rows_dev + g * rows_dev for n in news]
         nk = jnp.concatenate([n[0, i : i + rows_dev] for n, i in zip(news, firsts)], axis=0)
         nv = jnp.concatenate([n[1, i : i + rows_dev] for n, i in zip(news, firsts)], axis=0)
-        split = early * PAGE
-        left[...] = dense[:, split : split + left.shape[1], :]
-        paged = (dense[0, :split], dense[1, :split], bias_early[0:1, :])
-        for t, q in enumerate((q_own, q_end)):
-            fresh = (nk, nv, causal_bias(position ^ t, ids, rows, rows_dev))
-            top, total, acc = attend(heads_of(q), [paged, fresh])
-            tops[t] = jnp.broadcast_to(top, acc.shape)
-            totals[t] = jnp.broadcast_to(total, acc.shape)
-            accs[t] = acc
-
-
-def late_body(*refs, cap, g, tasks):
-    n = len(tasks)
-    marks, bias_late, bias_spare = refs[:3]
-    queries = refs[3 : 3 + n]
-    pack, taken, left, tops, totals, accs = refs[3 + n : 9 + n]
-    spilled = refs[9 + n : 13 + n]
-    outs = refs[13 + n : 13 + 2 * n]
-    extra, sem, dense = refs[13 + 2 * n :]
-
-    def finish(more):
-        rows_dev = queries[0].shape[0]
-        place_pages(dense, (left, pack), (0, marks[2]), cap)
+        if left is not None:
+            left[...] = dense[u, :, split : split + left.shape[1], :]
+        paged = (dense[u, 0, :split], dense[u, 1, :split], bias_early[0:1, :])
+        return [paged, (nk, nv, causal_bias(position ^ t, ids, rows, rows_dev))]
+
+    def keep(u, raw, blocks):
+        top, total, acc = softmax_of(raw, blocks)
+        tops[u] = jnp.broadcast_to(top, acc.shape)
+        totals[u] = jnp.broadcast_to(total, acc.shape)
+        accs[u] = acc
+
+    @pl.when(is_inner(position))
+    def _():
+        in_turn(
+            (functools.partial(heads_of, q, g), blocks_of(u, g), functools.partial(keep, u))
+            for u, g in enumerate(gs)
+        )
+
+
+def late_body(marks, bias_late, bias_spare, q, taken, tops, totals, accs, *refs, cap, gs):
+    n = len(gs)
+    lasts, lefts, spilled, outs = (refs[a:b] for a, b in ((0, n), (n, 2 * n), (2 * n, 2 * n + 4), (2 * n + 4, 3 * n + 4)))
+    extra, sem, dense = refs[3 * n + 4 :]
+    rows_dev = q.shape[1]
+
+    def blocks_of(u, g, more):
+        place_pages(dense.at[u], (lefts[u], lasts[u]), (0, marks[2]), cap)
         new = slice(g * rows_dev, (g + 1) * rows_dev)
         shut = jnp.where(lax.axis_index("grp") == 1, 0.0, neg_floor).astype(jnp.float32)
         tk = jnp.concatenate([taken[i, 0, new] for i in range(taken.shape[0])], axis=0)
         tv = jnp.concatenate([taken[i, 1, new] for i in range(taken.shape[0])], axis=0)
         blocks = [
-            (dense[0, : cap * PAGE], dense[1, : cap * PAGE], bias_late[0:1, :]),
+            (dense[u, 0, : cap * PAGE], dense[u, 1, : cap * PAGE], bias_late[0:1, :]),
             (tk, tv, jnp.full((1, tk.shape[0]), shut, jnp.float32)),
         ]
         if more:
             copies = [
-                pltpu.make_async_copy(ref.at[g], extra.at[i], sem.at[i])
+                pltpu.make_async_copy(ref.at[g], extra.at[u, i], sem.at[i])
                 for i, ref in enumerate(spilled)
             ]
             for copy in copies:
@@ -307,12 +324,17 @@
             for copy in copies:
                 copy.wait()
             for i in range(len(spilled)):
-                blocks.append((extra[i, 0], extra[i, 1], bias_spare[i, 0:1, :]))
-        for t, q, out in zip(tasks, queries, outs):
-            total, num = attend(heads_of(q), blocks, (tops[t], totals[t], accs[t]))
+                blocks.append((extra[u, i, 0], extra[u, i, 1], bias_spare[i, 0:1, :]))
+        return blocks
+
+    def finish(more):
+        for u, g in enumerate(gs):
+            blocks = blocks_of(u, g, more)
+            raw = scores_of(heads_of(q, g), blocks)
+            total, num = softmax_of(raw, blocks, (tops[u], totals[u], accs[u]))
             result = (num / total).astype(jnp.bfloat16)
-            for i in range(out.shape[1] // HD):
-                out[:, i * HD : (i + 1) * HD] = result[i * rows_dev : (i + 1) * rows_dev]
+            for i in range(outs[u].shape[1] // HD):
+                outs[u][:, i * HD : (i + 1) * HD] = result[i * rows_dev : (i + 1) * rows_dev]
 
     inner = is_inner(lax.axis_index("ctx"))
     over = marks[3] > cap
@@ -375,14 +397,14 @@
     def swap_pools(x):
         return lax.ppermute(x, "grp", [(0, 1), (1, 0)])
 
-    new_keys, new_values, queries, page_table, page_slot, page_length, page_keys, page_values = [
+    new_keys, new_values, page_table, page_slot, page_length, page_keys, page_values = [
         pltpu.with_memory_space_constraint(x, pltpu.HBM)
         for x in (
-            new_keys, new_values, queries, page_table, page_slot, page_length, page_keys,
-            page_values,
+            new_keys, new_values, page_table, page_slot, page_length, page_keys, page_values,
         )
     ]
     half = sds((rows_dev, group * HD))
+    q_end = swap_side(queries)
     tables = (page_table, page_slot, page_length, page_keys, page_values)
     scalars = [
         pltpu.SMEM(page_table.shape, jnp.int32),
@@ -391,31 +413,27 @@
         pltpu.SMEM((holders * held,), jnp.int32),
         pltpu.SMEM((holders,), jnp.int32),
     ]
-    pack0, pack1, fresh, q0, q1, limits, most = call(
+    pack0, pack1, fresh, limits, most = call(
         functools.partial(pack_body, cap=cap),
         (
             sds((2, keys + 2 * rows_dev, HD)),
             sds((2, keys, HD)),
             sds((2, 2 * rows_dev, HD)),
-            half,
-            half,
             sds((holders * held + holders,), jnp.int32),
             sds((1,), jnp.int32),
         ),
-        [HBM] * 8,
-        (VMEM,) * 5 + (SMEM, SMEM),
-        scalars + [pltpu.SemaphoreType.DMA((cap * 4,)), pltpu.SemaphoreType.DMA((10,))],
+        [HBM] * 7,
+        (VMEM,) * 3 + (SMEM, SMEM),
+        scalars + [pltpu.SemaphoreType.DMA((cap * 4,)), pltpu.SemaphoreType.DMA((8,))],
         nbytes=3 << 20,
-    )(*tables, new_keys, new_values, queries)
+    )(*tables, new_keys, new_values)
 
     near0 = swap_side(pack0)
     far0 = swap_middle(pack0)
     n_last = lax.ppermute(fresh, "ctx", [(0, 2), (2, 3), (3, 1), (1, 0)])
-    q0_end = swap_side(q0)
     far1 = swap_middle(pack1)
     near1 = swap_side(pack1)
     last0 = swap_middle(near0[:, :keys])
-    q1_end = swap_side(q1)
     taken = swap_pools(jnp.stack([fresh, near0[:, keys:], far0[:, keys:], n_last]))
     last1 = swap_middle(near1)
     early_pages = page_table.shape[2] - cap
@@ -459,42 +477,49 @@
 
     rows = group * rows_dev
     pair_flops = 4 * rows * HD
-    state = (sds((2, rows, HD), jnp.float32),) * 3 + (sds((2, keys, HD)),)
-
-    def early(g, q, q_end, packs, news):
+    news = (pack0, near0, far0, n_last)
+
+    def early(gs, q, t):
+        n = len(gs)
+        packs = (pack1, near1, far1) if 1 in gs else ()
+        outs = (sds((n, rows, HD), jnp.float32),) * 3 + ((sds((2, keys, HD)),) if t else ())
         return call(
-            functools.partial(early_body, cap=cap, early=early_pages, g=g),
-            state,
-            [SMEM] + [VMEM] * (6 + len(news)),
-            (VMEM,) * 4,
-            [pltpu.VMEM((2, (early_pages + 2 * cap) * PAGE, HD), jnp.bfloat16)],
-            flops=2 * pair_flops * (early_pages * PAGE + 4 * rows_dev),
-            nbytes=4 << 20,
-        )(marks, bias_early, q, q_end, *packs, *news)
-
-    def late(g, tasks, queries, pack, carried):
-        tops, totals, accs, left = carried
+            functools.partial(early_body, cap=cap, early=early_pages, gs=gs, t=t),
+            outs,
+            [SMEM] + [VMEM] * (6 + len(packs)),
+            (VMEM,) * len(outs),
+            [pltpu.VMEM((n, 2, (early_pages + 2 * cap) * PAGE, HD), jnp.bfloat16)],
+            flops=n * pair_flops * (early_pages * PAGE + 4 * rows_dev),
+            nbytes=2 << 20,
+        )(marks, bias_early, q, *news, *packs)
+
+    def late(gs, q, carried, lefts):
+        n = len(gs)
         return call(
-            functools.partial(late_body, cap=cap, g=g, tasks=tasks),
-            (half,) * len(tasks),
-            [SMEM] + [VMEM] * (8 + len(tasks)) + [HBM] * 4,
-            (VMEM,) * len(tasks),
+            functools.partial(late_body, cap=cap, gs=gs),
+            (half,) * n,
+            [SMEM] + [VMEM] * (7 + 2 * n) + [HBM] * 4,
+            (VMEM,) * n,
             [
-                pltpu.VMEM((4, 2, (held - cap) * PAGE, HD), jnp.bfloat16),
+                pltpu.VMEM((n, 4, 2, (held - cap) * PAGE, HD), jnp.bfloat16),
                 pltpu.SemaphoreType.DMA((4,)),
-                pltpu.VMEM((2, 2 * keys, HD), jnp.bfloat16),
+                pltpu.VMEM((n, 2, 2 * keys, HD), jnp.bfloat16),
             ],
-            flops=len(tasks) * pair_flops * (keys + 4 * rows_dev),
-            nbytes=len(tasks) << 20,
-        )(marks, bias_late, bias_spare, *queries, pack, taken, left, tops, totals, accs, *spilled)
-
-    carried0 = early(0, q0, q0_end, (pack0, near0, far0), (n_last,))
-    carried1 = early(1, q1, q1_end, (pack1, near1, far1), (pack0, near0, far0, n_last))
-    end0, own0 = late(0, (1, 0), (q0_end, q0), last0, carried0)
+            flops=n * pair_flops * (keys + 4 * rows_dev),
+            nbytes=n << 20,
+        )(
+            marks, bias_late, bias_spare, q, taken, *carried, *[(last0, last1)[g] for g in gs],
+            *lefts, *spilled,
+        )
+
+    *end_state0, left0 = early((0,), q_end, 1)
+    *end_state1, left1 = early((1,), q_end, 1)
+    own_state = early((0, 1), queries, 0)
+    (end0,) = late((0,), q_end, end_state0, (left0,))
     back0 = swap_side(end0)
-    (end1,) = late(1, (1,), (q1_end,), last1, carried1)
+    (end1,) = late((1,), q_end, end_state1, (left1,))
     back1 = swap_side(end1)
-    (own1,) = late(1, (0,), (q1,), last1, carried1)
+    own0, own1 = late((0, 1), queries, own_state, (left0, left1))
     return call(join_body, sds(queries.shape), [VMEM] * 4, VMEM, nbytes=1 << 20)(
         own0, own1, back0, back1
     )

time: 43.2 us -> 44.9 us (1.039)
  waiting for transfers between devices: 11.1 us -> 15.4 us
  starting transfers between devices: 23.2 us -> 20.1 us
  Pallas kernels: 7.79 us -> 8.34 us
    ppermute x6 -> x5, starting transfers between devices: 20.5 us -> 15.4 us  [swap_side(): return lax.ppermute(x, 'ctx', side)]
    ppermute x6 -> x5, waiting for transfers between devices: 5.5 us -> 7.96 us  [swap_side(): return lax.ppermute(x, 'ctx', side)]
    ppermute x1, starting transfers between devices: 0.01 us -> 1.89 us  [chain_steps(): n_last = lax.ppermute(fresh, 'ctx', [(0, 2), (2, 3), (3, 1), (1, 0)])]
    ppermute x1, waiting for transfers between devices: 5.59 us -> 7.02 us  [chain_steps(): n_last = lax.ppermute(fresh, 'ctx', [(0, 2), (2, 3), (3, 1), (1, 0)])]
    pallas_call x5 -> x6, Pallas kernels: 3.09 us -> 3.65 us  [the longest x3 1.98 us: late(): call(functools.partial(late_body, cap=cap, gs=gs), (half,) * n, [SMEM] +...]
    ppermute x4, starting transfers between devices: 0.71 us -> 1.2 us  [swap_middle(): return lax.ppermute(x, ('ctx', 'head'), middle)]
  transfers between devices with their start and end apart: 12 -> 11, of which waited for: 4 -> 5; matrix products, arithmetic and copies ran while one was open for 0% -> 0% of each run, Pallas kernels for 10% -> 11%
where the time goes in v5:
time: 44.9 us; the launch traced here: 44.7 us
  starting transfers between devices  20.1 us (45%)
  waiting for transfers between devices  15.4 us (34%)
  Pallas kernels  8.34 us (19%)
  between operations  0.79 us (2%)
    ppermute x5, starting transfers between devices, swap_side(): return lax.ppermute(x, 'ctx', side)  15.4 us
    ppermute x5, waiting for transfers between devices, swap_side(): return lax.ppermute(x, 'ctx', side)  7.96 us
    ppermute x1, waiting for transfers between devices, chain_steps(): n_last = lax.ppermute(fresh, 'ctx', [(0, 2), (2, 3), (3, 1), (1, 0)])  7.02 us
    pallas_call x1, Pallas kernels, chain_steps(): call(functools.partial(pack_body, cap=cap), (sds((2, keys + 2 * rows_dev,...  2.78 us
    pallas_call x3, Pallas kernels, late(): call(functools.partial(late_body, cap=cap, gs=gs), (half,) * n, [SMEM] +...  1.98 us
    ppermute x1, starting transfers between devices, chain_steps(): n_last = lax.ppermute(fresh, 'ctx', [(0, 2), (2, 3), (3, 1), (1, 0)])  1.89 us
    pallas_call x3, Pallas kernels, early(): call(functools.partial(early_body, cap=cap, early=early_pages, gs=gs, t=t...  1.67 us
    ppermute x1, starting transfers between devices, swap_pools(): return lax.ppermute(x, 'grp', [(0, 1), (1, 0)])  1.58 us
  transfers between devices with their start and end apart: 11, of which 5 were waited for; matrix products, arithmetic and copies ran while one was open for 0% of the time, Pallas kernels for 11%

profile of v5, /device:TPU:0, one launch (start us, length us, event | category | flops | bytes accessed | tf_op | source)
XLA Modules:
  0.0 44.7 jit_solution(13862566261243540526)
XLA Ops:
  0.0 0.0 copy-start
  0.0 2.8 %shard_map.82 = (bf16[2,512,128]{2,1,0:T(8,128)(2,1)S(1)}, bf16[2,384,128]{2,1,0:T(8,128)(2,1)S(1)}, bf16[2,128,128]{2,1,0:T(8,128)(2,1)S(1)}, s32[36]{0:T(128)S(1)}, s32[1]{0:T(128)}) custom-call(s32[1,1,16]{2,1,0:T(1,128)} %table_in.1, s32[1,32]{1,0:T(1,128)} %slot_in.1, s32[1,32]{1,0:T(1,128)} %length_in.1, bf16[1,512,256]{2,1,0:T(8,128)(2,1)} %pk.1, ...), custom_call_target="tpu_custom_call" | custom-call | bytes 3145728 | tf_op jit(solution)/shard_map/pallas_call | solution.py:416
  2.8 0.6 %collective-permute-start.4 = (bf16[2,512,128]{2,1,0:T(8,128)(2,1)S(1)}, bf16[2,512,128]{2,1,0:T(8,128)(2,1)S(1)}, u32[]{:S(2)}, u32[]{:S(2)}) collective-permute-start(bf16[2,512,128]{2,1,0:T(8,128)(2,1)S(1)} %get-tuple-element.51.refs_0_), channel_id=1, source_target_pairs={{0,2},{8,16},{16,8},{24,26},{2,0},{10,18},{18,10},{26,24},{4,6},{1... | collective-permute-start | bytes 786440 | tf_op jit(solution)/shard_map/ppermute | solution.py:395
  3.3 4.1 %collective-permute-start.3 = (bf16[2,512,128]{2,1,0:T(8,128)(2,1)S(1)}, bf16[2,512,128]{2,1,0:T(8,128)(2,1)S(1)}, u32[]{:S(2)}, u32[]{:S(2)}) collective-permute-start(bf16[2,512,128]{2,1,0:T(8,128)(2,1)S(1)} %get-tuple-element.51.refs_0_), channel_id=1, source_target_pairs={{0,8},{8,0},{16,24},{24,16},{1,9},{9,1},{17,25},{25,17},{2,10},{10... | collective-permute-start | bytes 786440 | tf_op jit(solution)/shard_map/ppermute | solution.py:392
  7.5 0.0 copy-done
  7.5 0.0 collective-permute-start.11
  7.5 1.9 %collective-permute-start.5 = (bf16[2,128,128]{2,1,0:T(8,128)(2,1)S(1)}, bf16[2,128,128]{2,1,0:T(8,128)(2,1)S(1)}, u32[]{:S(2)}, u32[]{:S(2)}) collective-permute-start(bf16[2,128,128]{2,1,0:T(8,128)(2,1)S(1)} %get-tuple-element.50), channel_id=1, source_target_pairs={{0,16},{16,24},{24,8},{8,0},{1,17},{17,25},{25,9},{9,1},{2,18},{18... | collective-permute-start | bytes 196616 | tf_op jit(solution)/shard_map/ppermute | solution.py:433
  9.4 0.1 collective-permute-start.7
  9.5 0.0 collective-permute-done.4.refs_2_
  9.6 5.1 %collective-permute-done.3.refs_1_ = bf16[2,512,128]{2,1,0:T(8,128)(2,1)S(1)} collective-permute-done((bf16[2,512,128]{2,1,0:T(8,128)(2,1)S(1)}, bf16[2,512,128]{2,1,0:T(8,128)(2,1)S(1)}, u32[]{:S(2)}, u32[]{:S(2)}) %collective-permute-start.3) | collective-permute-done | bytes 262176 | tf_op jit(solution)/shard_map/ppermute | solution.py:392
  14.6 7.0 %collective-permute-done.5.refs_3_ = bf16[2,128,128]{2,1,0:T(8,128)(2,1)S(1)} collective-permute-done((bf16[2,128,128]{2,1,0:T(8,128)(2,1)S(1)}, bf16[2,128,128]{2,1,0:T(8,128)(2,1)S(1)}, u32[]{:S(2)}, u32[]{:S(2)}) %collective-permute-start.5) | collective-permute-done | bytes 65568 | tf_op jit(solution)/shard_map/ppermute | solution.py:433
  21.7 1.6 %collective-permute-start.6 = (bf16[4,2,128,128]{3,2,1,0:T(8,128)(2,1)S(1)}, bf16[4,2,128,128]{3,2,1,0:T(8,128)(2,1)S(1)}, u32[]{:S(2)}, u32[]{:S(2)}) collective-permute-start(bf16[4,2,128,128]{3,2,1,0:T(8,128)(2,1)S(1)} %pad_maximum_fusion), channel_id=1, source_target_pairs={{0,1},{1,0},{2,3},{3,2},{4,5},{5,4},{6,7},{7,6},{8,9},{9,8},{10,11... | collective-permute-start | bytes 786440 | tf_op jit(solution)/shard_map/ppermute | solution.py:398
  24.0 0.1 collective-permute-start.8
  24.0 0.7 %collective-permute-done.7.refs_5_ = bf16[2,384,128]{2,1,0:T(8,128)(2,1)S(1)} collective-permute-done((bf16[2,384,128]{2,1,0:T(8,128)(2,1)S(1)}, bf16[2,384,128]{2,1,0:T(8,128)(2,1)S(1)}, u32[]{:S(2)}, u32[]{:S(2)}) %collective-permute-start.7) | collective-permute-done | bytes 196640 | tf_op jit(solution)/shard_map/ppermute | solution.py:392
  24.7 0.0 collective-permute-start.10
  24.8 0.6 %collective-permute-start.9 = (bf16[2,384,128]{2,1,0:T(8,128)(2,1)S(1)}, bf16[2,384,128]{2,1,0:T(8,128)(2,1)S(1)}, u32[]{:S(2)}, u32[]{:S(2)}) collective-permute-start(bf16[2,384,128]{2,1,0:T(8,128)(2,1)S(1)} %slice.14), channel_id=1, source_target_pairs={{0,2},{8,16},{16,8},{24,26},{2,0},{10,18},{18,10},{26,24},{4,6},{1... | collective-permute-start | bytes 589832 | tf_op jit(solution)/shard_map/ppermute | solution.py:395
  25.3 1.2 %shard_map.83 = (s32[8]{0:T(128)S(1)}, f32[8,640]{1,0:T(8,128)S(1)}, f32[8,384]{1,0:T(8,128)S(1)}, f32[4,8,128]{2,1,0:T(8,128)S(1)}) custom-call(s32[36]{0:T(128)S(1)} %get-tuple-element.46.limits), custom_call_target="tpu_custom_call" | custom-call | bytes 524288 | tf_op jit(solution)/shard_map/pallas_call | solution.py:440
  26.5 0.0 collective-permute-done.11.q
  26.5 0.6 %shard_map.85 = (f32[1,512,128]{2,1,0:T(8,128)S(1)}, f32[1,512,128]{2,1,0:T(8,128)S(1)}, f32[1,512,128]{2,1,0:T(8,128)S(1)}, bf16[2,384,128]{2,1,0:T(8,128)(2,1)S(1)}) custom-call(s32[8]{0:T(128)S(1)} %get-tuple-element.47.marks, f32[8,640]{1,0:T(8,128)S(1)} %get-tuple-element.52.bias_early, bf16[1,64,2048]{2,1,0:T(8,128)(2,1)S(1)} %collective-permute-done.11.q, ...), custom_call_target="tpu_custom_call" | custom-call | flops 234881024 | bytes 2097152 | tf_op jit(solution)/shard_map/pallas_call | solution.py:486
  27.1 0.0 collective-permute-done.8.refs_6_
  27.1 0.6 %shard_map.86 = (f32[1,512,128]{2,1,0:T(8,128)S(1)}, f32[1,512,128]{2,1,0:T(8,128)S(1)}, f32[1,512,128]{2,1,0:T(8,128)S(1)}, bf16[2,384,128]{2,1,0:T(8,128)(2,1)S(1)}) custom-call(s32[8]{0:T(128)S(1)} %get-tuple-element.47.marks, f32[8,640]{1,0:T(8,128)S(1)} %get-tuple-element.52.bias_early, bf16[1,64,2048]{2,1,0:T(8,128)(2,1)S(1)} %collective-permute-done.11.q, ...), custom_call_target="tpu_custom_call" | custom-call | flops 234881024 | bytes 2097152 | tf_op jit(solution)/shard_map/pallas_call | solution.py:486
  27.7 0.0 collective-permute-done.10.refs_1_.refs_0_
  27.7 0.4 collective-permute-done.6.taken
  28.1 0.6 %shard_map.89 = bf16[64,1024]{1,0:T(8,128)(2,1)S(1)} custom-call(s32[8]{0:T(128)S(1)} %get-tuple-element.47.marks, f32[8,384]{1,0:T(8,128)S(1)} %get-tuple-element.48.bias_late, f32[4,8,128]{2,1,0:T(8,128)S(1)} %get-tuple-element.49.bias_spare, bf16[1,64,2048]{2,1,0:T(8,128)(2,1)S(1)} %collective-permute-done.11.q, ...), custom_call_target="tpu_custom_call" | custom-call | flops 167772160 | bytes 1048576 | tf_op jit(solution)/shard_map/pallas_call | solution.py:498
  28.7 9.6 %collective-permute-start.13 = (bf16[64,1024]{1,0:T(8,128)(2,1)S(1)}, bf16[64,1024]{1,0:T(8,128)(2,1)S(1)}, u32[]{:S(2)}, u32[]{:S(2)}) collective-permute-start(bf16[64,1024]{1,0:T(8,128)(2,1)S(1)} %shard_map.89), channel_id=1, source_target_pairs={{0,8},{8,0},{16,24},{24,16},{1,9},{9,1},{17,25},{25,17},{2,10},{10... | collective-permute-start | bytes 393224 | tf_op jit(solution)/shard_map/ppermute | solution.py:392
  38.4 0.0 collective-permute-done.9.refs_0_
  38.4 0.6 %shard_map.88 = bf16[64,1024]{1,0:T(8,128)(2,1)S(1)} custom-call(s32[8]{0:T(128)S(1)} %get-tuple-element.47.marks, f32[8,384]{1,0:T(8,128)S(1)} %get-tuple-element.48.bias_late, f32[4,8,128]{2,1,0:T(8,128)S(1)} %get-tuple-element.49.bias_spare, bf16[1,64,2048]{2,1,0:T(8,128)(2,1)S(1)} %collective-permute-done.11.q, ...), custom_call_target="tpu_custom_call" | custom-call | flops 167772160 | bytes 1048576 | tf_op jit(solution)/shard_map/pallas_call | solution.py:498
  39.0 1.5 %collective-permute-start.12 = (bf16[64,1024]{1,0:T(8,128)(2,1)S(1)}, bf16[64,1024]{1,0:T(8,128)(2,1)S(1)}, u32[]{:S(2)}, u32[]{:S(2)}) collective-permute-start(bf16[64,1024]{1,0:T(8,128)(2,1)S(1)} %shard_map.88), channel_id=1, source_target_pairs={{0,8},{8,0},{16,24},{24,16},{1,9},{9,1},{17,25},{25,17},{2,10},{10... | collective-permute-start | bytes 393224 | tf_op jit(solution)/shard_map/ppermute | solution.py:392
  40.5 0.6 %shard_map.84 = (f32[2,512,128]{2,1,0:T(8,128)S(1)}, f32[2,512,128]{2,1,0:T(8,128)S(1)}, f32[2,512,128]{2,1,0:T(8,128)S(1)}) custom-call(s32[8]{0:T(128)S(1)} %get-tuple-element.47.marks, f32[8,640]{1,0:T(8,128)S(1)} %get-tuple-element.52.bias_early, bf16[1,64,2048]{2,1,0:T(8,128)(2,1)S(1)} %copy-done, bf16[2,512,128]{2,1,0:T(8,128)(2,1)S(1)} %get-tuple-element.51.refs_0_, ...), custom_call_target="tpu_custom_call" | custom-call | flops 469762048 | bytes 2097152 | tf_op jit(solution)/shard_map/pallas_call | solution.py:486
  41.0 0.8 %shard_map.87 = (bf16[64,1024]{1,0:T(8,128)(2,1)S(1)}, bf16[64,1024]{1,0:T(8,128)(2,1)S(1)}) custom-call(s32[8]{0:T(128)S(1)} %get-tuple-element.47.marks, f32[8,384]{1,0:T(8,128)S(1)} %get-tuple-element.48.bias_late, f32[4,8,128]{2,1,0:T(8,128)S(1)} %get-tuple-element.49.bias_spare, bf16[1,64,2048]{2,1,0:T(8,128)(2,1)S(1)} %copy-done, ...), custom_call_target="tpu_custom_call" | custom-call | flops 335544320 | bytes 2097152 | tf_op jit(solution)/shard_map/pallas_call | solution.py:498
  41.8 0.0 collective-permute-done.13.back1
  41.9 2.2 %collective-permute-done.12.back0 = bf16[64,1024]{1,0:T(8,128)(2,1)S(1)} collective-permute-done((bf16[64,1024]{1,0:T(8,128)(2,1)S(1)}, bf16[64,1024]{1,0:T(8,128)(2,1)S(1)}, u32[]{:S(2)}, u32[]{:S(2)}) %collective-permute-start.12) | collective-permute-done | bytes 131104 | tf_op jit(solution)/shard_map/ppermute | solution.py:392
  44.0 0.7 %shard_map.90 = bf16[1,64,2048]{2,1,0:T(8,128)(2,1)} custom-call(bf16[64,1024]{1,0:T(8,128)(2,1)S(1)} %get-tuple-element.64.own0, bf16[64,1024]{1,0:T(8,128)(2,1)S(1)} %get-tuple-element.65.own1, bf16[64,1024]{1,0:T(8,128)(2,1)S(1)} %collective-permute-done.12.back0, bf16[64,1024]{1,0:T(8,128)(2,1)S(1)} %collective-permute-done.13.back1), custom_call_target="tpu_custom_call" | custom-call | bytes 1048576 | tf_op jit(solution)/shard_map/pallas_call | solution.py:523
  (6 shorter events, 0.1 us)
Async XLA Ops:
  0.0 7.5 %copy-start = (bf16[1,64,2048]{2,1,0:T(8,128)(2,1)S(1)}, bf16[1,64,2048]{2,1,0:T(8,128)(2,1)}, u32[]{:S(2)}) copy-start(bf16[1,64,2048]{2,1,0:T(8,128)(2,1)} %q.3) | copy-start | bytes 786436
  2.8 6.8 %collective-permute-start.4 = (bf16[2,512,128]{2,1,0:T(8,128)(2,1)S(1)}, bf16[2,512,128]{2,1,0:T(8,128)(2,1)S(1)}, u32[]{:S(2)}, u32[]{:S(2)}) collective-permute-start(bf16[2,512,128]{2,1,0:T(8,128)(2,1)S(1)} %get-tuple-element.51.refs_0_), channel_id=1, source_target_pairs={{0,2},{8,16},{16,8},{24,26},{2,0},{10,18},{18,10},{26,24},{4,6},{1... | collective-permute-start | bytes 786440 | tf_op jit(solution)/shard_map/ppermute | solution.py:395
  3.3 11.3 %collective-permute-start.3 = (bf16[2,512,128]{2,1,0:T(8,128)(2,1)S(1)}, bf16[2,512,128]{2,1,0:T(8,128)(2,1)S(1)}, u32[]{:S(2)}, u32[]{:S(2)}) collective-permute-start(bf16[2,512,128]{2,1,0:T(8,128)(2,1)S(1)} %get-tuple-element.51.refs_0_), channel_id=1, source_target_pairs={{0,8},{8,0},{16,24},{24,16},{1,9},{9,1},{17,25},{25,17},{2,10},{10... | collective-permute-start | bytes 786440 | tf_op jit(solution)/shard_map/ppermute | solution.py:392
  7.5 19.1 %collective-permute-start.11 = (bf16[1,64,2048]{2,1,0:T(8,128)(2,1)S(1)}, bf16[1,64,2048]{2,1,0:T(8,128)(2,1)S(1)}, u32[]{:S(2)}, u32[]{:S(2)}) collective-permute-start(bf16[1,64,2048]{2,1,0:T(8,128)(2,1)S(1)} %copy-done), channel_id=1, source_target_pairs={{0,8},{8,0},{16,24},{24,16},{1,9},{9,1},{17,25},{25,17},{2,10},{10... | collective-permute-start | bytes 786440 | tf_op jit(solution)/shard_map/ppermute | solution.py:392
  7.5 14.1 %collective-permute-start.5 = (bf16[2,128,128]{2,1,0:T(8,128)(2,1)S(1)}, bf16[2,128,128]{2,1,0:T(8,128)(2,1)S(1)}, u32[]{:S(2)}, u32[]{:S(2)}) collective-permute-start(bf16[2,128,128]{2,1,0:T(8,128)(2,1)S(1)} %get-tuple-element.50), channel_id=1, source_target_pairs={{0,16},{16,24},{24,8},{8,0},{1,17},{17,25},{25,9},{9,1},{2,18},{18... | collective-permute-start | bytes 196616 | tf_op jit(solution)/shard_map/ppermute | solution.py:433
  9.4 15.3 %collective-permute-start.7 = (bf16[2,384,128]{2,1,0:T(8,128)(2,1)S(1)}, bf16[2,384,128]{2,1,0:T(8,128)(2,1)S(1)}, u32[]{:S(2)}, u32[]{:S(2)}) collective-permute-start(bf16[2,384,128]{2,1,0:T(8,128)(2,1)S(1)} %get-tuple-element.53.refs_4_), channel_id=1, source_target_pairs={{0,8},{8,0},{16,24},{24,16},{1,9},{9,1},{17,25},{25,17},{2,10},{10... | collective-permute-start | bytes 589832 | tf_op jit(solution)/shard_map/ppermute | solution.py:392
  21.7 6.4 %collective-permute-start.6 = (bf16[4,2,128,128]{3,2,1,0:T(8,128)(2,1)S(1)}, bf16[4,2,128,128]{3,2,1,0:T(8,128)(2,1)S(1)}, u32[]{:S(2)}, u32[]{:S(2)}) collective-permute-start(bf16[4,2,128,128]{3,2,1,0:T(8,128)(2,1)S(1)} %pad_maximum_fusion), channel_id=1, source_target_pairs={{0,1},{1,0},{2,3},{3,2},{4,5},{5,4},{6,7},{7,6},{8,9},{9,8},{10,11... | collective-permute-start | bytes 786440 | tf_op jit(solution)/shard_map/ppermute | solution.py:398
  24.0 3.2 %collective-permute-start.8 = (bf16[2,384,128]{2,1,0:T(8,128)(2,1)S(1)}, bf16[2,384,128]{2,1,0:T(8,128)(2,1)S(1)}, u32[]{:S(2)}, u32[]{:S(2)}) collective-permute-start(bf16[2,384,128]{2,1,0:T(8,128)(2,1)S(1)} %get-tuple-element.53.refs_4_), channel_id=1, source_target_pairs={{0,2},{8,16},{16,8},{24,26},{2,0},{10,18},{18,10},{26,24},{4,6},{1... | collective-permute-start | bytes 589832 | tf_op jit(solution)/shard_map/ppermute | solution.py:395
  24.7 2.9 %collective-permute-start.10 = (bf16[2,384,128]{2,1,0:T(8,128)(2,1)S(1)}, bf16[2,384,128]{2,1,0:T(8,128)(2,1)S(1)}, u32[]{:S(2)}, u32[]{:S(2)}) collective-permute-start(bf16[2,384,128]{2,1,0:T(8,128)(2,1)S(1)} %collective-permute-done.7.refs_5_), channel_id=1, source_target_pairs={{0,2},{8,16},{16,8},{24,26},{2,0},{10,18},{18,10},{26,24},{4,6},{1... | collective-permute-start | bytes 589832 | tf_op jit(solution)/shard_map/ppermute | solution.py:395
  24.8 13.6 %collective-permute-start.9 = (bf16[2,384,128]{2,1,0:T(8,128)(2,1)S(1)}, bf16[2,384,128]{2,1,0:T(8,128)(2,1)S(1)}, u32[]{:S(2)}, u32[]{:S(2)}) collective-permute-start(bf16[2,384,128]{2,1,0:T(8,128)(2,1)S(1)} %slice.14), channel_id=1, source_target_pairs={{0,2},{8,16},{16,8},{24,26},{2,0},{10,18},{18,10},{26,24},{4,6},{1... | collective-permute-start | bytes 589832 | tf_op jit(solution)/shard_map/ppermute | solution.py:395
  28.7 13.1 %collective-permute-start.13 = (bf16[64,1024]{1,0:T(8,128)(2,1)S(1)}, bf16[64,1024]{1,0:T(8,128)(2,1)S(1)}, u32[]{:S(2)}, u32[]{:S(2)}) collective-permute-start(bf16[64,1024]{1,0:T(8,128)(2,1)S(1)} %shard_map.89), channel_id=1, source_target_pairs={{0,8},{8,0},{16,24},{24,16},{1,9},{9,1},{17,25},{25,17},{2,10},{10... | collective-permute-start | bytes 393224 | tf_op jit(solution)/shard_map/ppermute | solution.py:392
  39.0 5.0 %collective-permute-start.12 = (bf16[64,1024]{1,0:T(8,128)(2,1)S(1)}, bf16[64,1024]{1,0:T(8,128)(2,1)S(1)}, u32[]{:S(2)}, u32[]{:S(2)}) collective-permute-start(bf16[64,1024]{1,0:T(8,128)(2,1)S(1)} %shard_map.88), channel_id=1, source_target_pairs={{0,8},{8,0},{16,24},{24,16},{1,9},{9,1},{17,25},{25,17},{2,10},{10... | collective-permute-start | bytes 393224 | tf_op jit(solution)/shard_map/ppermute | solution.py:392
